TPU v7x, 32 devices: a whole 2x2x4 slice. The times are simulated.
32 devices in a mesh: dp: 16 (over z, y, core), space: 2 (over x).
Axes of the slice: x: 2, y: 2, z: 4, core: 2. Of those that a mesh axis runs over, the one named last changes fastest.
Arguments:
- image_in: bfloat16 [96, 14, 14, 1024], P('dp', 'space'), may hold values from -6 to 6
- text_in: bfloat16 [96, 64, 768], P(('dp', 'space')), may hold values from -6 to 6
- prefix: int32 [96], P(('dp', 'space')), may hold values from 0 to 32
- text_len: int32 [96], P(('dp', 'space')), may hold values from 33 to 64
- cotangent: bfloat16 [96, 260, 768], P(('dp', 'space')), may hold values from -6 to 6
- conv_in_w: bfloat16 [1024, 256], replicated, may hold values from -0.1875 to 0.1875
- bn1_gain: float32 [256], replicated, may hold values from 0.5 to 1.5
- bn1_shift: float32 [256], replicated, may hold values from -1.5 to 1.5
- conv_mid_w: bfloat16 [3, 3, 256, 256], replicated, may hold values from -0.125 to 0.125
- bn2_gain: float32 [256], replicated, may hold values from 0.5 to 1.5
- bn2_shift: float32 [256], replicated, may hold values from -1.5 to 1.5
- conv_out_w: bfloat16 [256, 1024], replicated, may hold values from -0.375 to 0.375
- bn3_gain: float32 [1024], replicated, may hold values from 0.5 to 1.5
- bn3_shift: float32 [1024], replicated, may hold values from -1.5 to 1.5
- proj_w: bfloat16 [1024, 768], replicated, may hold values from -0.1875 to 0.1875
- proj_b: float32 [768], replicated, may hold values from -1.5 to 1.5
- ln1_gain: float32 [768], replicated, may hold values from 0.5 to 1.5
- ln1_shift: float32 [768], replicated, may hold values from -1.5 to 1.5
- qkv_w: bfloat16 [768, 2304], replicated, may hold values from -0.21875 to 0.21875
- query_bias: float32 [768], replicated, may hold values from -1.5 to 1.5
- value_bias: float32 [768], replicated, may hold values from -1.5 to 1.5
- out_w: bfloat16 [768, 768], replicated, may hold values from -0.875 to 0.875
- out_b: float32 [768], replicated, may hold values from -1.5 to 1.5
- ln2_gain: float32 [768], replicated, may hold values from 0.5 to 1.5
- ln2_shift: float32 [768], replicated, may hold values from -1.5 to 1.5
- up_w: bfloat16 [768, 3072], replicated, may hold values from -0.21875 to 0.21875
- up_b: float32 [3072], replicated, may hold values from -1.5 to 1.5
- down_w: bfloat16 [3072, 768], replicated, may hold values from -0.109375 to 0.109375
- down_b: float32 [768], replicated, may hold values from -1.5 to 1.5
Outputs:
- block_out: bfloat16 [96, 260, 768], P(('dp', 'space'))
- image_grad: bfloat16 [96, 14, 14, 1024], P('dp', 'space')
- text_grad: bfloat16 [96, 64, 768], P(('dp', 'space'))
- conv_in_grad: float32 [1024, 256], P('space', 'dp')
- bn1_gain_grad: float32 [256], replicated
- bn1_shift_grad: float32 [256], replicated
- conv_mid_grad: float32 [3, 3, 256, 256], P(None, None, 'space', 'dp')
- bn2_gain_grad: float32 [256], replicated
- bn2_shift_grad: float32 [256], replicated
- conv_out_grad: float32 [256, 1024], P('space', 'dp')
- bn3_gain_grad: float32 [1024], replicated
- bn3_shift_grad: float32 [1024], replicated
- proj_w_grad: float32 [1024, 768], P('space', 'dp')
- proj_b_grad: float32 [768], replicated
- ln1_gain_grad: float32 [768], replicated
- ln1_shift_grad: float32 [768], replicated
- qkv_w_grad: float32 [768, 2304], P('space', 'dp')
- query_bias_grad: float32 [768], replicated
- value_bias_grad: float32 [768], replicated
- out_w_grad: float32 [768, 768], P('space', 'dp')
- out_b_grad: float32 [768], replicated
- ln2_gain_grad: float32 [768], replicated
- ln2_shift_grad: float32 [768], replicated
- up_w_grad: float32 [768, 3072], P('space', 'dp')
- up_b_grad: float32 [3072], replicated
- down_w_grad: float32 [3072, 768], P('space', 'dp')
- down_b_grad: float32 [768], replicated
Inputs may be any that keep to these rules, and one draw needn't show every extreme that they name: prefix never exceeds the example's text_len. Text rows from text_len on are padding that no position attends to.
All inputs are finite; a program needn't handle non-finite values.
Results may differ from a plain program's by a relative error of at most 0.02.
Values may be sent and summed in bfloat16 or wider, within the bound.
No kernel may reach another device: no remote copies, remote signals or barrier semaphores. Data moves between devices by JAX's collectives and lax.ppermute only.
A program may use at most 192 MiB of HBM per device.

v0:
```python
import jax
import jax.numpy as jnp
from jax import lax
from jax.sharding import PartitionSpec as P

HD = 64


eps_batch = 1e-05
eps_layer = 1e-06
masked_value = -1e30
score_scale = 0.125


def padded_2(x, sides, width):
    for axis, dim in sides:
        size, length = (lax.axis_size(axis), x.shape[dim])
        up = [(i, (i + 1) % size) for i in range(size - 1)]
        down = [(j, i) for i, j in up]
        last = lax.slice_in_dim(x, length - width, length, axis=dim)
        initial = lax.slice_in_dim(x, 0, width, axis=dim)
        before = lax.ppermute(last, axis, up)
        after = lax.ppermute(initial, axis, down)
        x = jnp.concatenate([before, x, after], axis=dim)
    return x


def matmul(left, right):
    return jnp.dot(left, right, preferred_element_type=jnp.float32)


def by_transpose(left, right):
    return lax.dot_general(
        left, right, (((1,), (1,)), ((), ())), preferred_element_type=jnp.float32
    )


def weight_grad(left, right):
    return lax.dot_general(
        left, right, (((0,), (0,)), ((), ())), preferred_element_type=jnp.float32
    )


def layer_norm(hidden, ln_gain, ln_shift):
    row_mean = jnp.mean(hidden, axis=-1, keepdims=True)
    centered = hidden - row_mean
    spread = jnp.mean(centered * centered, axis=-1, keepdims=True)
    return centered * lax.rsqrt(spread + eps_layer) * ln_gain + ln_shift


def batch_stats(values, pixel_count):
    totals = lax.psum((jnp.sum(values, axis=0), jnp.sum(values * values, axis=0)), ("dp", "space"))
    batch_mean = totals[0] / pixel_count
    spread = totals[1] / pixel_count - batch_mean * batch_mean
    return (batch_mean, lax.rsqrt(spread + eps_batch))


def batch_back(grad_out, normed, inv_std, bn_gain, pixel_count):
    totals = lax.psum(
        (jnp.sum(grad_out, axis=0), jnp.sum(grad_out * normed, axis=0)), ("dp", "space")
    )
    grad_in = (
        bn_gain
        * inv_std
        * (grad_out - totals[0] / pixel_count - normed * (totals[1] / pixel_count))
    )
    return (grad_in, totals[1], totals[0])


def conv_taps(padded, band_rows, band_cols, flipped):
    tap_list = []
    for row_off in range(3):
        for col_off in range(3):
            start_row = 2 - row_off if flipped else row_off
            start_col = 2 - col_off if flipped else col_off
            tap_list.append(
                padded[:, start_row : start_row + band_rows, start_col : start_col + band_cols, :]
            )
    return jnp.concatenate(tap_list, axis=-1).reshape(-1, 9 * padded.shape[-1])


def band_halo_pad(values):
    return jnp.pad(values, ((0, 0), (0, 0), (1, 1), (0, 0)))


def shards(
    image_in,
    text_in,
    prefix,
    text_len,
    cotangent,
    conv_in_w,
    bn1_gain,
    bn1_shift,
    conv_mid_w,
    bn2_gain,
    bn2_shift,
    conv_out_w,
    bn3_gain,
    bn3_shift,
    proj_w,
    proj_b,
    ln1_gain,
    ln1_shift,
    qkv_w,
    query_bias,
    value_bias,
    out_w,
    out_b,
    ln2_gain,
    ln2_shift,
    up_w,
    up_b,
    down_w,
    down_b,
):
    band_ex, band_rows, band_cols, channels = image_in.shape
    middle = conv_in_w.shape[1]
    width = proj_w.shape[1]
    examples = text_in.shape[0]
    all_rows = band_rows * lax.axis_size("space")
    n_image = all_rows * band_cols
    seq_len = n_image + text_in.shape[1]
    rows_all = examples * seq_len
    heads = width // HD
    pixel_count = float(
        band_ex * band_rows * band_cols * lax.axis_size("dp") * lax.axis_size("space")
    )
    x_flat = image_in.reshape(-1, channels)
    act_one = matmul(x_flat, conv_in_w)
    mean_one, rstd_one = batch_stats(act_one, pixel_count)
    norm_one = (act_one - mean_one) * rstd_one
    pre_one = norm_one * bn1_gain + bn1_shift
    smooth_one, smooth_one_pull = jax.vjp(jax.nn.gelu, pre_one)
    relu_one = smooth_one.astype(jnp.bfloat16)
    halo_one = padded_2(relu_one.reshape(band_ex, band_rows, band_cols, middle), (("space", 1),), 1)
    patch_fwd = conv_taps(band_halo_pad(halo_one), band_rows, band_cols, False)
    act_two = matmul(patch_fwd, conv_mid_w.reshape(9 * middle, middle))
    mean_two, rstd_two = batch_stats(act_two, pixel_count)
    norm_two = (act_two - mean_two) * rstd_two
    pre_two = norm_two * bn2_gain + bn2_shift
    smooth_two, smooth_two_pull = jax.vjp(jax.nn.gelu, pre_two)
    relu_two = smooth_two.astype(jnp.bfloat16)
    act_three = matmul(relu_two, conv_out_w)
    mean_three, rstd_three = batch_stats(act_three, pixel_count)
    norm_three = (act_three - mean_three) * rstd_three
    pre_three = norm_three * bn3_gain + bn3_shift + x_flat.astype(jnp.float32)
    smooth_three, smooth_three_pull = jax.vjp(jax.nn.gelu, pre_three)
    stem_out = smooth_three.astype(jnp.bfloat16)
    tokens_img = (matmul(stem_out, proj_w) + proj_b).astype(jnp.bfloat16)
    moved = lax.all_to_all(
        tokens_img.reshape(band_ex, band_rows, band_cols, width),
        "space",
        split_axis=0,
        concat_axis=1,
        tiled=True,
    )
    hidden_in = jnp.concatenate(
        [moved.reshape(examples, n_image, width).astype(jnp.float32), text_in.astype(jnp.float32)],
        axis=1,
    )
    normed_one, ln_one_pull = jax.vjp(layer_norm, hidden_in, ln1_gain, ln1_shift)
    z_one = normed_one.astype(jnp.bfloat16).reshape(rows_all, width)
    qkv_all = matmul(z_one, qkv_w)
    query_rows = (
        (qkv_all[:, :width] + query_bias).astype(jnp.bfloat16).reshape(examples, seq_len, heads, HD)
    )
    key_rows = (
        qkv_all[:, width : 2 * width].astype(jnp.bfloat16).reshape(examples, seq_len, heads, HD)
    )
    value_rows = (
        (qkv_all[:, 2 * width :] + value_bias)
        .astype(jnp.bfloat16)
        .reshape(examples, seq_len, heads, HD)
    )
    positions = jnp.arange(seq_len, dtype=jnp.int32)
    open_end = (n_image + prefix)[:, None, None]
    valid_end = (n_image + text_len)[:, None, None]
    key_pos = positions[None, None, :]
    query_pos = positions[None, :, None]
    visible = (key_pos < valid_end) & ((key_pos < open_end) | (key_pos <= query_pos))

    def scores_of():
        raw_scores = (
            jnp.einsum("bqhe,bkhe->bhqk", query_rows, key_rows, preferred_element_type=jnp.float32)
            * score_scale
        )
        return jnp.where(visible[:, None], raw_scores, masked_value)

    scores = scores_of()
    row_max = jnp.max(scores, axis=-1, keepdims=True)
    expo = jnp.exp(scores - row_max)
    row_sum = jnp.sum(expo, axis=-1, keepdims=True)
    probs = expo / row_sum
    log_total = row_max + jnp.log(row_sum)
    attended = jnp.einsum(
        "bhqk,bkhe->bqhe",
        probs.astype(jnp.bfloat16),
        value_rows,
        preferred_element_type=jnp.float32,
    )
    attn_out = attended.astype(jnp.bfloat16).reshape(rows_all, width)
    resid_one = hidden_in.reshape(rows_all, width) + matmul(attn_out, out_w) + out_b
    normed_two, ln_two_pull = jax.vjp(layer_norm, resid_one, ln2_gain, ln2_shift)
    z_two = normed_two.astype(jnp.bfloat16)
    pre_gelu = matmul(z_two, up_w) + up_b
    gelu_out, gelu_pull = jax.vjp(jax.nn.gelu, pre_gelu)
    gelu_low = gelu_out.astype(jnp.bfloat16)
    block_out = (
        (resid_one + matmul(gelu_low, down_w) + down_b)
        .astype(jnp.bfloat16)
        .reshape(examples, seq_len, width)
    )
    grad_top = cotangent.astype(jnp.float32).reshape(rows_all, width)
    down_b_grad = jnp.sum(grad_top, axis=0)
    branch_low = grad_top.astype(jnp.bfloat16)
    down_w_grad = weight_grad(gelu_low, branch_low)
    gelu_grad = gelu_pull(by_transpose(branch_low, down_w))[0].astype(jnp.bfloat16)
    up_b_grad = jnp.sum(gelu_grad.astype(jnp.float32), axis=0)
    up_w_grad = weight_grad(z_two, gelu_grad)
    norm_grad_two, ln2_gain_grad, ln2_shift_grad = ln_two_pull(by_transpose(gelu_grad, up_w))
    resid_grad = grad_top + norm_grad_two
    out_b_grad = jnp.sum(resid_grad, axis=0)
    proj_low = resid_grad.astype(jnp.bfloat16)
    out_w_grad = weight_grad(attn_out, proj_low)
    attn_grad = (
        by_transpose(proj_low, out_w).astype(jnp.bfloat16).reshape(examples, seq_len, heads, HD)
    )
    probs_back = jnp.exp(scores_of() - log_total)
    value_grad = jnp.einsum(
        "bhqk,bqhe->bkhe",
        probs_back.astype(jnp.bfloat16),
        attn_grad,
        preferred_element_type=jnp.float32,
    ).astype(jnp.bfloat16)
    prob_grad = jnp.einsum(
        "bqhe,bkhe->bhqk", attn_grad, value_rows, preferred_element_type=jnp.float32
    )
    inner_sum = jnp.sum(probs_back * prob_grad, axis=-1, keepdims=True)
    score_grad = (probs_back * (prob_grad - inner_sum)).astype(jnp.bfloat16)
    query_grad = (
        jnp.einsum("bhqk,bkhe->bqhe", score_grad, key_rows, preferred_element_type=jnp.float32)
        * score_scale
    ).astype(jnp.bfloat16)
    key_grad = (
        jnp.einsum("bhqk,bqhe->bkhe", score_grad, query_rows, preferred_element_type=jnp.float32)
        * score_scale
    ).astype(jnp.bfloat16)
    qkv_grad = jnp.concatenate(
        [
            query_grad.reshape(rows_all, width),
            key_grad.reshape(rows_all, width),
            value_grad.reshape(rows_all, width),
        ],
        axis=1,
    )
    qkv_w_grad = weight_grad(z_one, qkv_grad)
    query_b_grad = jnp.sum(query_grad.astype(jnp.float32).reshape(rows_all, width), axis=0)
    value_b_grad = jnp.sum(value_grad.astype(jnp.float32).reshape(rows_all, width), axis=0)
    norm_grad_one, ln1_gain_grad, ln1_shift_grad = ln_one_pull(
        by_transpose(qkv_grad, qkv_w).reshape(examples, seq_len, width)
    )
    input_grad = resid_grad.reshape(examples, seq_len, width) + norm_grad_one
    text_grad = input_grad[:, n_image:].astype(jnp.bfloat16)
    image_tok_grad = (
        input_grad[:, :n_image].astype(jnp.bfloat16).reshape(examples, all_rows, band_cols, width)
    )
    back_bands = lax.all_to_all(
        image_tok_grad, "space", split_axis=1, concat_axis=0, tiled=True
    ).reshape(-1, width)
    proj_b_grad = jnp.sum(back_bands.astype(jnp.float32), axis=0)
    proj_w_grad = weight_grad(stem_out, back_bands)
    relu_grad_three = smooth_three_pull(by_transpose(back_bands, proj_w))[0]
    act_grad_three, bn3_gain_grad, bn3_shift_grad = batch_back(
        relu_grad_three, norm_three, rstd_three, bn3_gain, pixel_count
    )
    low_three = act_grad_three.astype(jnp.bfloat16)
    conv_out_grad = weight_grad(relu_two, low_three)
    relu_grad_two = smooth_two_pull(by_transpose(low_three, conv_out_w))[0]
    act_grad_two, bn2_gain_grad, bn2_shift_grad = batch_back(
        relu_grad_two, norm_two, rstd_two, bn2_gain, pixel_count
    )
    low_two = act_grad_two.astype(jnp.bfloat16)
    conv_mid_grad = weight_grad(patch_fwd, low_two).reshape(3, 3, middle, middle)
    halo_two = padded_2(low_two.reshape(band_ex, band_rows, band_cols, middle), (("space", 1),), 1)
    patch_back = conv_taps(band_halo_pad(halo_two), band_rows, band_cols, True)
    flipped_w = jnp.transpose(conv_mid_w, (0, 1, 3, 2)).reshape(9 * middle, middle)
    relu_grad_one = smooth_one_pull(matmul(patch_back, flipped_w))[0]
    act_grad_one, bn1_gain_grad, bn1_shift_grad = batch_back(
        relu_grad_one, norm_one, rstd_one, bn1_gain, pixel_count
    )
    low_one = act_grad_one.astype(jnp.bfloat16)
    conv_in_grad = weight_grad(x_flat, low_one)
    image_grad = (
        (by_transpose(low_one, conv_in_w) + relu_grad_three)
        .astype(jnp.bfloat16)
        .reshape(image_in.shape)
    )
    small_sums = lax.psum(
        (
            proj_b_grad,
            ln1_gain_grad,
            ln1_shift_grad,
            query_b_grad,
            value_b_grad,
            out_b_grad,
            ln2_gain_grad,
            ln2_shift_grad,
            up_b_grad,
            down_b_grad,
        ),
        ("dp", "space"),
    )
    data_part = (
        lax.psum_scatter(conv_in_grad, "dp", scatter_dimension=1, tiled=True),
        lax.psum_scatter(conv_mid_grad, "dp", scatter_dimension=3, tiled=True),
        lax.psum_scatter(conv_out_grad, "dp", scatter_dimension=1, tiled=True),
        lax.psum_scatter(proj_w_grad, "dp", scatter_dimension=1, tiled=True),
        lax.psum_scatter(qkv_w_grad, "dp", scatter_dimension=1, tiled=True),
        lax.psum_scatter(out_w_grad, "dp", scatter_dimension=1, tiled=True),
        lax.psum_scatter(up_w_grad, "dp", scatter_dimension=1, tiled=True),
        lax.psum_scatter(down_w_grad, "dp", scatter_dimension=1, tiled=True),
    )
    reduced = (
        lax.psum_scatter(
            data_part[0].astype(jnp.bfloat16), "space", scatter_dimension=0, tiled=True
        ).astype(jnp.float32),
        lax.psum_scatter(
            data_part[1].astype(jnp.bfloat16), "space", scatter_dimension=2, tiled=True
        ).astype(jnp.float32),
        lax.psum_scatter(
            data_part[2].astype(jnp.bfloat16), "space", scatter_dimension=0, tiled=True
        ).astype(jnp.float32),
        lax.psum_scatter(
            data_part[3].astype(jnp.bfloat16), "space", scatter_dimension=0, tiled=True
        ).astype(jnp.float32),
        lax.psum_scatter(
            data_part[4].astype(jnp.bfloat16), "space", scatter_dimension=0, tiled=True
        ).astype(jnp.float32),
        lax.psum_scatter(
            data_part[5].astype(jnp.bfloat16), "space", scatter_dimension=0, tiled=True
        ).astype(jnp.float32),
        lax.psum_scatter(
            data_part[6].astype(jnp.bfloat16), "space", scatter_dimension=0, tiled=True
        ).astype(jnp.float32),
        lax.psum_scatter(
            data_part[7].astype(jnp.bfloat16), "space", scatter_dimension=0, tiled=True
        ).astype(jnp.float32),
    )
    return (
        block_out,
        image_grad,
        text_grad,
        reduced[0],
        bn1_gain_grad,
        bn1_shift_grad,
        reduced[1],
        bn2_gain_grad,
        bn2_shift_grad,
        reduced[2],
        bn3_gain_grad,
        bn3_shift_grad,
        reduced[3],
        small_sums[0],
        small_sums[1],
        small_sums[2],
        reduced[4],
        small_sums[3],
        small_sums[4],
        reduced[5],
        small_sums[5],
        small_sums[6],
        small_sums[7],
        reduced[6],
        small_sums[8],
        reduced[7],
        small_sums[9],
    )


def solution(mesh):
    return jax.shard_map(
        shards,
        mesh=mesh,
        in_specs=(
            P("dp", "space", None, None),
            P(("dp", "space"), None, None),
            P(("dp", "space")),
            P(("dp", "space")),
            P(("dp", "space"), None, None),
            P(),
            P(),
            P(),
            P(),
            P(),
            P(),
            P(),
            P(),
            P(),
            P(),
            P(),
            P(),
            P(),
            P(),
            P(),
            P(),
            P(),
            P(),
            P(),
            P(),
            P(),
            P(),
            P(),
            P(),
        ),
        out_specs=(
            P(("dp", "space"), None, None),
            P("dp", "space", None, None),
            P(("dp", "space"), None, None),
            P("space", "dp"),
            P(),
            P(),
            P(None, None, "space", "dp"),
            P(),
            P(),
            P("space", "dp"),
            P(),
            P(),
            P("space", "dp"),
            P(),
            P(),
            P(),
            P("space", "dp"),
            P(),
            P(),
            P("space", "dp"),
            P(),
            P(),
            P(),
            P("space", "dp"),
            P(),
            P("space", "dp"),
            P(),
        ),
        check_vma=False,
    )
```

profile of v0, /device:TPU:0, one launch (start us, length us, event | category | flops | bytes accessed | tf_op | source)
XLA Modules:
  0.0 1364.8 jit_solution(4407853277952022843)
XLA Ops:
  13.0 42.0 %all-reduce.7 = (f32[256]{0:T(256)}, f32[256]{0:T(256)}) all-reduce(f32[256]{0:T(256)S(1)} %get-tuple-element.44, f32[256]{0:T(256)S(1)} %get-tuple-element.43), channel_id=1, replica_groups=mesh['dp'=16,'space'=2] {'dp','space'}, use_global_device_ids=true, to_apply=%region_3.0 | all-reduce | flops 512 | bytes 4096 | tf_op jit(solution)/shard_map/psum | solution.py:52
  61.5 4.8 collective-permute-start
  98.7 41.2 %all-reduce.6 = (f32[256]{0:T(256)}, f32[256]{0:T(256)}) all-reduce(f32[256]{0:T(256)S(1)} %get-tuple-element.42, f32[256]{0:T(256)S(1)} %get-tuple-element.41), channel_id=1, replica_groups=mesh['dp'=16,'space'=2] {'dp','space'}, use_global_device_ids=true, to_apply=%region_7.8 | all-reduce | flops 512 | bytes 4096 | tf_op jit(solution)/shard_map/psum | solution.py:52
  145.1 40.1 %all-reduce.5 = (f32[1024]{0:T(1024)}, f32[1024]{0:T(1024)}) all-reduce(f32[1024]{0:T(1024)S(1)} %get-tuple-element.34, f32[1024]{0:T(1024)S(1)} %get-tuple-element.33), channel_id=1, replica_groups=mesh['dp'=16,'space'=2] {'dp','space'}, use_global_device_ids=true, to_apply=%region_11.12 | all-reduce | flops 2048 | bytes 16384 | tf_op jit(solution)/shard_map/psum | solution.py:52
  195.2 4.9 all-to-all-start
  202.1 11.3 all-to-all-done
  228.1 4.9 fusion.63
  235.9 4.7 reshape.384
  240.6 5.7 copy.122
  246.3 4.7 reshape.385
  251.1 5.7 copy.123
  256.8 4.7 reshape.383
  261.5 5.9 copy.124
  267.4 10.1 fusion.81
  277.5 7.7 fusion
  285.9 8.0 convert_bitcast_fusion.1
  296.8 5.3 reshape.358
  302.1 3.9 fusion.82
  306.8 9.5 fusion.65
  316.3 12.5 convert_reduce_fusion
  328.8 4.9 multiply_reduce_fusion.4
  342.0 4.7 reshape.386
  346.7 6.1 copy.128
  352.9 9.3 convert_reduce_fusion.1
  362.2 9.8 multiply_reduce_fusion
  372.0 10.5 multiply_convert_fusion
  382.5 3.9 fusion.28
  386.5 3.7 convert_reduce_fusion.2
  393.1 5.3 reshape.365
  398.4 4.4 copy.135
  402.8 5.4 reshape.364
  408.3 4.4 copy.132
  412.7 5.3 reshape.363
  421.6 5.2 multiply_reduce_fusion.6
  433.6 4.1 multiply_reduce_fusion.5
  439.7 3.6 fusion.15
  449.8 4.4 all-to-all-start.1
  461.7 4.6 all-to-all-done.1
  470.7 7.9 fusion.66
  478.6 39.6 %all-reduce.4 = (f32[1024]{0:T(1024)}, f32[1024]{0:T(1024)}) all-reduce(f32[1024]{0:T(1024)} %get-tuple-element.32, f32[1024]{0:T(1024)} %get-tuple-element.31), channel_id=1, replica_groups=mesh['dp'=16,'space'=2] {'dp','space'}, use_global_device_ids=true, to_apply=%region_26.27 | all-reduce | flops 2048 | bytes 16384 | tf_op jit(solution)/shard_map/psum | solution.py:59
  526.9 39.9 %all-reduce.3 = (f32[256]{0:T(256)}, f32[256]{0:T(256)}) all-reduce(f32[256]{0:T(256)} %get-tuple-element.40, f32[256]{0:T(256)} %get-tuple-element.39), channel_id=1, replica_groups=mesh['dp'=16,'space'=2] {'dp','space'}, use_global_device_ids=true, to_apply=%region_30.31 | all-reduce | flops 512 | bytes 4096 | tf_op jit(solution)/shard_map/psum | solution.py:59
  573.6 4.8 collective-permute-start.2
  611.4 5.0 fusion.68
  616.3 41.7 %all-reduce.2 = (f32[256]{0:T(256)}, f32[256]{0:T(256)}, f32[768]{0:T(1024)}, f32[768]{0:T(1024)}, f32[768]{0:T(1024)}, /*index=5*/f32[768]{0:T(1024)}, f32[768]...) all-reduce(f32[256]{0:T(256)} %get-tuple-element.38, ...), channel_id=1, replica_groups=mesh['dp'=16,'space'=2] {'dp','space'}, use_global_device_ids=true, to_apply=%region_34.35 | all-reduce | flops 10496 | bytes 83968 | tf_op jit(solution)/shard_map/psum | solution.py:59
  664.4 4.9 fusion.42
  669.4 5.5 copy.143
  674.9 4.4 fusion.52
  679.4 4.6 fusion.83
  684.7 9.9 fusion.62
  695.3 10.5 fusion.64
  706.6 11.3 fusion.45
  723.8 64.3 %reduce-scatter.41.cloned.1.call-done = f32[768,48]{0,1:T(8,128)} async-done(((f32[768,768]{0,1:T(8,128)}), f32[768,48]{0,1:T(8,128)}) %reduce-scatter.41.cloned.1.call-update) | async-done | bytes 147472 | tf_op jit(solution)/shard_map/reduce_scatter | solution.py:320
  791.4 62.8 %reduce-scatter.31.cloned.1.call-done = f32[3,3,256,16]{2,3,1,0:T(8,128)} async-done(((f32[3,3,256,256]{2,3,1,0:T(8,128)}), f32[3,3,256,16]{2,3,1,0:T(8,128)}) %reduce-scatter.31.cloned.1.call-update) | async-done | bytes 147472 | tf_op jit(solution)/shard_map/reduce_scatter | solution.py:316
  860.0 63.0 %reduce-scatter.35.cloned.1.call-done = f32[1024,48]{0,1:T(8,128)} async-done(((f32[1024,768]{0,1:T(8,128)}), f32[1024,48]{0,1:T(8,128)}) %reduce-scatter.35.cloned.1.call-update) | async-done | bytes 196624 | tf_op jit(solution)/shard_map/reduce_scatter | solution.py:318
  924.7 91.3 %reduce-scatter.39.cloned.1.call-done = f32[768,144]{0,1:T(8,128)} async-done(((f32[768,2304]{0,1:T(8,128)}), f32[768,144]{0,1:T(8,128)}) %reduce-scatter.39.cloned.1.call-update) | async-done | bytes 442384 | tf_op jit(solution)/shard_map/reduce_scatter | solution.py:319
  1019.6 111.9 %reduce-scatter.43.cloned.1.call-done = f32[768,192]{0,1:T(8,128)} async-done(((f32[768,3072]{0,1:T(8,128)}), f32[768,192]{0,1:T(8,128)}) %reduce-scatter.43.cloned.1.call-update) | async-done | bytes 589840 | tf_op jit(solution)/shard_map/reduce_scatter | solution.py:321
  1135.5 111.2 %reduce-scatter.45.cloned.1.call-done = f32[3072,48]{0,1:T(8,128)} async-done(((f32[3072,768]{0,1:T(8,128)}), f32[3072,48]{0,1:T(8,128)}) %reduce-scatter.45.cloned.1.call-update) | async-done | bytes 589840 | tf_op jit(solution)/shard_map/reduce_scatter | solution.py:322
  1248.6 12.9 add_convert_fusion.1
  1274.7 11.0 reduce-scatter.55.cloned.1.call-done
  1288.7 9.4 reduce-scatter.49.cloned.1.call-done
  1303.2 7.8 reduce-scatter.37.cloned.1.call-done
  1312.4 13.9 %reduce-scatter.53.cloned.1.call-done = bf16[384,144]{1,0:T(8,128)(2,1)} async-done(((bf16[768,144]{1,0:T(8,128)(2,1)}), bf16[384,144]{1,0:T(8,128)(2,1)}) %reduce-scatter.53.cloned.1.call-update) | async-done | bytes 110608
  1329.6 12.0 reduce-scatter.57.cloned.1.call-done
  1344.9 11.4 reduce-scatter.47.cloned.1.call-done
  (368 shorter events, 239.4 us)
Async XLA Ops:
  7.2 220.9 %copy-start = (bf16[768,2304]{1,0:T(8,128)(2,1)S(1)}, bf16[768,2304]{1,0:T(8,128)(2,1)}, u32[]{:S(2)}) copy-start(bf16[768,2304]{1,0:T(8,128)(2,1)} %param.47) | copy-start | bytes 10616836
  7.2 47.7 %copy-start.55 = (f32[256]{0:T(256)S(1)}, f32[256]{0:T(256)}, u32[]{:S(2)}) copy-start(f32[256]{0:T(256)} %param.35) | copy-start | bytes 3076
  7.2 49.0 %copy-start.61 = (f32[256]{0:T(256)S(1)}, f32[256]{0:T(256)}, u32[]{:S(2)}) copy-start(f32[256]{0:T(256)} %param.36) | copy-start | bytes 3076
  56.2 40.2 %copy-start.45 = (f32[256]{0:T(256)}, f32[256]{0:T(256)S(1)}, u32[]{:S(2)}) copy-start(f32[256]{0:T(256)S(1)} %get-tuple-element.102) | copy-start | bytes 3076
  56.2 40.2 %copy-start.46 = (f32[256]{0:T(256)}, f32[256]{0:T(256)S(1)}, u32[]{:S(2)}) copy-start(f32[256]{0:T(256)S(1)} %get-tuple-element.105) | copy-start | bytes 3076
  61.5 11.8 collective-permute-start
  66.3 7.0 collective-permute-start.1
  92.2 4.6 copy-start.23
  92.2 4.6 copy-start.21
  92.2 4.6 copy-start.18
  98.7 86.5 %copy-start.43 = (f32[1024]{0:T(1024)S(1)}, f32[1024]{0:T(1024)}, u32[]{:S(2)}) copy-start(f32[1024]{0:T(1024)} %param.41) | copy-start | bytes 12292
  98.7 87.8 %copy-start.58 = (f32[1024]{0:T(1024)S(1)}, f32[1024]{0:T(1024)}, u32[]{:S(2)}) copy-start(f32[1024]{0:T(1024)} %param.42) | copy-start | bytes 12292
  186.5 4.5 copy-start.71
  193.0 7.1 copy-start.69
  193.0 7.1 copy-start.70
  195.2 18.2 %all-to-all-start = ((bf16[6,7,14,768]{3,2,1,0:T(8,128)(2,1)}), bf16[6,7,14,768]{3,2,1,0:T(8,128)(2,1)}, u32[]{:S(2)}, u32[]{:S(2)}) async-start(bf16[6,7,14,768]{3,2,1,0:T(8,128)(2,1)} %reshape.353), calls=%async_computation | async-start | bytes 2064384 | tf_op jit(solution)/shard_map/all_to_all | solution.py:151
  219.4 5.5 copy-start.29
  225.0 7.9 copy-start.53
  228.1 6.0 copy-start.56
  228.1 6.0 copy-start.57
  277.5 8.4 copy-start.4
  296.8 5.3 copy-start.77
  302.1 14.2 %slice-start.2 = ((s8[4718592]{0:T(1024)(128)(4,1)}), s8[4194304]{0:T(1024)(128)(4,1)S(1)}, s32[]{:S(2)}) async-start(s8[4718592]{0:T(1024)(128)(4,1)} %bitcast.97), calls=%async_computation.36 | async-start | bytes 8388608
  306.0 27.8 %copy-start.6 = (f32[780,768]{1,0:T(8,128)}, f32[780,768]{1,0:T(8,128)S(1)}, u32[]{:S(2)}) copy-start(f32[780,768]{1,0:T(8,128)S(1)} %get-tuple-element.113) | copy-start | bytes 7188484
  306.8 27.0 %copy-start.41 = (f32[780]{0:T(1024)}, f32[780]{0:T(1024)S(1)}, u32[]{:S(2)}) copy-start(f32[780]{0:T(1024)S(1)} %fusion.55) | copy-start | bytes 9364
  306.8 9.5 copy-start.7
  306.8 9.5 slice-start.3
  306.8 9.5 copy-start.74
  306.8 22.0 %slice-start = ((s8[4718592]{0:T(1024)(128)(4,1)}), s8[4194304]{0:T(1024)(128)(4,1)S(1)}, s32[]{:S(2)}) async-start(s8[4718592]{0:T(1024)(128)(4,1)} %bitcast.95), calls=%async_computation.34 | async-start | bytes 8388608
  316.3 12.5 slice-start.1
  328.8 5.0 copy-start.82
  352.8 9.4 copy-start.2
  352.8 9.4 copy-start.5
  352.9 9.4 copy-start.17
  372.0 10.5 copy-start.1
  421.5 5.2 copy-start.28
  421.5 5.8 copy-start.34
  421.5 7.7 copy-start.32
  433.6 6.1 copy-start.30
  449.8 16.5 %all-to-all-start.1 = ((bf16[3,14,14,768]{3,2,0,1:T(8,128)(2,1)}), bf16[3,14,14,768]{3,2,0,1:T(8,128)(2,1)}, u32[]{:S(2)}, u32[]{:S(2)}) async-start(bf16[3,14,14,768]{3,2,0,1:T(8,128)(2,1)} %copy.139), calls=%async_computation.1 | async-start | bytes 2064384 | tf_op jit(solution)/shard_map/all_to_all | solution.py:268
  454.2 263.7 %reduce-scatter.33.cloned.1.call-start = ((), (), s32[]{:S(2)}) async-start(), calls=%async_computation.21 | async-start | bytes 1114112 | tf_op jit(solution)/shard_map/reduce_scatter | solution.py:317
  456.9 13.8 %copy-start.36 = (f32[1024]{0:T(1024)S(1)}, f32[1024]{0:T(1024)}, u32[]{:S(2)}) copy-start(f32[1024]{0:T(1024)} %copy-done.35) | copy-start | bytes 12292
  456.9 13.9 %copy-start.38 = (f32[1024]{0:T(1024)S(1)}, f32[1024]{0:T(1024)}, u32[]{:S(2)}) copy-start(f32[1024]{0:T(1024)} %copy-done.37) | copy-start | bytes 12292
  525.1 43.1 %copy-start.62 = (f32[256]{0:T(256)S(1)}, f32[256]{0:T(256)}, u32[]{:S(2)}) copy-start(f32[256]{0:T(256)} %get-tuple-element.103) | copy-start | bytes 3076
  525.1 43.1 %copy-start.65 = (f32[256]{0:T(256)S(1)}, f32[256]{0:T(256)}, u32[]{:S(2)}) copy-start(f32[256]{0:T(256)} %copy-done.63) | copy-start | bytes 3076
  573.6 7.7 collective-permute-start.2
  578.4 6.3 collective-permute-start.3
  581.2 141.1 %reduce-scatter.27.cloned.1.call-start = ((), (), s32[]{:S(2)}) async-start(), calls=%async_computation.18 | async-start | bytes 1114112 | tf_op jit(solution)/shard_map/reduce_scatter | solution.py:315
  611.4 5.0 copy-start.40
  664.4 123.7 %reduce-scatter.41.cloned.1.call-start = ((), (), s32[]{:S(2)}) async-start(), calls=%async_computation.25 | async-start | bytes 2506752 | tf_op jit(solution)/shard_map/reduce_scatter | solution.py:320
  669.4 184.8 %reduce-scatter.31.cloned.1.call-start = ((), (), s32[]{:S(2)}) async-start(), calls=%async_computation.20 | async-start | bytes 2506752 | tf_op jit(solution)/shard_map/reduce_scatter | solution.py:316
  679.3 243.7 %reduce-scatter.35.cloned.1.call-start = ((), (), s32[]{:S(2)}) async-start(), calls=%async_computation.22 | async-start | bytes 3342336 | tf_op jit(solution)/shard_map/reduce_scatter | solution.py:318
  684.1 331.9 %reduce-scatter.39.cloned.1.call-start = ((), (), s32[]{:S(2)}) async-start(), calls=%async_computation.24 | async-start | bytes 7520256 | tf_op jit(solution)/shard_map/reduce_scatter | solution.py:319
  694.6 436.9 %reduce-scatter.43.cloned.1.call-start = ((), (), s32[]{:S(2)}) async-start(), calls=%async_computation.26 | async-start | bytes 10027008 | tf_op jit(solution)/shard_map/reduce_scatter | solution.py:321
  705.9 540.9 %reduce-scatter.45.cloned.1.call-start = ((), (), s32[]{:S(2)}) async-start(), calls=%async_computation.27 | async-start | bytes 10027008 | tf_op jit(solution)/shard_map/reduce_scatter | solution.py:322
  717.9 554.0 %reduce-scatter.51.cloned.1.call-start = ((), (), s32[]{:S(2)}) async-start(), calls=%async_computation.30 | async-start | bytes 98304
  720.9 552.4 %reduce-scatter.29.cloned.1.call-start = ((), (), s32[]{:S(2)}) async-start(), calls=%async_computation.19 | async-start | bytes 49152 | tf_op jit(solution)/shard_map/reduce_scatter | solution.py:325
  723.8 561.9 %reduce-scatter.55.cloned.1.call-start = ((), (), s32[]{:S(2)}) async-start(), calls=%async_computation.32 | async-start | bytes 294912
  791.4 506.8 %reduce-scatter.49.cloned.1.call-start = ((), (), s32[]{:S(2)}) async-start(), calls=%async_computation.29 | async-start | bytes 196608
  859.9 451.1 %reduce-scatter.37.cloned.1.call-start = ((), (), s32[]{:S(2)}) async-start(), calls=%async_computation.23 | async-start | bytes 147456 | tf_op jit(solution)/shard_map/reduce_scatter | solution.py:334
  924.6 324.0 %copy-start.80 = (f32[768]{0:T(1024)S(1)}, f32[768]{0:T(1024)}, u32[]{:S(2)}) copy-start(f32[768]{0:T(1024)} %param.57) | copy-start | bytes 9220
  924.6 401.7 %reduce-scatter.53.cloned.1.call-start = ((), (), s32[]{:S(2)}) async-start(), calls=%async_computation.31 | async-start | bytes 589824
  1019.6 322.0 %reduce-scatter.57.cloned.1.call-start = ((), (), s32[]{:S(2)}) async-start(), calls=%async_computation.33 | async-start | bytes 589824
  1135.3 221.1 %reduce-scatter.47.cloned.1.call-start = ((), (), s32[]{:S(2)}) async-start(), calls=%async_computation.28 | async-start | bytes 442368 | tf_op jit(solution)/shard_map/reduce_scatter | solution.py:346
  (45 other events, 103.6 us)
Sparse Core Ops, SparseCore 0:
  581.3 59.1 reduce-scatter.32
  664.5 57.7 reduce-scatter.26
  726.0 61.9 reduce-scatter.40
  792.2 61.9 reduce-scatter.30
  857.8 65.1 reduce-scatter.34
  926.9 89.0 reduce-scatter.38
  1020.6 110.8 reduce-scatter.42
  1135.6 111.0 reduce-scatter.44
  1249.6 9.6 reduce-scatter.50
  1262.0 9.8 reduce-scatter.28
  1274.7 10.9 reduce-scatter.54
  1287.8 10.2 reduce-scatter.48
  1301.0 9.9 reduce-scatter.36
  1313.2 13.1 reduce-scatter.52
  1328.4 13.1 reduce-scatter.56
  1344.3 12.0 reduce-scatter.46
where the time goes:
time: 1380 us; the launch traced here: 1360 us
  waiting for transfers between devices  591 us (43%)
  blocking collectives  244 us (18%)
  local copies, waits for them, and re-layouts  215 us (16%)
  matrix products  180 us (13%)
  other arithmetic  97.5 us (7%)
  starting transfers between devices  22.3 us (2%)
  between operations  15.2 us (1%)
    psum x3, blocking collectives, batch_stats(): lax.psum((jnp.sum(values, axis=0), jnp.sum(values * values, axis=0)), ('d...  123 us
    psum x3, blocking collectives, batch_back(): lax.psum((jnp.sum(grad_out, axis=0), jnp.sum(grad_out * normed, axis=0)),...  121 us
    reduce_scatter x1, waiting for transfers between devices, shards(): lax.psum_scatter(up_w_grad, 'dp', scatter_dimension=1, tiled=True)  112 us
    reduce_scatter x1, waiting for transfers between devices, shards(): lax.psum_scatter(down_w_grad, 'dp', scatter_dimension=1, tiled=True)  111 us
    reduce_scatter x1, waiting for transfers between devices, shards(): lax.psum_scatter(qkv_w_grad, 'dp', scatter_dimension=1, tiled=True)  91.3 us
    reduce_scatter x1, waiting for transfers between devices, shards(): lax.psum_scatter(out_w_grad, 'dp', scatter_dimension=1, tiled=True)  64.3 us
    reduce_scatter x1, waiting for transfers between devices, shards(): lax.psum_scatter(proj_w_grad, 'dp', scatter_dimension=1, tiled=True)  63 us
    reduce_scatter x1, waiting for transfers between devices, shards(): lax.psum_scatter(conv_mid_grad, 'dp', scatter_dimension=3, tiled=True)  62.8 us
  transfers between devices with their start and end apart: 22, of which 16 were waited for; matrix products, arithmetic and copies ran while one was open for 12% of the time, Pallas kernels for 0%

commit v1 on v0

--- a/solution.py
+++ b/solution.py
@@ -48,16 +48,71 @@
     return centered * lax.rsqrt(spread + eps_layer) * ln_gain + ln_shift
 
 
+EVERY = ("dp", "space")
+
+
+def group_sum(part):
+    count = lax.axis_size(EVERY)
+    copies = jnp.broadcast_to(part[None], (count,) + part.shape)
+    return jnp.sum(lax.all_to_all(copies, EVERY, split_axis=0, concat_axis=0, tiled=True), axis=0)
+
+
+def vector_sums(vectors):
+    count = lax.axis_size(EVERY)
+    sizes = [v.shape[0] for v in vectors]
+    flat = jnp.concatenate(vectors)
+    chunk = -(-flat.shape[0] // (count * 128)) * 128
+    flat = jnp.pad(flat, (0, chunk * count - flat.shape[0])).reshape(count, chunk)
+    mine = jnp.sum(lax.all_to_all(flat, EVERY, split_axis=0, concat_axis=0, tiled=True), axis=0)
+    copies = jnp.broadcast_to(mine[None], (count, chunk))
+    whole = lax.all_to_all(copies, EVERY, split_axis=0, concat_axis=0, tiled=True).reshape(-1)
+    out, at = [], 0
+    for size in sizes:
+        out.append(whole[at : at + size])
+        at += size
+    return out
+
+
+def halve_axis(x, axis, bit):
+    size = lax.axis_size("dp")
+    mine = (lax.axis_index("dp") // bit) % 2
+    keep = lax.dynamic_index_in_dim(x, mine, axis, keepdims=True)
+    send = lax.dynamic_index_in_dim(x, 1 - mine, axis, keepdims=True)
+    return keep + lax.ppermute(send, "dp", [(j, j ^ bit) for j in range(size)])
+
+
+def halve_space(x, axis):
+    mine = lax.axis_index("space")
+    keep = lax.dynamic_index_in_dim(x, mine, axis, keepdims=True)
+    send = lax.dynamic_index_in_dim(x, 1 - mine, axis, keepdims=True)
+    return keep + lax.ppermute(send, "space", [(0, 1), (1, 0)])
+
+
+def scattered(grad_t, order):
+    size = lax.axis_size("dp")
+    bits = size.bit_length() - 1
+    cols, rows = grad_t.shape
+    x = grad_t.astype(jnp.bfloat16).reshape((2,) * bits + (cols // size, 2, rows // 2))
+    x = halve_axis(x, bits - 1, 1)
+    rest = list(range(1, bits))
+    rest = rest[order % len(rest):] + rest[: order % len(rest)] if order else rest
+    stages = [("dp", b) for b in rest]
+    stages.insert((0, 1, len(stages))[order % 3], ("space", 0))
+    for kind, b in stages:
+        x = halve_space(x, bits + 1) if kind == "space" else halve_axis(x, bits - 1 - b, 1 << b)
+    return x.reshape(cols // size, rows // 2).astype(jnp.float32).T
+
+
 def batch_stats(values, pixel_count):
-    totals = lax.psum((jnp.sum(values, axis=0), jnp.sum(values * values, axis=0)), ("dp", "space"))
+    totals = group_sum(jnp.stack((jnp.sum(values, axis=0), jnp.sum(values * values, axis=0))))
     batch_mean = totals[0] / pixel_count
     spread = totals[1] / pixel_count - batch_mean * batch_mean
     return (batch_mean, lax.rsqrt(spread + eps_batch))
 
 
 def batch_back(grad_out, normed, inv_std, bn_gain, pixel_count):
-    totals = lax.psum(
-        (jnp.sum(grad_out, axis=0), jnp.sum(grad_out * normed, axis=0)), ("dp", "space")
+    totals = group_sum(
+        jnp.stack((jnp.sum(grad_out, axis=0), jnp.sum(grad_out * normed, axis=0)))
     )
     grad_in = (
         bn_gain
@@ -214,15 +269,15 @@
     grad_top = cotangent.astype(jnp.float32).reshape(rows_all, width)
     down_b_grad = jnp.sum(grad_top, axis=0)
     branch_low = grad_top.astype(jnp.bfloat16)
-    down_w_grad = weight_grad(gelu_low, branch_low)
+    down_w_grad = weight_grad(branch_low, gelu_low)
     gelu_grad = gelu_pull(by_transpose(branch_low, down_w))[0].astype(jnp.bfloat16)
     up_b_grad = jnp.sum(gelu_grad.astype(jnp.float32), axis=0)
-    up_w_grad = weight_grad(z_two, gelu_grad)
+    up_w_grad = weight_grad(gelu_grad, z_two)
     norm_grad_two, ln2_gain_grad, ln2_shift_grad = ln_two_pull(by_transpose(gelu_grad, up_w))
     resid_grad = grad_top + norm_grad_two
     out_b_grad = jnp.sum(resid_grad, axis=0)
     proj_low = resid_grad.astype(jnp.bfloat16)
-    out_w_grad = weight_grad(attn_out, proj_low)
+    out_w_grad = weight_grad(proj_low, attn_out)
     attn_grad = (
         by_transpose(proj_low, out_w).astype(jnp.bfloat16).reshape(examples, seq_len, heads, HD)
     )
@@ -254,7 +309,7 @@
         ],
         axis=1,
     )
-    qkv_w_grad = weight_grad(z_one, qkv_grad)
+    qkv_w_grad = weight_grad(qkv_grad, z_one)
     query_b_grad = jnp.sum(query_grad.astype(jnp.float32).reshape(rows_all, width), axis=0)
     value_b_grad = jnp.sum(value_grad.astype(jnp.float32).reshape(rows_all, width), axis=0)
     norm_grad_one, ln1_gain_grad, ln1_shift_grad = ln_one_pull(
@@ -269,19 +324,19 @@
         image_tok_grad, "space", split_axis=1, concat_axis=0, tiled=True
     ).reshape(-1, width)
     proj_b_grad = jnp.sum(back_bands.astype(jnp.float32), axis=0)
-    proj_w_grad = weight_grad(stem_out, back_bands)
+    proj_w_grad = weight_grad(back_bands, stem_out)
     relu_grad_three = smooth_three_pull(by_transpose(back_bands, proj_w))[0]
     act_grad_three, bn3_gain_grad, bn3_shift_grad = batch_back(
         relu_grad_three, norm_three, rstd_three, bn3_gain, pixel_count
     )
     low_three = act_grad_three.astype(jnp.bfloat16)
-    conv_out_grad = weight_grad(relu_two, low_three)
+    conv_out_grad = weight_grad(low_three, relu_two)
     relu_grad_two = smooth_two_pull(by_transpose(low_three, conv_out_w))[0]
     act_grad_two, bn2_gain_grad, bn2_shift_grad = batch_back(
         relu_grad_two, norm_two, rstd_two, bn2_gain, pixel_count
     )
     low_two = act_grad_two.astype(jnp.bfloat16)
-    conv_mid_grad = weight_grad(patch_fwd, low_two).reshape(3, 3, middle, middle)
+    conv_mid_grad = weight_grad(low_two, patch_fwd)
     halo_two = padded_2(low_two.reshape(band_ex, band_rows, band_cols, middle), (("space", 1),), 1)
     patch_back = conv_taps(band_halo_pad(halo_two), band_rows, band_cols, True)
     flipped_w = jnp.transpose(conv_mid_w, (0, 1, 3, 2)).reshape(9 * middle, middle)
@@ -290,14 +345,14 @@
         relu_grad_one, norm_one, rstd_one, bn1_gain, pixel_count
     )
     low_one = act_grad_one.astype(jnp.bfloat16)
-    conv_in_grad = weight_grad(x_flat, low_one)
+    conv_in_grad = weight_grad(low_one, x_flat)
     image_grad = (
         (by_transpose(low_one, conv_in_w) + relu_grad_three)
         .astype(jnp.bfloat16)
         .reshape(image_in.shape)
     )
-    small_sums = lax.psum(
-        (
+    small_sums = vector_sums(
+        [
             proj_b_grad,
             ln1_gain_grad,
             ln1_shift_grad,
@@ -308,44 +363,19 @@
             ln2_shift_grad,
             up_b_grad,
             down_b_grad,
-        ),
-        ("dp", "space"),
-    )
-    data_part = (
-        lax.psum_scatter(conv_in_grad, "dp", scatter_dimension=1, tiled=True),
-        lax.psum_scatter(conv_mid_grad, "dp", scatter_dimension=3, tiled=True),
-        lax.psum_scatter(conv_out_grad, "dp", scatter_dimension=1, tiled=True),
-        lax.psum_scatter(proj_w_grad, "dp", scatter_dimension=1, tiled=True),
-        lax.psum_scatter(qkv_w_grad, "dp", scatter_dimension=1, tiled=True),
-        lax.psum_scatter(out_w_grad, "dp", scatter_dimension=1, tiled=True),
-        lax.psum_scatter(up_w_grad, "dp", scatter_dimension=1, tiled=True),
-        lax.psum_scatter(down_w_grad, "dp", scatter_dimension=1, tiled=True),
-    )
+        ]
+    )
+    mid_t = conv_mid_grad.reshape(middle, 9, 2, middle // 2).transpose(0, 2, 1, 3).reshape(middle, -1)
+    mid_out = scattered(mid_t, 2)
     reduced = (
-        lax.psum_scatter(
-            data_part[0].astype(jnp.bfloat16), "space", scatter_dimension=0, tiled=True
-        ).astype(jnp.float32),
-        lax.psum_scatter(
-            data_part[1].astype(jnp.bfloat16), "space", scatter_dimension=2, tiled=True
-        ).astype(jnp.float32),
-        lax.psum_scatter(
-            data_part[2].astype(jnp.bfloat16), "space", scatter_dimension=0, tiled=True
-        ).astype(jnp.float32),
-        lax.psum_scatter(
-            data_part[3].astype(jnp.bfloat16), "space", scatter_dimension=0, tiled=True
-        ).astype(jnp.float32),
-        lax.psum_scatter(
-            data_part[4].astype(jnp.bfloat16), "space", scatter_dimension=0, tiled=True
-        ).astype(jnp.float32),
-        lax.psum_scatter(
-            data_part[5].astype(jnp.bfloat16), "space", scatter_dimension=0, tiled=True
-        ).astype(jnp.float32),
-        lax.psum_scatter(
-            data_part[6].astype(jnp.bfloat16), "space", scatter_dimension=0, tiled=True
-        ).astype(jnp.float32),
-        lax.psum_scatter(
-            data_part[7].astype(jnp.bfloat16), "space", scatter_dimension=0, tiled=True
-        ).astype(jnp.float32),
+        scattered(conv_in_grad, 0),
+        mid_out.reshape(3, 3, middle // 2, mid_out.shape[1]),
+        scattered(conv_out_grad, 1),
+        scattered(proj_w_grad, 2),
+        scattered(qkv_w_grad, 2),
+        scattered(out_w_grad, 1),
+        scattered(up_w_grad, 2),
+        scattered(down_w_grad, 1),
     )
     return (
         block_out,

time: 1380 us -> 873 us (0.63)
  waiting for transfers between devices: 591 us -> 177 us
  blocking collectives: 244 us -> 14.8 us
  local copies, waits for them, and re-layouts: 215 us -> 312 us
  starting transfers between devices: 22.3 us -> 83 us
  matrix products: 180 us -> 162 us
    reduce_scatter x11 -> x0, waiting for transfers between devices: 525 us -> none  [the longest x1 112 us: shards(): lax.psum_scatter(up_w_grad, 'dp', scatter_dimension=1, tiled=True)]
    psum x6 -> x0, blocking collectives: 244 us -> none  [the longest x3 123 us: batch_stats(): lax.psum((jnp.sum(values, axis=0), jnp.sum(values * values, axis=0)), ('d...]
    ppermute x0 -> x40, waiting for transfers between devices: none -> 157 us  [the longest x32 139 us: halve_axis(): return keep + lax.ppermute(send, 'dp', [(j, j ^ bit) for j in range(size)])]
    unnamed x21 -> x0, waiting for transfers between devices: 46.6 us -> none
    reshape x0 -> x8, local copies, waits for them, and re-layouts: none -> 42.9 us  [the longest x7 41.4 us: scattered(): grad_t.astype(jnp.bfloat16)]
    dynamic_slice x0 -> x42, local copies, waits for them, and re-layouts: none -> 39.6 us  [the longest x6 23 us: halve_axis(): keep = lax.dynamic_index_in_dim(x, mine, axis, keepdims=True)]
    ppermute x0 -> x40, starting transfers between devices: none -> 34.5 us  [the longest x32 27 us: halve_axis(): return keep + lax.ppermute(send, 'dp', [(j, j ^ bit) for j in range(size)])]
    all_to_all x0 -> x7, starting transfers between devices: none -> 29.7 us  [the longest x5 20.1 us: group_sum(): lax.all_to_all(copies, EVERY, split_axis=0, concat_axis=0, tiled=True)]
  transfers between devices with their start and end apart: 22 -> 53, of which waited for: 16 -> 19; matrix products, arithmetic and copies ran while one was open for 12% -> 27% of each run, Pallas kernels for 0% -> 0%
where the time goes in v1:
time: 873 us; the launch traced here: 860 us
  local copies, waits for them, and re-layouts  312 us (36%)
  waiting for transfers between devices  177 us (20%)
  matrix products  162 us (19%)
  other arithmetic  109 us (12%)
  starting transfers between devices  83 us (10%)
  blocking collectives  14.8 us (2%)
    ppermute x32, waiting for transfers between devices, halve_axis(): return keep + lax.ppermute(send, 'dp', [(j, j ^ bit) for j in range(size)])  139 us
    dot_general x9, matrix products, matmul(): return jnp.dot(left, right, preferred_element_type=jnp.float32)  42 us
    reshape x7, local copies, waits for them, and re-layouts, scattered(): grad_t.astype(jnp.bfloat16)  41.4 us
    dot_general x7, matrix products, by_transpose(): lax.dot_general(left, right, (((1,), (1,)), ((), ())), preferred_element_...  37.9 us
    dot_general x8, matrix products, weight_grad(): lax.dot_general(left, right, (((0,), (0,)), ((), ())), preferred_element_...  37.6 us
    unnamed x267, local copies, waits for them, and re-layouts  32 us
    concatenate x18, local copies, waits for them, and re-layouts, conv_taps(): return jnp.concatenate(tap_list, axis=-1).reshape(-1, 9 * padded.shape[-1])  28.6 us
    ppermute x32, starting transfers between devices, halve_axis(): return keep + lax.ppermute(send, 'dp', [(j, j ^ bit) for j in range(size)])  27 us
  transfers between devices with their start and end apart: 53, of which 19 were waited for; matrix products, arithmetic and copies ran while one was open for 27% of the time, Pallas kernels for 0%

profile of v1, /device:TPU:0, one launch (start us, length us, event | category | flops | bytes accessed | tf_op | source)
XLA Modules:
  0.0 860.2 jit_solution(7701784339124353181)
XLA Ops:
  6.5 14.8 %all_to_all.69 = f32[32,2,256]{2,1,0:T(2,128)} all-to-all(f32[32,2,256]{2,1,0:T(2,128)S(1)} %broadcast_in_dim.36), channel_id=1, replica_groups=mesh['dp'=16,'space'=2] {'dp','space'}, dimensions={0} | all-to-all | bytes 131072 | tf_op jit(solution)/shard_map/all_to_all | solution.py:57
  63.1 4.0 all-to-all-start.1
  69.2 5.5 all-to-all-done.1
  85.4 8.3 all-to-all-done.2
  103.5 4.6 all-to-all-start.3
  111.4 6.3 dot_general.119
  136.9 4.9 fusion.71
  144.8 4.8 reshape.512
  149.6 5.7 copy.257
  155.3 4.8 reshape.513
  160.0 5.7 copy.258
  165.8 4.8 reshape.511
  170.5 6.1 copy.259
  176.6 10.1 %fusion.91 = (f32[3,12,260]{2,1,0:T(8,128)S(1)}, f32[3,12,260,260]{2,3,1,0:T(8,128)}) fusion(bf16[3,260,12,64]{1,3,2,0:T(8,128)(2,1)} %copy.257, bf16[3,260,12,64]{1,3,2,0:T(8,128)(2,1)} %copy.258, pred[3,260,260]{1,2,0:T(8,128)(4,1)} %or_and_fusion), kind=kOutput, calls=%fused_computation.326 | convolution fusion | flops 318792256 | bytes 12370800 | tf_op jit(solution)/shard_map/bqhe,bkhe->bhqk/dot_general | solution.py:240
  186.7 7.7 fusion
  195.1 8.0 convert_bitcast_fusion.1
  206.0 5.3 reshape.472
  211.3 3.8 fusion.92
  215.9 9.3 %fusion.72 = f32[780,3072]{1,0:T(8,128)} fusion(bf16[768,3072]{1,0:T(8,128)(2,1)} %param.54, f32[780,768]{1,0:T(8,128)S(1)} %get-tuple-element.256, f32[768]{0:T(1024)S(1)} %copy-done.107, f32[768]{0:T(1024)S(1)} %copy-done.88, f32[780]{0:T(1024)S(1)} %fusion.65, f32[780]{0:T(1024)S(1)} %broadcast_multiply_fusion.1), kind=kOutput, calls=%fused_computation.310 | convolution fusion | flops 3683496960 | bytes 16711776 | tf_op jit(solution)/shard_map/dot_general | solution.py:29
  225.2 11.5 %fusion.13 = bf16[768,3072]{0,1:T(8,128)(2,1)} fusion(f32[780,768]{1,0:T(8,128)S(1)} %copy-done.8, f32[780,3072]{1,0:T(8,128)} %fusion.72, f32[3072]{0:T(1024)S(1)} %copy-done.103), kind=kOutput, calls=%fused_computation.25 | convolution fusion | flops 3707421696 | bytes 16711680 | tf_op jit(solution)/shard_map/dot_general | solution.py:39
  236.8 12.5 %convert_reduce_fusion = (f32[3072]{0:T(1024)}, bf16[780,3072]{1,0:T(8,128)(2,1)S(1)}) fusion(f32[780,3072]{1,0:T(8,128)} %fusion.72, f32[3072]{0:T(1024)S(1)} %copy-done.103, bf16[3072,768]{1,0:T(8,128)(2,1)S(1)} %bitcast.222, f32[780,768]{1,0:T(8,128)S(1)} %copy-done.8), kind=kOutput, calls=%fused_computation.17 | convolution fusion | flops 3736209408 | bytes 21516288 | tf_op jit(solution)/shard_map/dot_general | solution.py:33
  249.2 4.9 multiply_reduce_fusion.4
  254.1 7.8 convolution_convert_fusion.1
  272.0 4.7 reshape.514
  276.8 5.7 copy.263
  282.5 8.7 %convert_reduce_fusion.1 = (f32[12,64]{1,0:T(8,128)S(1)}, bf16[3,260,12,64]{1,3,2,0:T(8,128)(2,1)S(1)}) fusion(bf16[3,260,12,64]{1,3,2,0:T(8,128)(2,1)} %copy.263, f32[3,12,260,260]{2,3,1,0:T(8,128)} %get-tuple-element.254, f32[3,12,260]{2,1,0:T(8,128)} %log_add_fusion), kind=kOutput, calls=%fused_computation.29 | convolution fusion | flops 318164352 | bytes 12171072 | tf_op jit(solution)/shard_map/bhqk,bqhe->bkhe/dot_general | solution.py:285
  291.2 9.8 %multiply_reduce_fusion = (f32[3,12,260]{2,1,0:T(8,128)S(1)}, f32[3,12,260,260]{2,3,1,0:T(8,128)}) fusion(f32[3,12,260,260]{2,3,1,0:T(8,128)} %get-tuple-element.254, f32[3,12,260]{2,1,0:T(8,128)S(1)} %copy-done.24, bf16[3,260,12,64]{1,3,2,0:T(8,128)(2,1)S(1)} %copy-done.2, bf16[3,260,12,64]{1,3,2,0:T(8,128)(2,1)S(1)} %copy-done.5), kind=kOutput, calls=%fused_computation.1 | convolution fusion | flops 318792256 | bytes 21939840 | tf_op jit(solution)/shard_map/bqhe,bkhe->bhqk/dot_general | solution.py:291
  301.1 10.9 %multiply_convert_fusion = bf16[3,12,260,260]{2,3,1,0:T(8,128)(2,1)S(1)} fusion(f32[3,12,260,260]{2,3,1,0:T(8,128)} %get-tuple-element.259, f32[3,12,260,260]{2,3,1,0:T(8,128)} %get-tuple-element.254, f32[3,12,260]{2,1,0:T(8,128)S(1)} %get-tuple-element.258, f32[3,12,260]{2,1,0:T(8,128)S(1)} %copy-done.24), kind=kLoop, calls=%fused_computation | loop fusion | flops 9734400 | bytes 24410880 | tf_op jit(solution)/shard_map/convert_element_type | solution.py:295
  312.0 4.0 fusion.34
  322.6 5.3 reshape.479
  327.9 4.4 copy.270
  332.2 5.3 reshape.478
  337.5 4.4 copy.267
  341.9 5.4 reshape.477
  350.9 5.1 multiply_reduce_fusion.6
  356.0 5.9 convolution_convert_fusion.2
  366.2 4.2 multiply_reduce_fusion.5
  372.9 3.8 fusion.18
  378.6 12.1 %add_convert_fusion.1 = bf16[780,768]{1,0:T(8,128)(2,1)} fusion(f32[780,768]{1,0:T(8,128)S(1)} %copy-done.7, bf16[3072,768]{1,0:T(8,128)(2,1)} %param.56, f32[768]{0:T(1024)S(1)} %copy-done.109, f32[780,3072]{1,0:T(8,128)} %fusion.72, f32[3072]{0:T(1024)S(1)} %copy-done.104), kind=kOutput, calls=%fused_computation.65 | convolution fusion | flops 3706260480 | bytes 17912832 | tf_op jit(solution)/shard_map/dot_general | solution.py:29
  393.0 6.6 copy.296
  399.7 11.7 %reshape.494 = bf16[2,2,2,2,48,2,1536]{6,5,4,3,2,1,0:T(2,128)(2,1)} reshape(bf16[768,3072]{1,0:T(8,128)(2,1)} %copy.296) | data formatting | bytes 9437184 | tf_op jit(solution)/shard_map/reshape | solution.py:95
  411.3 4.7 constant_dynamic-slice_fusion.4
  416.0 10.1 %reshape.493 = bf16[2,2,2,2,192,2,384]{6,5,4,3,2,1,0:T(2,128)(2,1)} reshape(bf16[3072,768]{1,0:T(8,128)(2,1)} %convolution_convert_fusion.1) | data formatting | bytes 9437184 | tf_op jit(solution)/shard_map/reshape | solution.py:95
  434.6 4.4 all-to-all-start.4
  439.0 8.2 constant_dynamic-slice_fusion.10
  455.1 8.0 reshape.491
  463.0 5.6 constant_dynamic-slice_fusion.22
  480.8 8.0 fusion.73
  492.9 6.1 all-to-all-start.9
  504.4 3.9 reshape.490
  509.1 4.8 all-to-all-start.5
  546.4 4.8 all-to-all-start.6
  568.8 4.2 collective-permute-start.2
  657.4 16.3 %collective-permute-done.20 = bf16[1,2,2,1,48,2,512]{6,4,5,3,2,1,0:T(8,128)(2,1)S(1)} collective-permute-done((bf16[1,2,2,1,48,2,512]{6,4,5,3,2,1,0:T(8,128)(2,1)}, bf16[1,2,2,1,48,2,512]{6,4,5,3,2,1,0:T(8,128)(2,1)S(1)}, u32[]{:S(2)}, u32[]{:S(2)}) %collective-permute-start.20) | collective-permute-done | bytes 393248 | tf_op jit(solution)/shard_map/ppermute | solution.py:81
  675.3 3.8 collective-permute-done.5
  684.3 3.8 collective-permute-done.7
  688.2 7.4 collective-permute-done.8
  702.4 21.9 %collective-permute-done.10 = bf16[1,2,2,1,16,2,1152]{6,4,3,2,1,0,5:T(8,128)(2,1)S(1)} collective-permute-done((bf16[1,2,2,1,16,2,1152]{6,4,3,2,1,0,5:T(8,128)(2,1)S(1)}, bf16[1,2,2,1,16,2,1152]{6,4,3,2,1,0,5:T(8,128)(2,1)S(1)}, u32[]{:S(2)}, u32[]{:S(2)}) %collective-permute-start.10) | collective-permute-done | bytes 294944 | tf_op jit(solution)/shard_map/ppermute | solution.py:81
  731.1 13.3 %collective-permute-done.12 = bf16[1,1,1,1,16,2,1152]{6,4,3,2,1,0,5:T(8,128)(2,1)S(1)} collective-permute-done((bf16[1,1,1,1,16,2,1152]{6,4,3,2,1,0,5:T(8,128)(2,1)S(1)}, bf16[1,1,1,1,16,2,1152]{6,4,3,2,1,0,5:T(8,128)(2,1)S(1)}, u32[]{:S(2)}, u32[]{:S(2)}) %collective-permute-start.12) | collective-permute-done | bytes 73760 | tf_op jit(solution)/shard_map/ppermute | solution.py:81
  755.3 4.8 dynamic-slice_add_fusion
  768.2 46.3 %collective-permute-done.27 = bf16[1,1,1,1,144,2,384]{6,4,5,3,2,1,0:T(8,128)(2,1)S(1)} collective-permute-done((bf16[1,1,1,1,144,2,384]{6,4,5,3,2,1,0:T(8,128)(2,1)S(1)}, bf16[1,1,1,1,144,2,384]{6,4,5,3,2,1,0:T(8,128)(2,1)S(1)}, u32[]{:S(2)}, u32[]{:S(2)}) %collective-permute-start.27) | collective-permute-done | bytes 221216 | tf_op jit(solution)/shard_map/ppermute | solution.py:81
  821.4 10.1 %collective-permute-done.41 = bf16[2,1,2,1,48,1,1536]{6,4,5,3,2,1,0:T(8,128)(2,1)S(1)} collective-permute-done((bf16[2,1,2,1,48,1,1536]{6,4,5,3,2,1,0:T(8,128)(2,1)S(1)}, bf16[2,1,2,1,48,1,1536]{6,4,5,3,2,1,0:T(8,128)(2,1)S(1)}, u32[]{:S(2)}, u32[]{:S(2)}) %collective-permute-start.41) | collective-permute-done | bytes 589856 | tf_op jit(solution)/shard_map/ppermute | solution.py:88
  837.2 10.5 %collective-permute-done.42 = bf16[1,1,2,1,48,1,1536]{6,4,5,3,2,1,0:T(8,128)(2,1)S(1)} collective-permute-done((bf16[1,1,2,1,48,1,1536]{6,4,5,3,2,1,0:T(8,128)(2,1)S(1)}, bf16[1,1,2,1,48,1,1536]{6,4,5,3,2,1,0:T(8,128)(2,1)S(1)}, u32[]{:S(2)}, u32[]{:S(2)}) %collective-permute-start.42) | collective-permute-done | bytes 294944 | tf_op jit(solution)/shard_map/ppermute | solution.py:81
  849.5 8.2 collective-permute-done.43
  (583 shorter events, 358.8 us)
Async XLA Ops:
  0.7 136.2 %copy-start = (bf16[768,2304]{1,0:T(8,128)(2,1)S(1)}, bf16[768,2304]{1,0:T(8,128)(2,1)}, u32[]{:S(2)}) copy-start(bf16[768,2304]{1,0:T(8,128)(2,1)} %param.47) | copy-start | bytes 10616836
  0.7 21.5 %copy-start.80 = (f32[256]{0:T(256)S(1)}, f32[256]{0:T(256)}, u32[]{:S(2)}) copy-start(f32[256]{0:T(256)} %param.35) | copy-start | bytes 3076
  22.2 38.0 %copy-start.69 = (f32[1,256]{1,0:T(1,128)}, f32[1,256]{1,0:T(1,128)S(1)}, u32[]{:S(2)}) copy-start(f32[1,256]{1,0:T(1,128)S(1)} %get-tuple-element.248) | copy-start | bytes 3076
  22.2 88.6 %copy-start.60 = (f32[1,256]{1,0:T(1,128)}, f32[1,256]{1,0:T(1,128)S(1)}, u32[]{:S(2)}) copy-start(f32[1,256]{1,0:T(1,128)S(1)} %get-tuple-element.249) | copy-start | bytes 3076
  27.6 9.5 %collective-permute-start = (bf16[6,1,14,256]{3,2,1,0:T(8,128)(2,1)}, bf16[6,1,14,256]{3,2,1,0:T(8,128)(2,1)}, u32[]{:S(2)}, u32[]{:S(2)}) collective-permute-start(bf16[6,1,14,256]{3,2,1,0:T(8,128)(2,1)} %get-tuple-element.228), channel_id=1, source_target_pairs={{0,1},{2,3},{4,5},{6,7},{8,9},{10,11},{12,13},{14,15},{16,17},{18,... | collective-permute-start | bytes 129032 | tf_op jit(solution)/shard_map/ppermute | solution.py:22
  30.5 6.6 collective-permute-start.1
  63.1 11.6 %all-to-all-start.1 = ((f32[32,2,256]{2,1,0:T(2,128)}), f32[32,2,256]{2,1,0:T(2,128)}, u32[]{:S(2)}, u32[]{:S(2)}) async-start(f32[32,2,256]{2,1,0:T(2,128)} %broadcast_in_dim.37), calls=%async_computation.1 | async-start | bytes 131072 | tf_op jit(solution)/shard_map/all_to_all | solution.py:57
  79.7 14.0 %all-to-all-start.2 = ((f32[32,2,1024]{2,1,0:T(2,128)}), f32[32,2,1024]{2,1,0:T(2,128)}, u32[]{:S(2)}, u32[]{:S(2)}) async-start(f32[32,2,1024]{2,1,0:T(2,128)} %broadcast_in_dim.38), calls=%async_computation.2 | async-start | bytes 524288 | tf_op jit(solution)/shard_map/all_to_all | solution.py:57
  94.8 23.5 %copy-start.50 = (f32[1,1024]{1,0:T(1,128)}, f32[1,1024]{1,0:T(1,128)S(1)}, u32[]{:S(2)}) copy-start(f32[1,1024]{1,0:T(1,128)S(1)} %get-tuple-element.235) | copy-start | bytes 12292
  103.5 18.7 %all-to-all-start.3 = ((bf16[6,7,14,768]{3,2,1,0:T(8,128)(2,1)}), bf16[6,7,14,768]{3,2,1,0:T(8,128)(2,1)}, u32[]{:S(2)}, u32[]{:S(2)}) async-start(bf16[6,7,14,768]{3,2,1,0:T(8,128)(2,1)} %reshape.467), calls=%async_computation.3 | async-start | bytes 2064384 | tf_op jit(solution)/shard_map/all_to_all | solution.py:206
  215.1 46.8 %copy-start.6 = (f32[780,768]{1,0:T(8,128)}, f32[780,768]{1,0:T(8,128)S(1)}, u32[]{:S(2)}) copy-start(f32[780,768]{1,0:T(8,128)S(1)} %get-tuple-element.256) | copy-start | bytes 7188484
  215.9 20.8 %slice-start.2 = ((s8[4718592]{0:T(1024)(128)(4,1)}), s8[4194304]{0:T(1024)(128)(4,1)S(1)}, s32[]{:S(2)}) async-start(s8[4718592]{0:T(1024)(128)(4,1)} %bitcast.221), calls=%async_computation.12 | async-start | bytes 8388608
  225.2 24.0 %slice-start = ((s8[4718592]{0:T(1024)(128)(4,1)}), s8[4194304]{0:T(1024)(128)(4,1)S(1)}, s32[]{:S(2)}) async-start(s8[4718592]{0:T(1024)(128)(4,1)} %bitcast.219), calls=%async_computation.10 | async-start | bytes 8388608
  416.0 339.4 %collective-permute-start.39 = (bf16[2,2,2,1,48,2,1536]{6,5,4,3,2,1,0:T(2,128)(2,1)}, bf16[2,2,2,1,48,2,1536]{6,5,4,3,2,1,0:T(2,128)(2,1)}, u32[]{:S(2)}, u32[]{:S(2)}) collective-permute-start(bf16[2,2,2,1,48,2,1536]{6,5,4,3,2,1,0:T(2,128)(2,1)} %constant_dynamic-slice_fusion.4), channel_id=1, source_target_pairs={{0,2},{2,0},{4,6},{6,4},{8,10},{10,8},{12,14},{14,12},{16,18},{18,... | collective-permute-start | bytes 7077896 | tf_op jit(solution)/shard_map/ppermute | solution.py:81
  434.6 35.6 %all-to-all-start.4 = ((bf16[3,14,14,768]{3,2,0,1:T(8,128)(2,1)}), bf16[3,14,14,768]{3,2,0,1:T(8,128)(2,1)}, u32[]{:S(2)}, u32[]{:S(2)}) async-start(bf16[3,14,14,768]{3,2,0,1:T(8,128)(2,1)} %copy.274), calls=%async_computation.4 | async-start | bytes 2064384 | tf_op jit(solution)/shard_map/all_to_all | solution.py:323
  449.7 49.3 %collective-permute-start.29 = (bf16[2,2,2,1,48,2,384]{6,4,5,3,2,1,0:T(8,128)(2,1)}, bf16[2,2,2,1,48,2,384]{6,4,5,3,2,1,0:T(8,128)(2,1)}, u32[]{:S(2)}, u32[]{:S(2)}) collective-permute-start(bf16[2,2,2,1,48,2,384]{6,4,5,3,2,1,0:T(8,128)(2,1)} %copy.345), channel_id=1, source_target_pairs={{0,2},{2,0},{4,6},{6,4},{8,10},{10,8},{12,14},{14,12},{16,18},{18,... | collective-permute-start | bytes 1769480 | tf_op jit(solution)/shard_map/ppermute | solution.py:81
  454.4 310.6 %collective-permute-start.34 = (bf16[2,2,2,1,192,2,384]{6,4,5,3,2,1,0:T(8,128)(2,1)}, bf16[2,2,2,1,192,2,384]{6,4,5,3,2,1,0:T(8,128)(2,1)}, u32[]{:S(2)}, u32[]{:S(2)}) collective-permute-start(bf16[2,2,2,1,192,2,384]{6,4,5,3,2,1,0:T(8,128)(2,1)} %copy.347), channel_id=1, source_target_pairs={{0,2},{2,0},{4,6},{6,4},{8,10},{10,8},{12,14},{14,12},{16,18},{18,... | collective-permute-start | bytes 7077896 | tf_op jit(solution)/shard_map/ppermute | solution.py:81
  477.2 14.2 %all-to-all-start.8 = ((f32[32,1,384]{2,1,0:T(1,128)}), f32[32,1,384]{2,1,0:T(1,128)}, u32[]{:S(2)}, u32[]{:S(2)}) async-start(f32[32,1,384]{2,1,0:T(1,128)} %bitcast.168), calls=%async_computation.8 | async-start | bytes 98304 | tf_op jit(solution)/shard_map/all_to_all | solution.py:66
  492.9 15.4 %all-to-all-start.9 = ((f32[32,1,384]{2,1,0:T(1,128)}), f32[32,1,384]{2,1,0:T(1,128)}, u32[]{:S(2)}, u32[]{:S(2)}) async-start(f32[32,1,384]{2,1,0:T(1,128)} %broadcast_in_dim.53), calls=%async_computation.9 | async-start | bytes 98304 | tf_op jit(solution)/shard_map/all_to_all | solution.py:68
  502.0 29.3 %collective-permute-start.30 = (bf16[2,1,2,1,48,2,384]{6,4,5,3,2,1,0:T(8,128)(2,1)}, bf16[2,1,2,1,48,2,384]{6,4,5,3,2,1,0:T(8,128)(2,1)}, u32[]{:S(2)}, u32[]{:S(2)}) collective-permute-start(bf16[2,1,2,1,48,2,384]{6,4,5,3,2,1,0:T(8,128)(2,1)} %constant_dynamic-slice_fusion.14), channel_id=1, source_target_pairs={{0,8},{2,10},{4,12},{6,14},{8,0},{10,2},{12,4},{14,6},{16,24},{18,... | collective-permute-start | bytes 884744 | tf_op jit(solution)/shard_map/ppermute | solution.py:81
  509.1 26.4 %all-to-all-start.5 = ((f32[32,2,1024]{2,1,0:T(2,128)}), f32[32,2,1024]{2,1,0:T(2,128)}, u32[]{:S(2)}, u32[]{:S(2)}) async-start(f32[32,2,1024]{2,1,0:T(2,128)} %broadcast_in_dim.50), calls=%async_computation.5 | async-start | bytes 524288 | tf_op jit(solution)/shard_map/all_to_all | solution.py:57
  518.2 104.9 %collective-permute-start.19 = (bf16[2,2,2,1,48,2,512]{6,4,5,3,2,1,0:T(8,128)(2,1)}, bf16[2,2,2,1,48,2,512]{6,4,5,3,2,1,0:T(8,128)(2,1)}, u32[]{:S(2)}, u32[]{:S(2)}) collective-permute-start(bf16[2,2,2,1,48,2,512]{6,4,5,3,2,1,0:T(8,128)(2,1)} %copy.341), channel_id=1, source_target_pairs={{0,2},{2,0},{4,6},{6,4},{8,10},{10,8},{12,14},{14,12},{16,18},{18,... | collective-permute-start | bytes 2359304 | tf_op jit(solution)/shard_map/ppermute | solution.py:81
  533.8 20.3 %collective-permute-start.31 = (bf16[2,1,2,1,48,1,384]{6,4,5,3,2,1,0:T(8,128)(2,1)}, bf16[2,1,2,1,48,1,384]{6,4,5,3,2,1,0:T(8,128)(2,1)}, u32[]{:S(2)}, u32[]{:S(2)}) collective-permute-start(bf16[2,1,2,1,48,1,384]{6,4,5,3,2,1,0:T(8,128)(2,1)} %constant_dynamic-slice_fusion.13), channel_id=1, source_target_pairs={{0,1},{1,0},{2,3},{3,2},{4,5},{5,4},{6,7},{7,6},{8,9},{9,8},{10,11... | collective-permute-start | bytes 442376 | tf_op jit(solution)/shard_map/ppermute | solution.py:88
  546.4 12.6 %all-to-all-start.6 = ((f32[32,2,256]{2,1,0:T(2,128)}), f32[32,2,256]{2,1,0:T(2,128)}, u32[]{:S(2)}, u32[]{:S(2)}) async-start(f32[32,2,256]{2,1,0:T(2,128)} %broadcast_in_dim.51), calls=%async_computation.6 | async-start | bytes 131072 | tf_op jit(solution)/shard_map/all_to_all | solution.py:57
  556.3 24.4 %collective-permute-start.32 = (bf16[1,1,2,1,48,1,384]{6,4,5,3,2,1,0:T(8,128)(2,1)}, bf16[1,1,2,1,48,1,384]{6,4,5,3,2,1,0:T(8,128)(2,1)}, u32[]{:S(2)}, u32[]{:S(2)}) collective-permute-start(bf16[1,1,2,1,48,1,384]{6,4,5,3,2,1,0:T(8,128)(2,1)} %constant_dynamic-slice_fusion.12), channel_id=1, source_target_pairs={{0,16},{2,18},{4,20},{6,22},{8,24},{10,26},{12,28},{14,30},{16,0},... | collective-permute-start | bytes 221192 | tf_op jit(solution)/shard_map/ppermute | solution.py:81
  568.8 15.5 %collective-permute-start.2 = (bf16[6,1,14,256]{3,2,1,0:T(8,128)(2,1)}, bf16[6,1,14,256]{3,2,1,0:T(8,128)(2,1)}, u32[]{:S(2)}, u32[]{:S(2)}) collective-permute-start(bf16[6,1,14,256]{3,2,1,0:T(8,128)(2,1)} %get-tuple-element.224), channel_id=1, source_target_pairs={{0,1},{2,3},{4,5},{6,7},{8,9},{10,11},{12,13},{14,15},{16,17},{18,... | collective-permute-start | bytes 129032 | tf_op jit(solution)/shard_map/ppermute | solution.py:22
  580.8 6.2 collective-permute-start.3
  584.3 35.3 %collective-permute-start.14 = (bf16[2,2,2,1,64,2,128]{6,4,5,3,2,1,0:T(8,128)(2,1)}, bf16[2,2,2,1,64,2,128]{6,4,5,3,2,1,0:T(8,128)(2,1)}, u32[]{:S(2)}, u32[]{:S(2)}) collective-permute-start(bf16[2,2,2,1,64,2,128]{6,4,5,3,2,1,0:T(8,128)(2,1)} %copy.339), channel_id=1, source_target_pairs={{0,2},{2,0},{4,6},{6,4},{8,10},{10,8},{12,14},{14,12},{16,18},{18,... | collective-permute-start | bytes 786440 | tf_op jit(solution)/shard_map/ppermute | solution.py:81
  587.0 31.1 %collective-permute-start.33 = (bf16[1,1,1,1,48,1,384]{6,4,5,3,2,1,0:T(8,128)(2,1)}, bf16[1,1,1,1,48,1,384]{6,4,5,3,2,1,0:T(8,128)(2,1)}, u32[]{:S(2)}, u32[]{:S(2)}) collective-permute-start(bf16[1,1,1,1,48,1,384]{6,4,5,3,2,1,0:T(8,128)(2,1)} %constant_dynamic-slice_fusion.11), channel_id=1, source_target_pairs={{0,4},{2,6},{4,0},{6,2},{8,12},{10,14},{12,8},{14,10},{16,20},{18,... | collective-permute-start | bytes 110600 | tf_op jit(solution)/shard_map/ppermute | solution.py:81
  614.7 11.5 %all-to-all-start.7 = ((f32[32,2,256]{2,1,0:T(2,128)}), f32[32,2,256]{2,1,0:T(2,128)}, u32[]{:S(2)}, u32[]{:S(2)}) async-start(f32[32,2,256]{2,1,0:T(2,128)} %broadcast_in_dim.52), calls=%async_computation.7 | async-start | bytes 131072 | tf_op jit(solution)/shard_map/all_to_all | solution.py:57
  618.0 78.2 %collective-permute-start.24 = (bf16[2,2,2,1,144,2,384]{6,4,5,3,2,1,0:T(8,128)(2,1)}, bf16[2,2,2,1,144,2,384]{6,4,5,3,2,1,0:T(8,128)(2,1)}, u32[]{:S(2)}, u32[]{:S(2)}) collective-permute-start(bf16[2,2,2,1,144,2,384]{6,4,5,3,2,1,0:T(8,128)(2,1)} %copy.343), channel_id=1, source_target_pairs={{0,2},{2,0},{4,6},{6,4},{8,10},{10,8},{12,14},{14,12},{16,18},{18,... | collective-permute-start | bytes 5308424 | tf_op jit(solution)/shard_map/ppermute | solution.py:81
  621.4 7.8 collective-permute-start.15
  631.5 6.4 collective-permute-start.16
  638.8 5.4 collective-permute-start.17
  644.3 12.1 %collective-permute-start.4 = (bf16[2,2,2,1,16,2,512]{6,4,5,3,2,1,0:T(8,128)(2,1)}, bf16[2,2,2,1,16,2,512]{6,4,5,3,2,1,0:T(8,128)(2,1)}, u32[]{:S(2)}, u32[]{:S(2)}) collective-permute-start(bf16[2,2,2,1,16,2,512]{6,4,5,3,2,1,0:T(8,128)(2,1)} %copy.337), channel_id=1, source_target_pairs={{0,2},{2,0},{4,6},{6,4},{8,10},{10,8},{12,14},{14,12},{16,18},{18,... | collective-permute-start | bytes 786440 | tf_op jit(solution)/shard_map/ppermute | solution.py:81
  644.9 8.1 collective-permute-start.18
  652.9 31.3 %copy-start.18 = (bf16[2,2,2,2,16,2,1152]{6,4,3,2,1,0,5:T(8,128)(2,1)S(1)}, bf16[2,2,2,2,16,2,1152]{6,4,3,2,1,0,5:T(8,128)(2,1)}, u32[]{:S(2)}) copy-start(bf16[2,2,2,2,16,2,1152]{6,4,3,2,1,0,5:T(8,128)(2,1)} %convert_element_type.230) | copy-start | bytes 3538948
  652.9 20.8 %collective-permute-start.20 = (bf16[1,2,2,1,48,2,512]{6,4,5,3,2,1,0:T(8,128)(2,1)}, bf16[1,2,2,1,48,2,512]{6,4,5,3,2,1,0:T(8,128)(2,1)S(1)}, u32[]{:S(2)}, u32[]{:S(2)}) collective-permute-start(bf16[1,2,2,1,48,2,512]{6,4,5,3,2,1,0:T(8,128)(2,1)} %constant_dynamic-slice_fusion.26), channel_id=1, source_target_pairs={{0,16},{2,18},{4,20},{6,22},{8,24},{10,26},{12,28},{14,30},{16,0},... | collective-permute-start | bytes 1179656 | tf_op jit(solution)/shard_map/ppermute | solution.py:81
  656.3 27.8 %collective-permute-start.9 = (bf16[2,2,2,1,16,2,1152]{6,4,3,2,1,0,5:T(8,128)(2,1)}, bf16[2,2,2,1,16,2,1152]{6,4,3,2,1,0,5:T(8,128)(2,1)S(1)}, u32[]{:S(2)}, u32[]{:S(2)}) collective-permute-start(bf16[2,2,2,1,16,2,1152]{6,4,3,2,1,0,5:T(8,128)(2,1)} %constant_dynamic-slice_fusion.40), channel_id=1, source_target_pairs={{0,2},{2,0},{4,6},{6,4},{8,10},{10,8},{12,14},{14,12},{16,18},{18,... | collective-permute-start | bytes 1769480 | tf_op jit(solution)/shard_map/ppermute | solution.py:81
  657.4 38.9 %copy-start.13 = (bf16[2,2,2,1,144,2,384]{6,5,4,3,2,1,0:T(2,128)(2,1)S(1)}, bf16[2,2,2,1,144,2,384]{6,5,4,3,2,1,0:T(2,128)(2,1)}, u32[]{:S(2)}) copy-start(bf16[2,2,2,1,144,2,384]{6,5,4,3,2,1,0:T(2,128)(2,1)} %get-tuple-element.200) | copy-start | bytes 5308420
  673.7 5.4 collective-permute-start.5
  679.2 4.3 collective-permute-start.6
  683.5 18.7 %collective-permute-start.21 = (bf16[1,2,1,1,48,2,512]{6,4,5,3,2,1,0:T(8,128)(2,1)S(1)}, bf16[1,2,1,1,48,2,512]{6,4,5,3,2,1,0:T(8,128)(2,1)S(1)}, u32[]{:S(2)}, u32[]{:S(2)}) collective-permute-start(bf16[1,2,1,1,48,2,512]{6,4,5,3,2,1,0:T(8,128)(2,1)S(1)} %constant_dynamic-slice_fusion.25), channel_id=1, source_target_pairs={{0,4},{2,6},{4,0},{6,2},{8,12},{10,14},{12,8},{14,10},{16,20},{18,... | collective-permute-start | bytes 589832 | tf_op jit(solution)/shard_map/ppermute | solution.py:81
  684.1 4.0 collective-permute-start.7
  688.1 7.5 collective-permute-start.8
  695.6 28.6 %collective-permute-start.10 = (bf16[1,2,2,1,16,2,1152]{6,4,3,2,1,0,5:T(8,128)(2,1)S(1)}, bf16[1,2,2,1,16,2,1152]{6,4,3,2,1,0,5:T(8,128)(2,1)S(1)}, u32[]{:S(2)}, u32[]{:S(2)}) collective-permute-start(bf16[1,2,2,1,16,2,1152]{6,4,3,2,1,0,5:T(8,128)(2,1)S(1)} %constant_dynamic-slice_fusion.39), channel_id=1, source_target_pairs={{0,16},{2,18},{4,20},{6,22},{8,24},{10,26},{12,28},{14,30},{16,0},... | collective-permute-start | bytes 884744 | tf_op jit(solution)/shard_map/ppermute | solution.py:81
  698.1 46.3 %copy-start.12 = (bf16[2,2,2,1,144,2,384]{6,4,5,3,2,1,0:T(8,128)(2,1)}, bf16[2,2,2,1,144,2,384]{6,4,5,3,2,1,0:T(8,128)(2,1)S(1)}, u32[]{:S(2)}) copy-start(bf16[2,2,2,1,144,2,384]{6,4,5,3,2,1,0:T(8,128)(2,1)S(1)} %copy_add_fusion.1) | copy-start | bytes 5308420
  699.3 52.9 %collective-permute-start.25 = (bf16[1,2,2,1,144,2,384]{6,4,5,3,2,1,0:T(8,128)(2,1)}, bf16[1,2,2,1,144,2,384]{6,4,5,3,2,1,0:T(8,128)(2,1)}, u32[]{:S(2)}, u32[]{:S(2)}) collective-permute-start(bf16[1,2,2,1,144,2,384]{6,4,5,3,2,1,0:T(8,128)(2,1)} %constant_dynamic-slice_fusion.20), channel_id=1, source_target_pairs={{0,16},{2,18},{4,20},{6,22},{8,24},{10,26},{12,28},{14,30},{16,0},... | collective-permute-start | bytes 2654216 | tf_op jit(solution)/shard_map/ppermute | solution.py:81
  702.3 23.6 %collective-permute-start.22 = (bf16[1,1,1,1,48,2,512]{6,4,5,3,2,1,0:T(8,128)(2,1)S(1)}, bf16[1,1,1,1,48,2,512]{6,4,5,3,2,1,0:T(8,128)(2,1)S(1)}, u32[]{:S(2)}, u32[]{:S(2)}) collective-permute-start(bf16[1,1,1,1,48,2,512]{6,4,5,3,2,1,0:T(8,128)(2,1)S(1)} %constant_dynamic-slice_fusion.24), channel_id=1, source_target_pairs={{0,8},{2,10},{4,12},{6,14},{8,0},{10,2},{12,4},{14,6},{16,24},{18,... | collective-permute-start | bytes 294920 | tf_op jit(solution)/shard_map/ppermute | solution.py:81
  724.3 5.2 collective-permute-start.11
  729.6 14.8 %collective-permute-start.12 = (bf16[1,1,1,1,16,2,1152]{6,4,3,2,1,0,5:T(8,128)(2,1)S(1)}, bf16[1,1,1,1,16,2,1152]{6,4,3,2,1,0,5:T(8,128)(2,1)S(1)}, u32[]{:S(2)}, u32[]{:S(2)}) collective-permute-start(bf16[1,1,1,1,16,2,1152]{6,4,3,2,1,0,5:T(8,128)(2,1)S(1)} %constant_dynamic-slice_fusion.37), channel_id=1, source_target_pairs={{0,8},{2,10},{4,12},{6,14},{8,0},{10,2},{12,4},{14,6},{16,24},{18,... | collective-permute-start | bytes 221192 | tf_op jit(solution)/shard_map/ppermute | solution.py:81
  730.5 14.5 %collective-permute-start.23 = (bf16[1,1,1,1,48,1,512]{6,4,5,3,2,1,0:T(8,128)(2,1)S(1)}, bf16[1,1,1,1,48,1,512]{6,4,5,3,2,1,0:T(8,128)(2,1)S(1)}, u32[]{:S(2)}, u32[]{:S(2)}) collective-permute-start(bf16[1,1,1,1,48,1,512]{6,4,5,3,2,1,0:T(8,128)(2,1)S(1)} %constant_dynamic-slice_fusion.23), channel_id=1, source_target_pairs={{0,1},{1,0},{2,3},{3,2},{4,5},{5,4},{6,7},{7,6},{8,9},{9,8},{10,11... | collective-permute-start | bytes 147464 | tf_op jit(solution)/shard_map/ppermute | solution.py:88
  744.4 4.0 collective-permute-start.13
  753.8 11.0 %collective-permute-start.26 = (bf16[1,2,1,1,144,2,384]{6,4,5,3,2,1,0:T(8,128)(2,1)S(1)}, bf16[1,2,1,1,144,2,384]{6,4,5,3,2,1,0:T(8,128)(2,1)S(1)}, u32[]{:S(2)}, u32[]{:S(2)}) collective-permute-start(bf16[1,2,1,1,144,2,384]{6,4,5,3,2,1,0:T(8,128)(2,1)S(1)} %constant_dynamic-slice_fusion.19), channel_id=1, source_target_pairs={{0,4},{2,6},{4,0},{6,2},{8,12},{10,14},{12,8},{14,10},{16,20},{18,... | collective-permute-start | bytes 1327112 | tf_op jit(solution)/shard_map/ppermute | solution.py:81
  761.0 54.1 %collective-permute-start.40 = (bf16[2,1,2,1,48,2,1536]{6,5,4,3,2,1,0:T(2,128)(2,1)S(1)}, bf16[2,1,2,1,48,2,1536]{6,5,4,3,2,1,0:T(2,128)(2,1)S(1)}, u32[]{:S(2)}, u32[]{:S(2)}) collective-permute-start(bf16[2,1,2,1,48,2,1536]{6,5,4,3,2,1,0:T(2,128)(2,1)S(1)} %constant_dynamic-slice_fusion.3), channel_id=1, source_target_pairs={{0,8},{2,10},{4,12},{6,14},{8,0},{10,2},{12,4},{14,6},{16,24},{18,... | collective-permute-start | bytes 3538952 | tf_op jit(solution)/shard_map/ppermute | solution.py:81
  764.9 49.6 %collective-permute-start.27 = (bf16[1,1,1,1,144,2,384]{6,4,5,3,2,1,0:T(8,128)(2,1)S(1)}, bf16[1,1,1,1,144,2,384]{6,4,5,3,2,1,0:T(8,128)(2,1)S(1)}, u32[]{:S(2)}, u32[]{:S(2)}) collective-permute-start(bf16[1,1,1,1,144,2,384]{6,4,5,3,2,1,0:T(8,128)(2,1)S(1)} %constant_dynamic-slice_fusion.18), channel_id=1, source_target_pairs={{0,8},{2,10},{4,12},{6,14},{8,0},{10,2},{12,4},{14,6},{16,24},{18,... | collective-permute-start | bytes 663560 | tf_op jit(solution)/shard_map/ppermute | solution.py:81
  767.2 53.9 %collective-permute-start.35 = (bf16[1,2,2,1,192,2,384]{6,4,5,3,2,1,0:T(8,128)(2,1)S(1)}, bf16[1,2,2,1,192,2,384]{6,4,5,3,2,1,0:T(8,128)(2,1)S(1)}, u32[]{:S(2)}, u32[]{:S(2)}) collective-permute-start(bf16[1,2,2,1,192,2,384]{6,4,5,3,2,1,0:T(8,128)(2,1)S(1)} %constant_dynamic-slice_fusion.8), channel_id=1, source_target_pairs={{0,16},{2,18},{4,20},{6,22},{8,24},{10,26},{12,28},{14,30},{16,0},... | collective-permute-start | bytes 3538952 | tf_op jit(solution)/shard_map/ppermute | solution.py:81
  814.5 5.9 collective-permute-start.28
  817.7 13.9 %collective-permute-start.41 = (bf16[2,1,2,1,48,1,1536]{6,4,5,3,2,1,0:T(8,128)(2,1)S(1)}, bf16[2,1,2,1,48,1,1536]{6,4,5,3,2,1,0:T(8,128)(2,1)S(1)}, u32[]{:S(2)}, u32[]{:S(2)}) collective-permute-start(bf16[2,1,2,1,48,1,1536]{6,4,5,3,2,1,0:T(8,128)(2,1)S(1)} %copy.297), channel_id=1, source_target_pairs={{0,1},{1,0},{2,3},{3,2},{4,5},{5,4},{6,7},{7,6},{8,9},{9,8},{10,11... | collective-permute-start | bytes 1769480 | tf_op jit(solution)/shard_map/ppermute | solution.py:88
  821.3 13.2 %collective-permute-start.36 = (bf16[1,2,1,1,192,2,384]{6,4,5,3,2,1,0:T(8,128)(2,1)S(1)}, bf16[1,2,1,1,192,2,384]{6,4,5,3,2,1,0:T(8,128)(2,1)S(1)}, u32[]{:S(2)}, u32[]{:S(2)}) collective-permute-start(bf16[1,2,1,1,192,2,384]{6,4,5,3,2,1,0:T(8,128)(2,1)S(1)} %constant_dynamic-slice_fusion.7), channel_id=1, source_target_pairs={{0,4},{2,6},{4,0},{6,2},{8,12},{10,14},{12,8},{14,10},{16,20},{18,... | collective-permute-start | bytes 1769480 | tf_op jit(solution)/shard_map/ppermute | solution.py:81
  834.0 13.7 %collective-permute-start.42 = (bf16[1,1,2,1,48,1,1536]{6,4,5,3,2,1,0:T(8,128)(2,1)S(1)}, bf16[1,1,2,1,48,1,1536]{6,4,5,3,2,1,0:T(8,128)(2,1)S(1)}, u32[]{:S(2)}, u32[]{:S(2)}) collective-permute-start(bf16[1,1,2,1,48,1,1536]{6,4,5,3,2,1,0:T(8,128)(2,1)S(1)} %copy.299), channel_id=1, source_target_pairs={{0,16},{2,18},{4,20},{6,22},{8,24},{10,26},{12,28},{14,30},{16,0},... | collective-permute-start | bytes 884744 | tf_op jit(solution)/shard_map/ppermute | solution.py:81
  834.7 14.3 %collective-permute-start.37 = (bf16[1,1,1,1,192,2,384]{6,4,5,3,2,1,0:T(8,128)(2,1)S(1)}, bf16[1,1,1,1,192,2,384]{6,4,5,3,2,1,0:T(8,128)(2,1)S(1)}, u32[]{:S(2)}, u32[]{:S(2)}) collective-permute-start(bf16[1,1,1,1,192,2,384]{6,4,5,3,2,1,0:T(8,128)(2,1)S(1)} %constant_dynamic-slice_fusion.6), channel_id=1, source_target_pairs={{0,8},{2,10},{4,12},{6,14},{8,0},{10,2},{12,4},{14,6},{16,24},{18,... | collective-permute-start | bytes 884744 | tf_op jit(solution)/shard_map/ppermute | solution.py:81
  848.9 8.8 %collective-permute-start.43 = (bf16[1,1,1,1,48,1,1536]{6,5,4,3,2,1,0:T(2,128)(2,1)S(1)}, bf16[1,1,1,1,48,1,1536]{6,5,4,3,2,1,0:T(2,128)(2,1)S(1)}, u32[]{:S(2)}, u32[]{:S(2)}) collective-permute-start(bf16[1,1,1,1,48,1,1536]{6,5,4,3,2,1,0:T(2,128)(2,1)S(1)} %constant_dynamic-slice_fusion), channel_id=1, source_target_pairs={{0,4},{2,6},{4,0},{6,2},{8,12},{10,14},{12,8},{14,10},{16,20},{18,... | collective-permute-start | bytes 442376 | tf_op jit(solution)/shard_map/ppermute | solution.py:81
  849.0 9.9 %collective-permute-start.38 = (bf16[1,1,1,1,192,1,384]{6,4,5,3,2,1,0:T(8,128)(2,1)S(1)}, bf16[1,1,1,1,192,1,384]{6,4,5,3,2,1,0:T(8,128)(2,1)S(1)}, u32[]{:S(2)}, u32[]{:S(2)}) collective-permute-start(bf16[1,1,1,1,192,1,384]{6,4,5,3,2,1,0:T(8,128)(2,1)S(1)} %constant_dynamic-slice_fusion.5), channel_id=1, source_target_pairs={{0,1},{1,0},{2,3},{3,2},{4,5},{5,4},{6,7},{7,6},{8,9},{9,8},{10,11... | collective-permute-start | bytes 442376 | tf_op jit(solution)/shard_map/ppermute | solution.py:88
  (105 other events, 481.0 us)

commit v2 on v1

v2 whole, which is shorter than its diff:
```python
import functools
import jax
import jax.numpy as jnp
from jax import lax
from jax.experimental import pallas as pl
from jax.experimental.pallas import tpu as pltpu
from jax.sharding import PartitionSpec as P

HD = 64
F32 = jnp.float32
BF16 = jnp.bfloat16
eps_batch = 1e-05
eps_layer = 1e-06
masked_value = -1e30
GELU_C = 0.7978845608028654
GELU_A = 0.044715


def nn(a, b):
    return lax.dot_general(a, b, (((1,), (0,)), ((), ())), preferred_element_type=F32)


def nt(a, b):
    return lax.dot_general(a, b, (((1,), (1,)), ((), ())), preferred_element_type=F32)


def tn(a, b):
    return lax.dot_general(a, b, (((0,), (0,)), ((), ())), preferred_element_type=F32)


def gelu_of(x):
    t = jnp.tanh(GELU_C * (x + GELU_A * x * x * x))
    return 0.5 * x * (1.0 + t)


def gelu_and_slope(x):
    x2 = x * x
    t = jnp.tanh(x * (GELU_C + (GELU_C * GELU_A) * x2))
    half = 0.5 + 0.5 * t
    slope = half + (0.5 * x) * (1.0 - t * t) * (GELU_C + (3.0 * GELU_C * GELU_A) * x2)
    return x * half, slope


def ln_parts(x):
    mean = jnp.mean(x, axis=-1, keepdims=True)
    c = x - mean
    var = jnp.mean(c * c, axis=-1, keepdims=True)
    r = lax.rsqrt(var + eps_layer)
    return c * r, r


def ln_back(dz, nrm, r, gain):
    u = dz * gain
    return r * (u - jnp.mean(u, axis=-1, keepdims=True) - nrm * jnp.mean(u * nrm, axis=-1, keepdims=True))


def mlp_kernel(ex, seq, pad, z2_ref, h1_ref, cot_ref, upw_ref, upb_ref, dnw_ref, dnb_ref, g_ref, s_ref,
               out_ref, dnwg_ref, upwg_ref, upbg_ref, g1_ref, vec_ref,
               g2_s, g2t_s, acc_o, acc_d):
    i = pl.program_id(0)
    last = pl.num_programs(0) - 1

    @pl.when(i == 0)
    def _():
        g2_s[...] = jnp.zeros_like(g2_s)
        for e in range(ex):
            g2_s[e * pad : e * pad + seq, :] = cot_ref[e]
        g2t_s[...] = g2_s[...].T
        acc_o[...] = jnp.zeros_like(acc_o)
        acc_d[...] = jnp.zeros_like(acc_d)

    z2 = z2_ref[...]
    g2 = g2_s[...]
    pre = nn(z2, upw_ref[...]) + upb_ref[...]
    act, slope = gelu_and_slope(pre)
    low = act.astype(BF16)
    dg32 = nt(g2, dnw_ref[...]) * slope
    dg = dg32.astype(BF16)
    acc_o[...] += nn(low, dnw_ref[...])
    dnwg_ref[...] = nn(g2t_s[...], low).astype(BF16)
    upwg_ref[...] = tn(dg, z2).astype(BF16)
    acc_d[...] += nt(dg, upw_ref[...])
    upbg_ref[...] = jnp.sum(dg.astype(F32), axis=0, keepdims=True)

    @pl.when(i == last)
    def _():
        h1 = h1_ref[...]
        out = (h1 + acc_o[...] + dnb_ref[...]).astype(BF16)
        for e in range(ex):
            out_ref[e] = out[e * pad : e * pad + seq, :]
        nrm, r = ln_parts(h1)
        dz = acc_d[...]
        gf = g2_s[...].astype(F32)
        g1 = gf + ln_back(dz, nrm, r, g_ref[...])
        g1_ref[...] = g1
        vec_ref[0:1, :] = jnp.sum(gf, axis=0, keepdims=True)
        vec_ref[1:2, :] = jnp.sum(dz * nrm, axis=0, keepdims=True)
        vec_ref[2:3, :] = jnp.sum(dz, axis=0, keepdims=True)
        vec_ref[3:4, :] = jnp.sum(g1, axis=0, keepdims=True)


def whole(shape):
    return pl.BlockSpec(shape, lambda *_: (0,) * len(shape))


def mlp(z2, h1, cot, up_w, up_b, down_w, down_b, gain, shift, pad, tile=256):
    ex, seq, width = cot.shape
    rows = z2.shape[0]
    ff = up_w.shape[1]
    steps = ff // tile
    return pl.pallas_call(
        functools.partial(mlp_kernel, ex, seq, pad),
        grid=(steps,),
        in_specs=[
            whole((rows, width)), whole((rows, width)), whole((ex, seq, width)),
            pl.BlockSpec((width, tile), lambda i: (0, i)),
            pl.BlockSpec((1, tile), lambda i: (0, i)),
            pl.BlockSpec((tile, width), lambda i: (i, 0)),
            whole((1, width)), whole((1, width)), whole((1, width)),
        ],
        out_specs=[
            whole((ex, seq, width)),
            pl.BlockSpec((width, tile), lambda i: (0, i)),
            pl.BlockSpec((tile, width), lambda i: (i, 0)),
            pl.BlockSpec((1, tile), lambda i: (0, i)),
            whole((rows, width)),
            whole((8, width)),
        ],
        out_shape=[
            jax.ShapeDtypeStruct((ex, seq, width), BF16),
            jax.ShapeDtypeStruct((width, ff), BF16),
            jax.ShapeDtypeStruct((ff, width), BF16),
            jax.ShapeDtypeStruct((1, ff), F32),
            jax.ShapeDtypeStruct((rows, width), F32),
            jax.ShapeDtypeStruct((8, width), F32),
        ],
        scratch_shapes=[
            pltpu.VMEM((rows, width), BF16),
            pltpu.VMEM((width, rows), BF16),
            pltpu.VMEM((rows, width), F32),
            pltpu.VMEM((rows, width), F32),
        ],
        compiler_params=pltpu.CompilerParams(dimension_semantics=("arbitrary",), vmem_limit_bytes=56 << 20),
        cost_estimate=pl.CostEstimate(flops=12 * rows * width * ff, bytes_accessed=40 << 20, transcendentals=rows * ff),
        name="mlp_both_ways",
    )(z2, h1, cot, up_w, up_b.reshape(1, -1), down_w, down_b.reshape(1, -1), gain.reshape(1, -1), shift.reshape(1, -1))


def head_mask(rows, second):
    lane = lax.broadcasted_iota(jnp.int32, (rows, 2 * HD), 1)
    return (lane >= HD) if second else (lane < HD)


def attn_fwd_kernel(ex, n_image, pad, pre_ref, len_ref, h0_ref, g_ref, s_ref, wq_ref, wk_ref, wv_ref, qb_ref, vb_ref,
                    ow_ref, ob_ref, g2_ref, s2_ref,
                    z1_ref, q_ref, k_ref, v_ref, p_ref, attn_ref, h1_ref, z2_ref, acc):
    i = pl.program_id(0)
    last = pl.num_programs(0) - 1
    wide = wq_ref.shape[1]

    @pl.when(i == 0)
    def _():
        nrm, _r = ln_parts(h0_ref[...].astype(F32))
        z1_ref[...] = (nrm * g_ref[...] + s_ref[...]).astype(BF16)
        acc[...] = jnp.zeros_like(acc)

    z1 = z1_ref[...]
    q_ref[...] = (nn(z1, wq_ref[...]) + qb_ref[...]).astype(BF16)
    k_ref[...] = nn(z1, wk_ref[...]).astype(BF16)
    v_ref[...] = (nn(z1, wv_ref[...]) + vb_ref[...]).astype(BF16)
    zero = jnp.zeros((pad, 2 * HD), BF16)
    first = head_mask(pad, False)

    def example(e, carry):
        row0 = pl.multiple_of(e * pad, 16)
        key = lax.broadcasted_iota(jnp.int32, (pad, pad), 1)
        qry = lax.broadcasted_iota(jnp.int32, (pad, pad), 0)
        limit = jnp.maximum(qry + 1, n_image + pre_ref[e])
        limit = jnp.minimum(limit, n_image + len_ref[e])
        vis = key < limit
        for pair in range(wide // (2 * HD)):
            cols = slice(pair * 2 * HD, (pair + 1) * 2 * HD)
            q2 = q_ref[pl.ds(row0, pad), cols] * jnp.asarray(0.125, BF16)
            k2 = k_ref[pl.ds(row0, pad), cols]
            v2 = v_ref[pl.ds(row0, pad), cols]
            out = None
            for h in range(2):
                sel = first if h == 0 else jnp.logical_not(first)
                sc = nt(jnp.where(sel, q2, zero), k2)
                sc = jnp.where(vis, sc, masked_value)
                top = jnp.max(sc, axis=-1, keepdims=True)
                ex_ = jnp.exp(sc - top)
                tot = jnp.sum(ex_, axis=-1, keepdims=True)
                p = (ex_ * (1.0 / tot)).astype(BF16)
                p_ref[e, pair * 2 + h] = p
                o = nn(p, jnp.where(sel, v2, zero))
                out = o if out is None else out + o
            attn_ref[pl.ds(row0, pad), cols] = out.astype(BF16)
        return carry

    lax.fori_loop(0, ex, example, 0)
    acc[...] += nn(attn_ref[...], ow_ref[...])

    @pl.when(i == last)
    def _():
        h1 = h0_ref[...].astype(F32) + acc[...] + ob_ref[...]
        h1_ref[...] = h1
        nrm, _r = ln_parts(h1)
        z2_ref[...] = (nrm * g2_ref[...] + s2_ref[...]).astype(BF16)


def attn_fwd(h0, prefix, text_len, ln1_gain, ln1_shift, qkv_w, qb, vb, out_w, out_b, ln2_gain, ln2_shift, ex, n_image, pad, wide=256):
    rows, width = h0.shape
    groups = width // wide
    heads = width // HD
    hg = wide // HD
    cols = lambda off: pl.BlockSpec((width, wide), lambda i, *_: (0, i + off * groups))
    vec = whole((1, width))
    part = pl.BlockSpec((rows, wide), lambda i, *_: (0, i))
    bias = pl.BlockSpec((1, wide), lambda i, *_: (0, i))
    row = lambda v: v.reshape(1, -1)
    return pl.pallas_call(
        functools.partial(attn_fwd_kernel, ex, n_image, pad),
        grid_spec=pltpu.PrefetchScalarGridSpec(
            num_scalar_prefetch=2,
            grid=(groups,),
            in_specs=[whole((rows, width)), vec, vec, cols(0), cols(1), cols(2), bias, bias,
                      pl.BlockSpec((wide, width), lambda i, *_: (i, 0)), vec, vec, vec],
            out_specs=[whole((rows, width)), part, part, part,
                       pl.BlockSpec((ex, hg, pad, pad), lambda i, *_: (0, i, 0, 0)),
                       part, whole((rows, width)), whole((rows, width))],
            scratch_shapes=[pltpu.VMEM((rows, width), F32)],
        ),
        out_shape=[jax.ShapeDtypeStruct((rows, width), BF16)] * 4 + [
            jax.ShapeDtypeStruct((ex, heads, pad, pad), BF16),
            jax.ShapeDtypeStruct((rows, width), BF16),
            jax.ShapeDtypeStruct((rows, width), F32),
            jax.ShapeDtypeStruct((rows, width), BF16)],
        compiler_params=pltpu.CompilerParams(dimension_semantics=("arbitrary",), vmem_limit_bytes=56 << 20),
        cost_estimate=pl.CostEstimate(flops=8 * rows * width * width + 4 * heads * rows * pad * 128, bytes_accessed=30 << 20, transcendentals=heads * rows * pad),
        name="attention_forward",
    )(prefix, text_len, h0, row(ln1_gain), row(ln1_shift), qkv_w, qkv_w, qkv_w, row(qb), row(vb), out_w, row(out_b), row(ln2_gain), row(ln2_shift))


def attn_bwd_kernel(ex, n_image, txt, cols_real, pad, g1_ref, ow_ref, attn_ref, q_ref, k_ref, v_ref, p_ref, z1_ref, h0_ref, wq_ref, wk_ref, wv_ref, g_ref,
                    owg_ref, qkvg_ref, bias_ref, text_ref, dtok_ref, vec_ref,
                    g1b_s, g1t_s, dat_s, dq_s, dk_s, dv_s, acc):
    i = pl.program_id(0)
    last = pl.num_programs(0) - 1
    wide = wq_ref.shape[1]

    @pl.when(i == 0)
    def _():
        g1b_s[...] = g1_ref[...].astype(BF16)
        g1t_s[...] = g1b_s[...].T
        acc[...] = jnp.zeros_like(acc)

    owg_ref[...] = nn(g1t_s[...], attn_ref[...]).astype(BF16)
    dat_s[...] = nt(g1b_s[...], ow_ref[...]).astype(BF16)
    zero = jnp.zeros((pad, 2 * HD), BF16)
    first = head_mask(pad, False)

    def example(e, carry):
        row0 = pl.multiple_of(e * pad, 16)
        for pair in range(wide // (2 * HD)):
            cols = slice(pair * 2 * HD, (pair + 1) * 2 * HD)
            q2 = q_ref[pl.ds(row0, pad), cols]
            k2 = k_ref[pl.ds(row0, pad), cols]
            v2 = v_ref[pl.ds(row0, pad), cols]
            da2 = dat_s[pl.ds(row0, pad), cols]
            dq = dk = dv = None
            for h in range(2):
                sel = first if h == 0 else jnp.logical_not(first)
                pb = p_ref[e, pair * 2 + h]
                p = pb.astype(F32)
                dah = jnp.where(sel, da2, zero)
                dp = nt(dah, v2)
                inner = jnp.sum(p * dp, axis=-1, keepdims=True)
                ds = (p * (dp - inner)).astype(BF16)
                dvh = tn(pb, dah)
                dqh = nn(ds, jnp.where(sel, k2, zero))
                dkh = tn(ds, jnp.where(sel, q2, zero))
                dq = dqh if dq is None else dq + dqh
                dk = dkh if dk is None else dk + dkh
                dv = dvh if dv is None else dv + dvh
            dq_s[pl.ds(row0, pad), cols] = (dq * 0.125).astype(BF16)
            dk_s[pl.ds(row0, pad), cols] = (dk * 0.125).astype(BF16)
            dv_s[pl.ds(row0, pad), cols] = dv.astype(BF16)
        return carry

    lax.fori_loop(0, ex, example, 0)
    z1 = z1_ref[...]
    dq, dk, dv = dq_s[...], dk_s[...], dv_s[...]
    qkvg_ref[0] = tn(dq, z1).astype(BF16)
    qkvg_ref[1] = tn(dk, z1).astype(BF16)
    qkvg_ref[2] = tn(dv, z1).astype(BF16)
    acc[...] += nt(dq, wq_ref[...]) + nt(dk, wk_ref[...]) + nt(dv, wv_ref[...])
    bias_ref[0:1, :] = jnp.sum(dq.astype(F32), axis=0, keepdims=True)
    bias_ref[1:2, :] = jnp.sum(dv.astype(F32), axis=0, keepdims=True)

    @pl.when(i == last)
    def _():
        nrm, r = ln_parts(h0_ref[...].astype(F32))
        dz = acc[...]
        g0 = g1_ref[...] + ln_back(dz, nrm, r, g_ref[...])
        vec_ref[0:1, :] = jnp.sum(dz * nrm, axis=0, keepdims=True)
        vec_ref[1:2, :] = jnp.sum(dz, axis=0, keepdims=True)
        gb = g0.astype(BF16)
        px = dtok_ref.shape[0] // ex
        pick_image = image_pick(px, pad, n_image, cols_real)
        tr = lax.broadcasted_iota(jnp.int32, (txt, pad), 0)
        tc = lax.broadcasted_iota(jnp.int32, (txt, pad), 1)
        pick_text = jnp.where(tc == tr + n_image, 1.0, 0.0).astype(BF16)
        tot = jnp.zeros((1, gb.shape[1]), F32)
        for e in range(ex):
            ge = gb[e * pad : (e + 1) * pad, :]
            text_ref[e] = nn(pick_text, ge).astype(BF16)
            dt = nn(pick_image, ge)
            dtok_ref[e * px : (e + 1) * px, :] = dt.astype(BF16)
            tot = tot + jnp.sum(dt, axis=0, keepdims=True)
        vec_ref[2:3, :] = tot


def image_pick(px, pad, n_image, cols_real):
    p = lax.broadcasted_iota(jnp.int32, (px, pad), 0)
    t = lax.broadcasted_iota(jnp.int32, (px, pad), 1)
    col = p & 15
    tok = (p >> 4) * cols_real + col
    return jnp.where((col < cols_real) & (tok == t) & (t < n_image), 1.0, 0.0).astype(BF16)


def attn_bwd(g1, out_w, attn, q, k, v, p, z1, h0, qkv_w, ln1_gain, ex, n_image, txt, img_rows, img_cols, pad, wide=256):
    rows, width = h0.shape
    groups = width // wide
    heads = width // HD
    hg = wide // HD
    px = img_rows * 16
    cols = lambda off: pl.BlockSpec((width, wide), lambda i: (0, i + off * groups))
    part = pl.BlockSpec((rows, wide), lambda i: (0, i))
    return pl.pallas_call(
        functools.partial(attn_bwd_kernel, ex, n_image, txt, img_cols, pad),
        grid=(groups,),
        in_specs=[whole((rows, width)), pl.BlockSpec((wide, width), lambda i: (i, 0)), part, part, part, part,
                  pl.BlockSpec((ex, hg, pad, pad), lambda i: (0, i, 0, 0)),
                  whole((rows, width)), whole((rows, width)), cols(0), cols(1), cols(2), whole((1, width))],
        out_specs=[pl.BlockSpec((width, wide), lambda i: (0, i)),
                   pl.BlockSpec((3, wide, width), lambda i: (0, i, 0)),
                   pl.BlockSpec((8, wide), lambda i: (0, i)),
                   whole((ex, txt, width)), whole((ex * px, width)), whole((8, width))],
        out_shape=[jax.ShapeDtypeStruct((width, width), BF16),
                   jax.ShapeDtypeStruct((3, width, width), BF16),
                   jax.ShapeDtypeStruct((8, width), F32),
                   jax.ShapeDtypeStruct((ex, txt, width), BF16),
                   jax.ShapeDtypeStruct((ex * px, width), BF16),
                   jax.ShapeDtypeStruct((8, width), F32)],
        scratch_shapes=[pltpu.VMEM((rows, width), BF16), pltpu.VMEM((width, rows), BF16)]
        + [pltpu.VMEM((rows, wide), BF16)] * 4 + [pltpu.VMEM((rows, width), F32)],
        compiler_params=pltpu.CompilerParams(dimension_semantics=("arbitrary",), vmem_limit_bytes=56 << 20),
        cost_estimate=pl.CostEstimate(flops=16 * rows * width * width + 10 * heads * rows * pad * 128, bytes_accessed=40 << 20, transcendentals=0),
        name="attention_backward",
    )(g1, out_w, attn, q, k, v, p, z1, h0, qkv_w, qkv_w, qkv_w, ln1_gain.reshape(1, -1))


def stat_rows(channels):
    return max(8, 2 * channels // 128)


def put_stats(ref, first, second):
    lanes = jnp.concatenate([first, second], axis=1)
    n = ref.shape[0]
    for r in range(lanes.shape[1] // 128):
        ref[:, r, :] = jnp.broadcast_to(lanes[:, r * 128 : (r + 1) * 128], (n, 128))


def get_stats(ref, channels):
    total = jnp.sum(ref[...], axis=0)
    rows = 2 * channels // 128
    half = rows // 2
    first = jnp.concatenate([total[r : r + 1, :] for r in range(half)], axis=1)
    second = jnp.concatenate([total[r : r + 1, :] for r in range(half, rows)], axis=1)
    return first, second


def mean_rstd(ref, channels, count):
    s1, s2 = get_stats(ref, channels)
    mean = s1 * (1.0 / count)
    return mean, lax.rsqrt(s2 * (1.0 / count) - mean * mean + eps_batch)


def real_columns(rows, cols):
    return (lax.broadcasted_iota(jnp.int32, (rows, 1), 0) & 15) < cols


def col_sum(x):
    return jnp.sum(x, axis=0, keepdims=True)


def stats_kernel(cols, x_ref, w_ref, parts_ref, xp):
    xp[...] = jnp.zeros_like(xp)
    shape = x_ref.shape
    xp[:, 0:cols, :] = x_ref[...].reshape(shape[0] * shape[1], cols, shape[3])
    a = nn(xp[...].reshape(shape[0] * shape[1] * 16, shape[3]), w_ref[...])
    put_stats(parts_ref, col_sum(a), col_sum(a * a))


def conv_fwd_kernel(count, ex, rows, cols, sp_ref, parts_ref, own_ref, got_ref, win_ref, g_ref, s_ref, wmid_ref,
                    xs_ref, act1_ref, wide_ref, act2_ref, parts2_ref):
    s = sp_ref[0]
    half = rows // 2
    px = rows * 16
    chan = xs_ref.shape[-1]
    xs_ref[...] = jnp.zeros_like(xs_ref)
    for e in range(ex):
        xs_ref[e, pl.ds(s * half, half), 0:cols, :] = own_ref[s * ex + e]
        xs_ref[e, pl.ds((1 - s) * half, half), 0:cols, :] = got_ref[e]
    a1 = nn(xs_ref[...].reshape(ex * px, chan), win_ref[...])
    act1_ref[...] = a1
    mid = a1.shape[1]
    mean, rstd = mean_rstd(parts_ref, mid, count)
    real = real_columns(ex * px, cols)
    act = gelu_of((a1 - mean) * rstd * g_ref[...] + s_ref[...])
    act = jnp.where(real, act, 0.0)
    for e in range(ex):
        part = act[e * px : (e + 1) * px]
        wide_ref[e, 0:16, :] = jnp.zeros((16, 3 * mid), BF16)
        wide_ref[e, px + 16 : px + 32, :] = jnp.zeros((16, 3 * mid), BF16)
        wide_ref[e, 16 : px + 16, 0:mid] = pltpu.roll(part, 1, 0).astype(BF16)
        wide_ref[e, 16 : px + 16, mid : 2 * mid] = part.astype(BF16)
        wide_ref[e, 16 : px + 16, 2 * mid : 3 * mid] = pltpu.roll(part, px - 1, 0).astype(BF16)
    one = real_columns(px, cols)
    t1 = jnp.zeros((1, mid), F32)
    t2 = jnp.zeros((1, mid), F32)
    for e in range(ex):
        a2 = nn(wide_ref[e, 0:px, :], wmid_ref[0])
        a2 = a2 + nn(wide_ref[e, 16 : px + 16, :], wmid_ref[1])
        a2 = a2 + nn(wide_ref[e, 32 : px + 32, :], wmid_ref[2])
        a2 = jnp.where(one, a2, 0.0)
        act2_ref[e * px : (e + 1) * px, :] = a2
        t1 = t1 + col_sum(a2)
        t2 = t2 + col_sum(a2 * a2)
    put_stats(parts2_ref, t1, t2)


def expand_kernel(count, cols, parts_ref, act2_ref, g_ref, s_ref, w_ref, relu2_ref, act3_ref, parts3_ref):
    a2 = act2_ref[...]
    mean, rstd = mean_rstd(parts_ref, a2.shape[1], count)
    act = gelu_of((a2 - mean) * rstd * g_ref[...] + s_ref[...])
    low = jnp.where(real_columns(a2.shape[0], cols), act, 0.0).astype(BF16)
    relu2_ref[...] = low
    a3 = nn(low, w_ref[...])
    act3_ref[...] = a3
    put_stats(parts3_ref, col_sum(a3), col_sum(a3 * a3))


def tokens_kernel(count, ex, cols, n_image, pad, parts_ref, act3_ref, xs_ref, g_ref, s_ref, w_ref, b_ref, text_ref,
                  stem_ref, h0_ref):
    a3 = act3_ref[...]
    mean, rstd = mean_rstd(parts_ref, a3.shape[1], count)
    pre = (a3 - mean) * rstd * g_ref[...] + s_ref[...] + xs_ref[...].reshape(a3.shape).astype(F32)
    stem = gelu_of(pre).astype(BF16)
    stem_ref[...] = stem
    tok = (nn(stem, w_ref[...]) + b_ref[...]).astype(BF16)
    px = a3.shape[0] // ex
    txt = text_ref.shape[1]
    t = lax.broadcasted_iota(jnp.int32, (pad, px), 0)
    p = lax.broadcasted_iota(jnp.int32, (pad, px), 1)
    col = p & 15
    pick = jnp.where((col < cols) & ((p >> 4) * cols + col == t), 1.0, 0.0).astype(BF16)
    tr = lax.broadcasted_iota(jnp.int32, (pad, txt), 0)
    tc = lax.broadcasted_iota(jnp.int32, (pad, txt), 1)
    pick_text = jnp.where(tr == tc + n_image, 1.0, 0.0).astype(BF16)
    for e in range(ex):
        both = nn(pick, tok[e * px : (e + 1) * px, :]) + nn(pick_text, text_ref[e])
        h0_ref[e * pad : (e + 1) * pad, :] = both.astype(BF16)


def dpre_kernel(count, ex, rows, sp_ref, parts_ref, act3_ref, xs_ref, g_ref, s_ref, dtok_ref, w_ref, dpre_ref, send_ref, parts4_ref):
    a3 = act3_ref[...]
    mean, rstd = mean_rstd(parts_ref, a3.shape[1], count)
    nrm = (a3 - mean) * rstd
    pre = nrm * g_ref[...] + s_ref[...] + xs_ref[...].reshape(a3.shape).astype(F32)
    _, slope = gelu_and_slope(pre)
    d = nt(dtok_ref[...], w_ref[...]) * slope
    dpre_ref[...] = d.reshape(dpre_ref.shape)
    put_stats(parts4_ref, col_sum(d), col_sum(d * nrm))
    half = rows // 2
    other = 1 - sp_ref[0]
    for e in range(ex):
        send_ref[e] = dpre_ref[e, pl.ds(other * half, half)].astype(BF16)


def back3_kernel(count, cols, parts4_ref, parts3_ref, parts2_ref, act3_ref, dpre_ref, g3_ref, w_ref, act2_ref, g2_ref, s2_ref,
                 low3_ref, t2_ref, parts5_ref, bn_ref):
    a3 = act3_ref[...]
    chan = a3.shape[1]
    mean, rstd = mean_rstd(parts3_ref, chan, count)
    s1, s2 = get_stats(parts4_ref, chan)
    bn_ref[0:1, :] = s2
    bn_ref[1:2, :] = s1
    nrm = (a3 - mean) * rstd
    d = (g3_ref[...] * rstd) * (dpre_ref[...].reshape(a3.shape) - s1 * (1.0 / count) - nrm * (s2 * (1.0 / count)))
    low = jnp.where(real_columns(a3.shape[0], cols), d, 0.0).astype(BF16)
    low3_ref[...] = low
    a2 = act2_ref[...]
    mean2, rstd2 = mean_rstd(parts2_ref, a2.shape[1], count)
    nrm2 = (a2 - mean2) * rstd2
    _, slope = gelu_and_slope(nrm2 * g2_ref[...] + s2_ref[...])
    t2 = nt(low, w_ref[...]) * slope
    t2_ref[...] = t2
    put_stats(parts5_ref, col_sum(t2), col_sum(t2 * nrm2))


def back2_kernel(count, ex, rows, cols, sp_ref, parts5_ref, parts2_ref, parts1_ref, act2_ref, t2_ref, g2_ref, wmid_ref, act1_ref, g1_ref, s1_ref,
                 low2_ref, t1_ref, send_ref, parts6_ref, bn_ref, wide):
    a2 = act2_ref[...]
    mid = a2.shape[1]
    px = rows * 16
    mean, rstd = mean_rstd(parts2_ref, mid, count)
    s1, s2 = get_stats(parts5_ref, mid)
    bn_ref[0:1, :] = s2
    bn_ref[1:2, :] = s1
    nrm = (a2 - mean) * rstd
    d = (g2_ref[...] * rstd) * (t2_ref[...] - s1 * (1.0 / count) - nrm * (s2 * (1.0 / count)))
    d = jnp.where(real_columns(ex * px, cols), d, 0.0)
    low2_ref[...] = d.astype(BF16)
    for e in range(ex):
        part = d[e * px : (e + 1) * px]
        wide[e, 0:16, :] = jnp.zeros((16, 3 * mid), BF16)
        wide[e, px + 16 : px + 32, :] = jnp.zeros((16, 3 * mid), BF16)
        wide[e, 16 : px + 16, 0:mid] = pltpu.roll(part, px - 1, 0).astype(BF16)
        wide[e, 16 : px + 16, mid : 2 * mid] = part.astype(BF16)
        wide[e, 16 : px + 16, 2 * mid : 3 * mid] = pltpu.roll(part, 1, 0).astype(BF16)
    mean1, rstd1 = mean_rstd(parts1_ref, mid, count)
    one = real_columns(px, cols)
    q1 = jnp.zeros((1, mid), F32)
    q2 = jnp.zeros((1, mid), F32)
    for e in range(ex):
        t = None
        for r in range(3):
            for c in range(3):
                term = nt(wide[e, (2 - r) * 16 : (2 - r) * 16 + px, c * mid : (c + 1) * mid], wmid_ref[r, c * mid : (c + 1) * mid, :])
                t = term if t is None else t + term
        nrm1 = (act1_ref[e * px : (e + 1) * px, :] - mean1) * rstd1
        _, slope = gelu_and_slope(nrm1 * g1_ref[...] + s1_ref[...])
        t = jnp.where(one, t * slope, 0.0)
        t1_ref[e] = t.reshape(rows, 16, mid)
        q1 = q1 + col_sum(t)
        q2 = q2 + col_sum(t * nrm1)
    put_stats(parts6_ref, q1, q2)
    half = rows // 2
    other = 1 - sp_ref[0]
    for e in range(ex):
        send_ref[e] = t1_ref[e, pl.ds(other * half, half)].astype(BF16)


def mid_grad_kernel(ex, px, low2_ref, wide_ref, out_ref):
    mid = low2_ref.shape[1]
    for r in range(3):
        tot = None
        for e in range(ex):
            term = tn(low2_ref[e * px : (e + 1) * px, :], wide_ref[e, r * 16 : r * 16 + px, :])
            tot = term if tot is None else tot + term
        for c in range(3):
            for h in range(2):
                at = (r * 3 + c) * (mid // 2)
                src = c * mid + h * (mid // 2)
                out_ref[h, :, at : at + mid // 2] = tot[:, src : src + mid // 2].astype(BF16)


def tn_kernel(a_ref, b_ref, out_ref):
    out_ref[...] = tn(a_ref[...], b_ref[...]).astype(BF16)


def image_kernel(count, ex, rows, cols, sp_ref, parts6_ref, parts1_ref, x_ref, win_ref, g_ref, t1_ref, gott_ref, dpre_ref, gotd_ref,
                 grad_ref, win_grad_ref, bn_ref, xp):
    s = sp_ref[0]
    half = rows // 2
    chan = x_ref.shape[-1]
    mid = win_ref.shape[1]
    mean, rstd = mean_rstd(parts1_ref, mid, count)
    s1, s2 = get_stats(parts6_ref, mid)
    bn_ref[0:1, :] = s2
    bn_ref[1:2, :] = s1
    real = real_columns(ex * half * 16, cols)
    size = ex * half * 16
    xp[...] = jnp.zeros_like(xp)
    wg = None
    for own in (True, False):
        at = (s if own else 1 - s) * ex
        xp[:, 0:cols, :] = x_ref[pl.ds(at, ex)].reshape(ex * half, cols, chan)
        x = xp[...].reshape(size, chan)
        nrm = (nn(x, win_ref[...]) - mean) * rstd
        if own:
            t = t1_ref[:, pl.ds(s * half, half)].reshape(size, mid)
            dp = dpre_ref[:, pl.ds(s * half, half)].reshape(size, chan)
        else:
            t = gott_ref[...].reshape(size, mid).astype(F32)
            dp = gotd_ref[...].reshape(size, chan).astype(F32)
        d = (g_ref[...] * rstd) * (t - s1 * (1.0 / count) - nrm * (s2 * (1.0 / count)))
        low = jnp.where(real, d, 0.0).astype(BF16)
        grad = (nt(low, win_ref[...]) + dp).astype(BF16).reshape(ex, half, 16, chan)
        grad_ref[pl.ds(at, ex)] = grad[:, :, 0:cols, :]
        term = tn(low, x)
        wg = term if wg is None else wg + term
    win_grad_ref[...] = wg.astype(BF16)


def call(kernel, outs, *args, scalars=(), scratch=(), name=None, flops=0):
    n_s = len(scalars)
    nbytes = sum(a.size * a.dtype.itemsize for a in args)
    params = dict(
        out_shape=[jax.ShapeDtypeStruct(s, d) for s, d in outs],
        compiler_params=pltpu.CompilerParams(vmem_limit_bytes=48 << 20),
        cost_estimate=pl.CostEstimate(flops=flops, bytes_accessed=nbytes, transcendentals=0),
        name=name,
    )
    spec = lambda s: pl.BlockSpec(s, lambda *_: (0,) * len(s))
    return pl.pallas_call(
        kernel,
        grid_spec=pltpu.PrefetchScalarGridSpec(
            num_scalar_prefetch=n_s, grid=(1,),
            in_specs=[spec(a.shape) for a in args],
            out_specs=[spec(s) for s, _ in outs],
            scratch_shapes=list(scratch),
        ),
        **params,
    )(*scalars, *args)


EVERY = ("dp", "space")


def spread(parts):
    return lax.all_to_all(parts, EVERY, split_axis=0, concat_axis=0, tiled=True)


def swap(x):
    return lax.ppermute(x, "space", [(0, 1), (1, 0)])


def vector_sums(vectors):
    count = lax.axis_size(EVERY)
    sizes = [v.shape[0] for v in vectors]
    flat = jnp.concatenate(vectors)
    chunk = -(-flat.shape[0] // (count * 128)) * 128
    flat = jnp.pad(flat, (0, chunk * count - flat.shape[0])).reshape(count, chunk)
    mine = jnp.sum(spread(flat), axis=0)
    whole_v = spread(jnp.broadcast_to(mine[None], (count, chunk))).reshape(-1)
    out, at = [], 0
    for size in sizes:
        out.append(whole_v[at : at + size])
        at += size
    return out


def halve_dp(x, axis, bit):
    size = lax.axis_size("dp")
    mine = (lax.axis_index("dp") // bit) % 2
    keep = lax.dynamic_index_in_dim(x, mine, axis, keepdims=True)
    send = lax.dynamic_index_in_dim(x, 1 - mine, axis, keepdims=True)
    return keep + lax.ppermute(send, "dp", [(j, j ^ bit) for j in range(size)])


def halve_columns(x):
    half = x.shape[-1] // 2
    mine = lax.axis_index("space")
    keep = lax.dynamic_slice_in_dim(x, mine * half, half, axis=x.ndim - 1)
    send = lax.dynamic_slice_in_dim(x, (1 - mine) * half, half, axis=x.ndim - 1)
    return keep + swap(send)


def scattered(grad_t, order):
    size = lax.axis_size("dp")
    bits = size.bit_length() - 1
    cols, rows = grad_t.shape
    x = grad_t.reshape((2,) * bits + (cols // size, rows))
    x = halve_dp(x, bits - 1, 1)
    stages = list(range(1, bits))
    if order == 0:
        stages = stages + ["space"]
    elif order == 1:
        stages = ["space"] + stages[1:] + stages[:1]
    else:
        stages = stages[:1] + stages[1:] + ["space"]
    for b in stages:
        x = halve_columns(x) if b == "space" else halve_dp(x, bits - 1 - b, 1 << b)
    return x.reshape(cols // size, rows // 2).astype(F32).T


def shards(
    image_in, text_in, prefix, text_len, cotangent,
    conv_in_w, bn1_gain, bn1_shift, conv_mid_w, bn2_gain, bn2_shift, conv_out_w, bn3_gain, bn3_shift,
    proj_w, proj_b, ln1_gain, ln1_shift, qkv_w, query_bias, value_bias, out_w, out_b,
    ln2_gain, ln2_shift, up_w, up_b, down_w, down_b,
):
    n_dev = lax.axis_size(EVERY)
    band_ex, band_rows, cols, chan = image_in.shape
    mid = conv_in_w.shape[1]
    width = proj_w.shape[1]
    ex, txt, _ = text_in.shape
    rows = band_rows * lax.axis_size("space")
    n_image = rows * cols
    seq = n_image + txt
    pad = -(-seq // 16) * 16
    px = rows * 16
    count = float(band_ex * band_rows * cols * n_dev)
    me = lax.axis_index("space").astype(jnp.int32)
    sp = me.reshape(1)
    row = lambda v: v.reshape(1, -1)
    small, large = (n_dev, stat_rows(mid), 128), (n_dev, stat_rows(chan), 128)
    wmid = conv_mid_w.reshape(3, 3 * mid, mid)

    got_x = swap(lax.dynamic_slice_in_dim(image_in, (1 - me) * ex, ex, axis=0))
    parts1, = call(functools.partial(stats_kernel, cols), [(small, F32)], image_in, conv_in_w,
                   scratch=[pltpu.VMEM((band_ex * band_rows, 16, chan), BF16)], name="stats_one")
    parts1 = spread(parts1)
    xs, act1, wide, act2, parts2 = call(
        functools.partial(conv_fwd_kernel, count, ex, rows, cols),
        [((ex, rows, 16, chan), BF16), ((ex * px, mid), F32), ((ex, px + 32, 3 * mid), BF16), ((ex * px, mid), F32), (small, F32)],
        parts1, image_in, got_x, conv_in_w, row(bn1_gain), row(bn1_shift), wmid, scalars=(sp,), name="conv_three")
    parts2 = spread(parts2)
    relu2, act3, parts3 = call(
        functools.partial(expand_kernel, count, cols),
        [((ex * px, mid), BF16), ((ex * px, chan), F32), (large, F32)],
        parts2, act2, row(bn2_gain), row(bn2_shift), conv_out_w, name="expand")
    parts3 = spread(parts3)
    stem, h0 = call(
        functools.partial(tokens_kernel, count, ex, cols, n_image, pad),
        [((ex * px, chan), BF16), ((ex * pad, width), BF16)],
        parts3, act3, xs, row(bn3_gain), row(bn3_shift), proj_w, row(proj_b), text_in, name="tokens")
    z1, q, k, v, p, attn, h1, z2 = attn_fwd(h0, prefix, text_len, ln1_gain, ln1_shift, qkv_w, query_bias, value_bias,
                                            out_w, out_b, ln2_gain, ln2_shift, ex, n_image, pad)
    block_out, down_g, up_g, up_bg, g1, vec2 = mlp(z2, h1, cotangent, up_w, up_b, down_w, down_b, ln2_gain, ln2_shift, pad)
    out_g, qkv_g, bias, text_grad, dtok, vec1 = attn_bwd(g1, out_w, attn, q, k, v, p, z1, h0, qkv_w, ln1_gain,
                                                         ex, n_image, txt, rows, cols, pad)
    dpre, dsend, parts4 = call(
        functools.partial(dpre_kernel, count, ex, rows),
        [((ex, rows, 16, chan), F32), ((ex, band_rows, 16, chan), BF16), (large, F32)],
        parts3, act3, xs, row(bn3_gain), row(bn3_shift), dtok, proj_w, scalars=(sp,), name="stem_back")
    got_d = swap(dsend)
    parts4 = spread(parts4)
    proj_g, = call(tn_kernel, [((width, chan), BF16)], dtok, stem, name="proj_grad", flops=2 * ex * px * width * chan)
    low3, t2, parts5, bn3 = call(
        functools.partial(back3_kernel, count, cols),
        [((ex * px, chan), BF16), ((ex * px, mid), F32), (small, F32), ((8, chan), F32)],
        parts4, parts3, parts2, act3, dpre, row(bn3_gain), conv_out_w, act2, row(bn2_gain), row(bn2_shift), name="back_three")
    parts5 = spread(parts5)
    conv_out_g, = call(tn_kernel, [((chan, mid), BF16)], low3, relu2, name="conv_out_grad", flops=2 * ex * px * mid * chan)
    low2, t1, tsend, parts6, bn2 = call(
        functools.partial(back2_kernel, count, ex, rows, cols),
        [((ex * px, mid), BF16), ((ex, rows, 16, mid), F32), ((ex, band_rows, 16, mid), BF16), (small, F32), ((8, mid), F32)],
        parts5, parts2, parts1, act2, t2, row(bn2_gain), wmid, act1, row(bn1_gain), row(bn1_shift),
        scalars=(sp,), scratch=[pltpu.VMEM((ex, px + 32, 3 * mid), BF16)], name="back_two")
    got_t = swap(tsend)
    parts6 = spread(parts6)
    mid_g, = call(functools.partial(mid_grad_kernel, ex, px), [((2, mid, 9 * mid // 2), BF16)], low2, wide, name="conv_mid_grad",
                  flops=18 * ex * px * mid * mid)
    image_grad, conv_in_g, bn1 = call(
        functools.partial(image_kernel, count, ex, rows, cols),
        [(image_in.shape, BF16), ((mid, chan), BF16), ((8, mid), F32)],
        parts6, parts1, image_in, conv_in_w, row(bn1_gain), t1, got_t, dpre, got_d,
        scalars=(sp,), scratch=[pltpu.VMEM((ex * band_rows, 16, chan), BF16)], name="image_back")
    small_sums = vector_sums([vec1[2], vec1[0], vec1[1], bias[0], bias[1], vec2[3], vec2[1], vec2[2], up_bg[0], vec2[0]])
    mid_out = scattered(mid_g.transpose(1, 0, 2).reshape(mid, 9 * mid), 0)
    return (
        block_out, image_grad, text_grad,
        scattered(conv_in_g, 0), bn1[0], bn1[1],
        mid_out.reshape(3, 3, mid // 2, mid_out.shape[1]), bn2[0], bn2[1],
        scattered(conv_out_g, 1), bn3[0], bn3[1],
        scattered(proj_g, 1), small_sums[0], small_sums[1], small_sums[2],
        scattered(qkv_g.reshape(3 * width, width), 0), small_sums[3], small_sums[4],
        scattered(out_g, 1), small_sums[5], small_sums[6], small_sums[7],
        scattered(up_g, 0), small_sums[8],
        scattered(down_g, 1), small_sums[9],
    )


def solution(mesh):
    return jax.shard_map(
        shards,
        mesh=mesh,
        in_specs=(
            P("dp", "space", None, None),
            P(("dp", "space"), None, None),
            P(("dp", "space")),
            P(("dp", "space")),
            P(("dp", "space"), None, None),
            P(),
            P(),
            P(),
            P(),
            P(),
            P(),
            P(),
            P(),
            P(),
            P(),
            P(),
            P(),
            P(),
            P(),
            P(),
            P(),
            P(),
            P(),
            P(),
            P(),
            P(),
            P(),
            P(),
            P(),
        ),
        out_specs=(
            P(("dp", "space"), None, None),
            P("dp", "space", None, None),
            P(("dp", "space"), None, None),
            P("space", "dp"),
            P(),
            P(),
            P(None, None, "space", "dp"),
            P(),
            P(),
            P("space", "dp"),
            P(),
            P(),
            P("space", "dp"),
            P(),
            P(),
            P(),
            P("space", "dp"),
            P(),
            P(),
            P("space", "dp"),
            P(),
            P(),
            P(),
            P("space", "dp"),
            P(),
            P("space", "dp"),
            P(),
        ),
        check_vma=False,
    )
```

time: 873 us -> 447 us (0.51)
  local copies, waits for them, and re-layouts: 312 us -> 66.5 us
  matrix products: 162 us -> 0 us
  Pallas kernels: 0 us -> 137 us
  other arithmetic: 109 us -> 17.5 us
  waiting for transfers between devices: 177 us -> 115 us
  blocking collectives: 14.8 us -> 29.6 us
  starting transfers between devices: 83 us -> 73.5 us
    dot_general x30 -> x0, matrix products: 162 us -> none  [the longest x9 42 us: matmul(): return jnp.dot(left, right, preferred_element_type=jnp.float32)]
    pallas_call x0 -> x14, Pallas kernels: none -> 137 us  [the longest x1 40.7 us: mlp(): pl.pallas_call(functools.partial(mlp_kernel, ex, seq, pad), grid=(steps,)...]
    reshape x33 -> x10, local copies, waits for them, and re-layouts: 140 us -> 4.68 us  [the longest x7 4.06 us: attn_fwd(): row = lambda v: v.reshape(1, -1)]
    ppermute x44 -> x43, waiting for transfers between devices: 159 us -> 105 us  [the longest x32 84.8 us: halve_dp(): return keep + lax.ppermute(send, 'dp', [(j, j ^ bit) for j in range(size)])]
    convert_element_type x9 -> x0, local copies, waits for them, and re-layouts: 31.6 us -> none  [the longest x3 12.5 us: scattered(): grad_t.astype(jnp.bfloat16)]
    concatenate x19 -> x0, local copies, waits for them, and re-layouts: 28.8 us -> none  [the longest x18 28.6 us: conv_taps(): return jnp.concatenate(tap_list, axis=-1).reshape(-1, 9 * padded.shape[-1])]
    reduce_sum x16 -> x1, other arithmetic: 26.6 us -> 0.06 us  [vector_sums(): mine = jnp.sum(spread(flat), axis=0)]
    convert_element_type x7 -> x0, other arithmetic: 24.8 us -> none  [the longest x1 10.9 us: shards(): score_grad = (probs_back * (prob_grad - inner_sum)).astype(jnp.bfloat16)]
  transfers between devices with their start and end apart: 53 -> 49, of which waited for: 19 -> 27; matrix products, arithmetic and copies ran while one was open for 27% -> 12% of each run, Pallas kernels for 0% -> 5%
where the time goes in v2:
time: 447 us; the launch traced here: 442 us
  Pallas kernels  137 us (31%)
  waiting for transfers between devices  115 us (26%)
  starting transfers between devices  73.5 us (16%)
  local copies, waits for them, and re-layouts  66.5 us (15%)
  blocking collectives  29.6 us (7%)
  other arithmetic  17.5 us (4%)
    ppermute x32, waiting for transfers between devices, halve_dp(): return keep + lax.ppermute(send, 'dp', [(j, j ^ bit) for j in range(size)])  84.8 us
    pallas_call x1, Pallas kernels, mlp(): pl.pallas_call(functools.partial(mlp_kernel, ex, seq, pad), grid=(steps,)...  40.7 us
    pallas_call x1, Pallas kernels, attn_bwd(): pl.pallas_call(functools.partial(attn_bwd_kernel, ex, n_image, txt, img_c...  36.6 us
    ppermute x32, starting transfers between devices, halve_dp(): return keep + lax.ppermute(send, 'dp', [(j, j ^ bit) for j in range(size)])  32.2 us
    pallas_call x11, Pallas kernels, call(): pl.pallas_call(kernel, grid_spec=pltpu.PrefetchScalarGridSpec(num_scalar_...  31.8 us
    all_to_all x2, blocking collectives, spread(): return lax.all_to_all(parts, EVERY, split_axis=0, concat_axis=0, tiled=True)  29.6 us
    pallas_call x1, Pallas kernels, attn_fwd(): pl.pallas_call(functools.partial(attn_fwd_kernel, ex, n_image, pad), grid...  28 us
    unnamed x162, local copies, waits for them, and re-layouts  27 us
  transfers between devices with their start and end apart: 49, of which 27 were waited for; matrix products, arithmetic and copies ran while one was open for 12% of the time, Pallas kernels for 5%

profile of v2, /device:TPU:0, one launch (start us, length us, event | category | flops | bytes accessed | tf_op | source)
XLA Modules:
  0.0 441.6 jit_solution(2996416363560260455)
XLA Ops:
  2.0 3.0 collective-permute-start
  6.7 16.4 %all_to_all.45.parts_ref.parts1_ref = f32[32,8,128]{2,1,0:T(8,128)S(1)} all-to-all(f32[32,8,128]{2,1,0:T(8,128)S(1)} %stats_one.1), channel_id=1, replica_groups=mesh['dp'=16,'space'=2] {'dp','space'}, dimensions={0} | all-to-all | bytes 262144 | tf_op jit(solution)/shard_map/all_to_all | solution.py:634
  23.1 3.7 conv_three.1
  28.8 13.3 %all_to_all.46.parts_ref.parts2_ref = f32[32,8,128]{2,1,0:T(8,128)S(1)} all-to-all(f32[32,8,128]{2,1,0:T(8,128)S(1)} %get-tuple-element.72), channel_id=1, replica_groups=mesh['dp'=16,'space'=2] {'dp','space'}, dimensions={0} | all-to-all | bytes 262144 | tf_op jit(solution)/shard_map/all_to_all | solution.py:634
  43.1 1.5 copy-done
  46.0 3.5 all-to-all-start.2
  54.3 5.9 %all-to-all-done.2.parts_ref.parts3_ref = f32[32,16,128]{2,1,0:T(8,128)} async-done(((f32[32,16,128]{2,1,0:T(8,128)}), f32[32,16,128]{2,1,0:T(8,128)}, u32[]{:S(2)}, u32[]{:S(2)}) %all-to-all-start.2) | async-done | bytes 262176 | tf_op jit(solution)/shard_map/all_to_all | solution.py:634
  62.5 4.7 %tokens.1 = (bf16[672,1024]{1,0:T(8,128)(2,1)S(1)}, bf16[816,768]{1,0:T(8,128)(2,1)S(1)}) custom-call(f32[32,16,128]{2,1,0:T(8,128)} %all-to-all-done.2.parts_ref.parts3_ref, f32[672,1024]{1,0:T(8,128)} %copy-done, bf16[3,14,16,1024]{3,2,1,0:T(8,128)(2,1)S(1)} %copy-done.4, f32[1,1024]{1,0:T(1,128)S(1)} %bitcast.81, f32[1,1024]{1,0:T(1,128)S(1)} %bitcast.84, ...), custom_call_target="tpu_custom_call" | custom-call | bytes 6269952 | tf_op jit(solution)/shard_map/tokens/pallas_call | solution.py:618
  69.4 28.0 %attention_forward.1 = (bf16[816,768]{1,0:T(8,128)(2,1)}, bf16[816,768]{1,0:T(8,128)(2,1)}, bf16[816,768]{1,0:T(8,128)(2,1)}, bf16[816,768]{1,0:T(8,128)(2,1)}, ...) custom-call(s32[3]{0:T(128)} %pre_ref.1, ...), custom_call_target="tpu_custom_call" | custom-call | flops 5214044160 | bytes 31457280 | tf_op jit(solution)/shard_map/attention_forward/pallas_call | solution.py:222
  97.4 40.7 %mlp_both_ways.1 = (bf16[3,260,768]{2,1,0:T(8,128)(2,1)}, bf16[768,3072]{1,0:T(8,128)(2,1)}, bf16[3072,768]{1,0:T(8,128)(2,1)}, f32[1,3072]{1,0:T(1,128)}, f32[816,768]{1,0:T(8,128)}, /*index=5*/f32[8,768]{1,0:T(8,128)}) custom-call(bf16[816,768]{1,0:T(8,128)(2,1)} %get-tuple-element.78.z2_ref, f32[816,768]{1,0:T(8,128)} %get-tuple-element.79.h1_ref, ...), custom_call_target="tpu_custom_call" | custom-call | flops 23102226432 | bytes 41943040 | tf_op jit(solution)/shard_map/mlp_both_ways/pallas_call | solution.py:111
  139.0 36.6 %attention_backward.1 = (bf16[768,768]{1,0:T(8,128)(2,1)}, bf16[3,768,768]{2,1,0:T(8,128)(2,1)}, f32[8,768]{1,0:T(8,128)}, bf16[3,64,768]{2,1,0:T(8,128)(2,1)}, ...) custom-call(f32[816,768]{1,0:T(8,128)} %get-tuple-element.81.g1_ref, bf16[768,768]{1,0:T(8,128)(2,1)} %ow_ref.3, ...), custom_call_target="tpu_custom_call" | custom-call | flops 11109924864 | bytes 41943040 | tf_op jit(solution)/shard_map/attention_backward/pallas_call | solution.py:340
  177.2 2.6 all-to-all-start.6
  179.8 3.2 constant_dynamic-slice_fusion.4
  183.1 4.1 all-to-all-done.6
  188.0 2.6 all-to-all-start.7
  190.6 3.5 constant_dynamic-slice_fusion.9
  194.2 6.7 %stem_back.1 = (f32[3,14,16,1024]{3,2,1,0:T(8,128)}, bf16[3,7,16,1024]{3,2,1,0:T(8,128)(2,1)}, f32[32,16,128]{2,1,0:T(8,128)S(1)}) custom-call(s32[1]{0:T(128)} %bitcast.sp_ref, f32[32,16,128]{2,1,0:T(8,128)} %all-to-all-done.2.parts_ref.parts3_ref, f32[672,1024]{1,0:T(8,128)} %copy-done, bf16[3,14,16,1024]{3,2,1,0:T(8,128)(2,1)S(1)} %copy-done.5, ...), custom_call_target="tpu_custom_call" | custom-call | bytes 7004160 | tf_op jit(solution)/shard_map/stem_back/pallas_call | solution.py:618
  201.6 6.5 %all-to-all-start.3 = ((f32[32,16,128]{2,1,0:T(8,128)}), f32[32,16,128]{2,1,0:T(8,128)}, u32[]{:S(2)}, u32[]{:S(2)}) async-start(f32[32,16,128]{2,1,0:T(8,128)} %copy-done.36), calls=%async_computation.3 | async-start | bytes 524288 | tf_op jit(solution)/shard_map/all_to_all | solution.py:634
  208.0 1.9 constant_dynamic-slice_fusion.14
  215.5 1.9 collective-permute-start.2
  226.7 4.2 back_three.1
  233.5 4.8 %all-to-all-start.4 = ((f32[32,8,128]{2,1,0:T(8,128)}), f32[32,8,128]{2,1,0:T(8,128)}, u32[]{:S(2)}, u32[]{:S(2)}) async-start(f32[32,8,128]{2,1,0:T(8,128)} %copy-done.37), calls=%async_computation.4 | async-start | bytes 262144 | tf_op jit(solution)/shard_map/all_to_all | solution.py:634
  250.9 3.3 back_two.1
  255.3 2.2 copy.60
  257.5 3.2 reshape_reshape.6
  261.7 5.3 %all-to-all-start.5 = ((f32[32,8,128]{2,1,0:T(8,128)}), f32[32,8,128]{2,1,0:T(8,128)S(1)}, u32[]{:S(2)}, u32[]{:S(2)}) async-start(f32[32,8,128]{2,1,0:T(8,128)} %get-tuple-element.94), calls=%async_computation.5 | async-start | bytes 262144 | tf_op jit(solution)/shard_map/all_to_all | solution.py:634
  267.6 1.9 collective-permute-start.29
  272.1 8.9 %collective-permute-done.14 = bf16[2,2,2,1,64,128]{5,4,3,2,1,0:T(8,128)(2,1)S(1)} collective-permute-done((bf16[2,2,2,1,64,128]{5,4,3,2,1,0:T(8,128)(2,1)S(1)}, bf16[2,2,2,1,64,128]{5,4,3,2,1,0:T(8,128)(2,1)S(1)}, u32[]{:S(2)}, u32[]{:S(2)}) %collective-permute-start.14) | collective-permute-done | bytes 131104 | tf_op jit(solution)/shard_map/ppermute | solution.py:638
  283.3 2.1 collective-permute-done.15
  286.7 2.0 collective-permute-start.16
  288.8 2.8 collective-permute-done.16
  295.4 4.5 %image_back.1 = (bf16[6,7,14,1024]{3,2,1,0:T(8,128)(2,1)}, bf16[256,1024]{1,0:T(8,128)(2,1)S(1)}, f32[8,256]{1,0:T(8,128)S(1)}) custom-call(s32[1]{0:T(128)} %bitcast.sp_ref, f32[32,8,128]{2,1,0:T(8,128)S(1)} %all-to-all-done.5.parts6_ref, f32[32,8,128]{2,1,0:T(8,128)S(1)} %copy-done.21, bf16[6,7,14,1024]{3,2,1,0:T(8,128)(2,1)S(1)} %copy-done.2, ...), custom_call_target="tpu_custom_call" | custom-call | bytes 6292480 | tf_op jit(solution)/shard_map/image_back/pallas_call | solution.py:618
  302.6 3.2 collective-permute-done.30
  305.9 2.4 collective-permute-start.31
  308.9 2.4 collective-permute-done.31
  311.9 3.4 collective-permute-done.32
  319.8 5.0 %collective-permute-done.20 = bf16[2,1,2,1,48,512]{5,4,3,2,1,0:T(8,128)(2,1)S(1)} collective-permute-done((bf16[2,1,2,1,48,512]{5,4,3,2,1,0:T(8,128)(2,1)S(1)}, bf16[2,1,2,1,48,512]{5,4,3,2,1,0:T(8,128)(2,1)S(1)}, u32[]{:S(2)}, u32[]{:S(2)}) %collective-permute-start.20) | collective-permute-done | bytes 196640 | tf_op jit(solution)/shard_map/ppermute | solution.py:661
  326.9 2.9 collective-permute-done.5
  329.8 2.5 collective-permute-start.21
  332.3 4.1 collective-permute-done.21
  336.3 1.5 collective-permute-start.6
  337.9 3.3 collective-permute-done.6
  341.7 3.6 collective-permute-done.22
  345.2 2.3 collective-permute-start.7
  348.8 1.7 dynamic-slice_add_fusion.2
  350.5 3.0 collective-permute-done.10
  357.1 2.4 collective-permute-done.11
  360.4 3.2 collective-permute-done.12
  364.3 6.6 %collective-permute-done.24 = bf16[2,2,1,1,144,768]{5,4,3,2,1,0:T(8,128)(2,1)S(1)} collective-permute-done((bf16[2,2,1,1,144,768]{5,4,3,2,1,0:T(8,128)(2,1)}, bf16[2,2,1,1,144,768]{5,4,3,2,1,0:T(8,128)(2,1)S(1)}, u32[]{:S(2)}, u32[]{:S(2)}) %collective-permute-start.24) | collective-permute-done | bytes 884768 | tf_op jit(solution)/shard_map/ppermute | solution.py:661
  371.0 1.8 collective-permute-start.25
  372.8 2.6 dynamic-slice_add_fusion
  376.9 4.7 %collective-permute-done.25 = bf16[2,1,1,1,144,768]{5,4,3,2,1,0:T(8,128)(2,1)S(1)} collective-permute-done((bf16[2,1,1,1,144,768]{5,4,3,2,1,0:T(8,128)(2,1)S(1)}, bf16[2,1,1,1,144,768]{5,4,3,2,1,0:T(8,128)(2,1)S(1)}, u32[]{:S(2)}, u32[]{:S(2)}) %collective-permute-start.25) | collective-permute-done | bytes 442400 | tf_op jit(solution)/shard_map/ppermute | solution.py:661
  383.0 1.9 dynamic-slice_add_fusion.1
  385.0 1.8 collective-permute-start.34
  386.8 3.6 collective-permute-done.26
  390.4 1.5 collective-permute-start.27
  391.9 5.0 %collective-permute-done.39 = bf16[2,2,2,1,48,1536]{5,4,3,2,1,0:T(8,128)(2,1)S(1)} collective-permute-done((bf16[2,2,2,1,48,1536]{5,4,3,2,1,0:T(8,128)(2,1)S(1)}, bf16[2,2,2,1,48,1536]{5,4,3,2,1,0:T(8,128)(2,1)S(1)}, u32[]{:S(2)}, u32[]{:S(2)}) %collective-permute-start.39) | collective-permute-done | bytes 1179680 | tf_op jit(solution)/shard_map/ppermute | solution.py:638
  399.1 2.7 collective-permute-done.34
  402.0 1.5 collective-permute-start.35
  403.6 10.0 %collective-permute-done.40 = bf16[2,1,2,1,48,1536]{5,4,3,2,1,0:T(8,128)(2,1)S(1)} collective-permute-done((bf16[2,1,2,1,48,1536]{5,4,3,2,1,0:T(8,128)(2,1)S(1)}, bf16[2,1,2,1,48,1536]{5,4,3,2,1,0:T(8,128)(2,1)S(1)}, u32[]{:S(2)}, u32[]{:S(2)}) %collective-permute-start.40) | collective-permute-done | bytes 589856 | tf_op jit(solution)/shard_map/ppermute | solution.py:661
  413.7 11.2 %collective-permute-done.35 = bf16[2,1,1,1,192,768]{5,4,3,2,1,0:T(8,128)(2,1)S(1)} collective-permute-done((bf16[2,1,1,1,192,768]{5,4,3,2,1,0:T(8,128)(2,1)S(1)}, bf16[2,1,1,1,192,768]{5,4,3,2,1,0:T(8,128)(2,1)S(1)}, u32[]{:S(2)}, u32[]{:S(2)}) %collective-permute-start.35) | collective-permute-done | bytes 589856 | tf_op jit(solution)/shard_map/ppermute | solution.py:661
  425.6 1.9 collective-permute-start.42
  427.6 7.8 %collective-permute-done.36 = bf16[1,1,1,1,192,768]{5,4,3,2,1,0:T(8,128)(2,1)S(1)} collective-permute-done((bf16[1,1,1,1,192,768]{5,4,3,2,1,0:T(8,128)(2,1)S(1)}, bf16[1,1,1,1,192,768]{5,4,3,2,1,0:T(8,128)(2,1)S(1)}, u32[]{:S(2)}, u32[]{:S(2)}) %collective-permute-start.36) | collective-permute-done | bytes 294944 | tf_op jit(solution)/shard_map/ppermute | solution.py:661
  437.6 3.0 collective-permute-done.37
  (327 shorter events, 89.7 us)
Async XLA Ops:
  0.7 22.3 %copy-start.6 = (bf16[3,3,256,256]{3,2,1,0:T(8,128)(2,1)S(1)}, bf16[3,3,256,256]{3,2,1,0:T(8,128)(2,1)}, u32[]{:S(2)}) copy-start(bf16[3,3,256,256]{3,2,1,0:T(8,128)(2,1)} %param.37) | copy-start | bytes 3538948
  2.0 21.0 %collective-permute-start = (bf16[3,7,14,1024]{3,2,1,0:T(8,128)(2,1)S(1)}, bf16[3,7,14,1024]{3,2,1,0:T(8,128)(2,1)S(1)}, u32[]{:S(2)}, u32[]{:S(2)}) collective-permute-start(bf16[3,7,14,1024]{3,2,1,0:T(8,128)(2,1)S(1)} %constant_dynamic-slice_fusion.42), channel_id=1, source_target_pairs={{0,1},{1,0},{2,3},{3,2},{4,5},{5,4},{6,7},{7,6},{8,9},{9,8},{10,11... | collective-permute-start | bytes 1806344 | tf_op jit(solution)/shard_map/ppermute | solution.py:638
  28.7 22.7 %copy-start.69 = (f32[768]{0:T(1024)S(1)}, f32[768]{0:T(1024)}, u32[]{:S(2)}) copy-start(f32[768]{0:T(1024)} %param.46) | copy-start | bytes 9220
  28.7 23.3 %copy-start.70 = (f32[768]{0:T(1024)S(1)}, f32[768]{0:T(1024)}, u32[]{:S(2)}) copy-start(f32[768]{0:T(1024)} %param.48) | copy-start | bytes 9220
  28.7 23.8 %copy-start.71 = (f32[768]{0:T(1024)S(1)}, f32[768]{0:T(1024)}, u32[]{:S(2)}) copy-start(f32[768]{0:T(1024)} %param.49) | copy-start | bytes 9220
  28.7 24.4 %copy-start.72 = (f32[768]{0:T(1024)S(1)}, f32[768]{0:T(1024)}, u32[]{:S(2)}) copy-start(f32[768]{0:T(1024)} %param.51) | copy-start | bytes 9220
  28.7 25.0 %copy-start.73 = (f32[768]{0:T(1024)S(1)}, f32[768]{0:T(1024)}, u32[]{:S(2)}) copy-start(f32[768]{0:T(1024)} %param.57) | copy-start | bytes 9220
  28.7 31.4 %copy-start.3 = (bf16[1024,768]{1,0:T(8,128)(2,1)S(1)}, bf16[1024,768]{1,0:T(8,128)(2,1)}, u32[]{:S(2)}) copy-start(bf16[1024,768]{1,0:T(8,128)(2,1)} %w_ref.8) | copy-start | bytes 4718596
  28.7 31.4 %copy-start.38 = (f32[1024]{0:T(1024)S(1)}, f32[1024]{0:T(1024)}, u32[]{:S(2)}) copy-start(f32[1024]{0:T(1024)} %param.41) | copy-start | bytes 12292
  28.7 31.4 %copy-start.39 = (f32[1024]{0:T(1024)S(1)}, f32[1024]{0:T(1024)}, u32[]{:S(2)}) copy-start(f32[1024]{0:T(1024)} %param.42) | copy-start | bytes 12292
  46.0 14.2 %all-to-all-start.2 = ((f32[32,16,128]{2,1,0:T(8,128)}), f32[32,16,128]{2,1,0:T(8,128)}, u32[]{:S(2)}, u32[]{:S(2)}) async-start(f32[32,16,128]{2,1,0:T(8,128)} %copy-done.35), calls=%async_computation.2 | async-start | bytes 524288 | tf_op jit(solution)/shard_map/all_to_all | solution.py:634
  139.0 37.6 %copy-start.64 = (f32[1,3072]{1,0:T(1,128)S(1)}, f32[1,3072]{1,0:T(1,128)}, u32[]{:S(2)}) copy-start(f32[1,3072]{1,0:T(1,128)} %get-tuple-element.112) | copy-start | bytes 36868
  177.2 10.1 %all-to-all-start.6 = ((f32[32,1,384]{2,1,0:T(1,128)}), f32[32,1,384]{2,1,0:T(1,128)S(1)}, u32[]{:S(2)}, u32[]{:S(2)}) async-start(f32[32,1,384]{2,1,0:T(1,128)} %bitcast.106), calls=%async_computation.6 | async-start | bytes 98304 | tf_op jit(solution)/shard_map/all_to_all | solution.py:634
  183.0 189.8 %collective-permute-start.38 = (bf16[2,2,2,1,48,3072]{5,4,3,2,1,0:T(8,128)(2,1)}, bf16[2,2,2,1,48,3072]{5,4,3,2,1,0:T(8,128)(2,1)}, u32[]{:S(2)}, u32[]{:S(2)}) collective-permute-start(bf16[2,2,2,1,48,3072]{5,4,3,2,1,0:T(8,128)(2,1)} %constant_dynamic-slice_fusion.4), channel_id=1, source_target_pairs={{0,2},{2,0},{4,6},{6,4},{8,10},{10,8},{12,14},{14,12},{16,18},{18,... | collective-permute-start | bytes 7077896 | tf_op jit(solution)/shard_map/ppermute | solution.py:661
  188.0 13.6 %all-to-all-start.7 = ((f32[32,1,384]{2,1,0:T(1,128)}), f32[32,1,384]{2,1,0:T(1,128)S(1)}, u32[]{:S(2)}, u32[]{:S(2)}) async-start(f32[32,1,384]{2,1,0:T(1,128)} %broadcast_in_dim.2), calls=%async_computation.7 | async-start | bytes 98304 | tf_op jit(solution)/shard_map/all_to_all | solution.py:634
  194.0 188.9 %collective-permute-start.33 = (bf16[2,2,2,1,192,768]{5,4,3,2,1,0:T(8,128)(2,1)}, bf16[2,2,2,1,192,768]{5,4,3,2,1,0:T(8,128)(2,1)}, u32[]{:S(2)}, u32[]{:S(2)}) collective-permute-start(bf16[2,2,2,1,192,768]{5,4,3,2,1,0:T(8,128)(2,1)} %constant_dynamic-slice_fusion.9), channel_id=1, source_target_pairs={{0,2},{2,0},{4,6},{6,4},{8,10},{10,8},{12,14},{14,12},{16,18},{18,... | collective-permute-start | bytes 7077896 | tf_op jit(solution)/shard_map/ppermute | solution.py:661
  201.6 23.2 %all-to-all-start.3 = ((f32[32,16,128]{2,1,0:T(8,128)}), f32[32,16,128]{2,1,0:T(8,128)}, u32[]{:S(2)}, u32[]{:S(2)}) async-start(f32[32,16,128]{2,1,0:T(8,128)} %copy-done.36), calls=%async_computation.3 | async-start | bytes 524288 | tf_op jit(solution)/shard_map/all_to_all | solution.py:634
  210.0 33.4 %collective-permute-start.28 = (bf16[2,2,2,1,48,768]{5,4,3,2,1,0:T(8,128)(2,1)}, bf16[2,2,2,1,48,768]{5,4,3,2,1,0:T(8,128)(2,1)}, u32[]{:S(2)}, u32[]{:S(2)}) collective-permute-start(bf16[2,2,2,1,48,768]{5,4,3,2,1,0:T(8,128)(2,1)} %constant_dynamic-slice_fusion.14), channel_id=1, source_target_pairs={{0,2},{2,0},{4,6},{6,4},{8,10},{10,8},{12,14},{14,12},{16,18},{18,... | collective-permute-start | bytes 1769480 | tf_op jit(solution)/shard_map/ppermute | solution.py:661
  215.3 55.2 %collective-permute-start.18 = (bf16[2,2,2,1,48,1024]{5,4,3,2,1,0:T(8,128)(2,1)}, bf16[2,2,2,1,48,1024]{5,4,3,2,1,0:T(8,128)(2,1)}, u32[]{:S(2)}, u32[]{:S(2)}) collective-permute-start(bf16[2,2,2,1,48,1024]{5,4,3,2,1,0:T(8,128)(2,1)} %constant_dynamic-slice_fusion.24), channel_id=1, source_target_pairs={{0,2},{2,0},{4,6},{6,4},{8,10},{10,8},{12,14},{14,12},{16,18},{18,... | collective-permute-start | bytes 2359304 | tf_op jit(solution)/shard_map/ppermute | solution.py:661
  215.5 78.9 %collective-permute-start.2 = (bf16[3,7,16,1024]{3,2,1,0:T(8,128)(2,1)}, bf16[3,7,16,1024]{3,2,1,0:T(8,128)(2,1)}, u32[]{:S(2)}, u32[]{:S(2)}) collective-permute-start(bf16[3,7,16,1024]{3,2,1,0:T(8,128)(2,1)} %get-tuple-element.97), channel_id=1, source_target_pairs={{0,1},{1,0},{2,3},{3,2},{4,5},{5,4},{6,7},{7,6},{8,9},{9,8},{10,11... | collective-permute-start | bytes 2064392 | tf_op jit(solution)/shard_map/ppermute | solution.py:638
  233.5 13.4 %all-to-all-start.4 = ((f32[32,8,128]{2,1,0:T(8,128)}), f32[32,8,128]{2,1,0:T(8,128)}, u32[]{:S(2)}, u32[]{:S(2)}) async-start(f32[32,8,128]{2,1,0:T(8,128)} %copy-done.37), calls=%async_computation.4 | async-start | bytes 262144 | tf_op jit(solution)/shard_map/all_to_all | solution.py:634
  243.4 24.2 %collective-permute-start.13 = (bf16[2,2,2,1,64,256]{5,4,3,2,1,0:T(8,128)(2,1)}, bf16[2,2,2,1,64,256]{5,4,3,2,1,0:T(8,128)(2,1)}, u32[]{:S(2)}, u32[]{:S(2)}) collective-permute-start(bf16[2,2,2,1,64,256]{5,4,3,2,1,0:T(8,128)(2,1)} %constant_dynamic-slice_fusion.30), channel_id=1, source_target_pairs={{0,2},{2,0},{4,6},{6,4},{8,10},{10,8},{12,14},{14,12},{16,18},{18,... | collective-permute-start | bytes 786440 | tf_op jit(solution)/shard_map/ppermute | solution.py:661
  261.7 33.6 %all-to-all-start.5 = ((f32[32,8,128]{2,1,0:T(8,128)}), f32[32,8,128]{2,1,0:T(8,128)S(1)}, u32[]{:S(2)}, u32[]{:S(2)}) async-start(f32[32,8,128]{2,1,0:T(8,128)} %get-tuple-element.94), calls=%async_computation.5 | async-start | bytes 262144 | tf_op jit(solution)/shard_map/all_to_all | solution.py:634
  267.6 19.1 %collective-permute-start.29 = (bf16[2,2,2,1,48,384]{5,4,3,2,1,0:T(8,128)(2,1)}, bf16[2,2,2,1,48,384]{5,4,3,2,1,0:T(8,128)(2,1)S(1)}, u32[]{:S(2)}, u32[]{:S(2)}) collective-permute-start(bf16[2,2,2,1,48,384]{5,4,3,2,1,0:T(8,128)(2,1)} %constant_dynamic-slice_fusion.13), channel_id=1, source_target_pairs={{0,1},{1,0},{2,3},{3,2},{4,5},{5,4},{6,7},{7,6},{8,9},{9,8},{10,11... | collective-permute-start | bytes 884744 | tf_op jit(solution)/shard_map/ppermute | solution.py:638
  270.6 10.4 %collective-permute-start.14 = (bf16[2,2,2,1,64,128]{5,4,3,2,1,0:T(8,128)(2,1)S(1)}, bf16[2,2,2,1,64,128]{5,4,3,2,1,0:T(8,128)(2,1)S(1)}, u32[]{:S(2)}, u32[]{:S(2)}) collective-permute-start(bf16[2,2,2,1,64,128]{5,4,3,2,1,0:T(8,128)(2,1)S(1)} %constant_dynamic-slice_fusion.29), channel_id=1, source_target_pairs={{0,1},{1,0},{2,3},{3,2},{4,5},{5,4},{6,7},{7,6},{8,9},{9,8},{10,11... | collective-permute-start | bytes 393224 | tf_op jit(solution)/shard_map/ppermute | solution.py:638
  272.0 23.3 %copy-start.2 = (bf16[6,7,14,1024]{3,2,1,0:T(8,128)(2,1)S(1)}, bf16[6,7,14,1024]{3,2,1,0:T(8,128)(2,1)}, u32[]{:S(2)}) copy-start(bf16[6,7,14,1024]{3,2,1,0:T(8,128)(2,1)} %x_ref.3) | copy-start | bytes 3612676
  272.0 23.3 %copy-start.9 = (bf16[1024,256]{1,0:T(8,128)(2,1)S(1)}, bf16[1024,256]{1,0:T(8,128)(2,1)}, u32[]{:S(2)}) copy-start(bf16[1024,256]{1,0:T(8,128)(2,1)} %win_ref.3) | copy-start | bytes 1572868
  272.1 23.3 %copy-start.21 = (f32[32,8,128]{2,1,0:T(8,128)S(1)}, f32[32,8,128]{2,1,0:T(8,128)}, u32[]{:S(2)}) copy-start(f32[32,8,128]{2,1,0:T(8,128)} %copy-done.19) | copy-start | bytes 393220
  272.1 23.3 %copy-start.31 = (f32[3,14,16,256]{3,2,1,0:T(8,128)S(1)}, f32[3,14,16,256]{3,2,1,0:T(8,128)}, u32[]{:S(2)}) copy-start(f32[3,14,16,256]{3,2,1,0:T(8,128)} %copy-done.30) | copy-start | bytes 2064388
  281.0 4.3 collective-permute-start.15
  285.4 9.0 %collective-permute-start.1 = (bf16[3,7,16,256]{3,2,1,0:T(8,128)(2,1)S(1)}, bf16[3,7,16,256]{3,2,1,0:T(8,128)(2,1)S(1)}, u32[]{:S(2)}, u32[]{:S(2)}) collective-permute-start(bf16[3,7,16,256]{3,2,1,0:T(8,128)(2,1)S(1)} %copy-done.48), channel_id=1, source_target_pairs={{0,1},{1,0},{2,3},{3,2},{4,5},{5,4},{6,7},{7,6},{8,9},{9,8},{10,11... | collective-permute-start | bytes 516104 | tf_op jit(solution)/shard_map/ppermute | solution.py:638
  286.7 4.9 %collective-permute-start.16 = (bf16[1,1,2,1,64,128]{5,4,3,2,1,0:T(8,128)(2,1)S(1)}, bf16[1,1,2,1,64,128]{5,4,3,2,1,0:T(8,128)(2,1)S(1)}, u32[]{:S(2)}, u32[]{:S(2)}) collective-permute-start(bf16[1,1,2,1,64,128]{5,4,3,2,1,0:T(8,128)(2,1)S(1)} %constant_dynamic-slice_fusion.27), channel_id=1, source_target_pairs={{0,16},{2,18},{4,20},{6,22},{8,24},{10,26},{12,28},{14,30},{16,0},... | collective-permute-start | bytes 98312 | tf_op jit(solution)/shard_map/ppermute | solution.py:661
  292.2 7.7 %collective-permute-start.17 = (bf16[1,1,1,1,64,128]{5,4,3,2,1,0:T(8,128)(2,1)}, bf16[1,1,1,1,64,128]{5,4,3,2,1,0:T(8,128)(2,1)}, u32[]{:S(2)}, u32[]{:S(2)}) collective-permute-start(bf16[1,1,1,1,64,128]{5,4,3,2,1,0:T(8,128)(2,1)} %constant_dynamic-slice_fusion.25), channel_id=1, source_target_pairs={{0,4},{2,6},{4,0},{6,2},{8,12},{10,14},{12,8},{14,10},{16,20},{18,... | collective-permute-start | bytes 49160 | tf_op jit(solution)/shard_map/ppermute | solution.py:661
  294.3 54.4 %collective-permute-start.23 = (bf16[2,2,2,1,144,768]{5,4,3,2,1,0:T(8,128)(2,1)}, bf16[2,2,2,1,144,768]{5,4,3,2,1,0:T(8,128)(2,1)}, u32[]{:S(2)}, u32[]{:S(2)}) collective-permute-start(bf16[2,2,2,1,144,768]{5,4,3,2,1,0:T(8,128)(2,1)} %constant_dynamic-slice_fusion.19), channel_id=1, source_target_pairs={{0,2},{2,0},{4,6},{6,4},{8,10},{10,8},{12,14},{14,12},{16,18},{18,... | collective-permute-start | bytes 5308424 | tf_op jit(solution)/shard_map/ppermute | solution.py:661
  294.4 21.6 %collective-permute-start.19 = (bf16[2,2,2,1,48,512]{5,4,3,2,1,0:T(8,128)(2,1)}, bf16[2,2,2,1,48,512]{5,4,3,2,1,0:T(8,128)(2,1)}, u32[]{:S(2)}, u32[]{:S(2)}) collective-permute-start(bf16[2,2,2,1,48,512]{5,4,3,2,1,0:T(8,128)(2,1)} %constant_dynamic-slice_fusion.23), channel_id=1, source_target_pairs={{0,1},{1,0},{2,3},{3,2},{4,5},{5,4},{6,7},{7,6},{8,9},{9,8},{10,11... | collective-permute-start | bytes 1179656 | tf_op jit(solution)/shard_map/ppermute | solution.py:638
  299.9 6.0 %collective-permute-start.30 = (bf16[2,1,2,1,48,384]{5,4,3,2,1,0:T(8,128)(2,1)S(1)}, bf16[2,1,2,1,48,384]{5,4,3,2,1,0:T(8,128)(2,1)S(1)}, u32[]{:S(2)}, u32[]{:S(2)}) collective-permute-start(bf16[2,1,2,1,48,384]{5,4,3,2,1,0:T(8,128)(2,1)S(1)} %copy-done.61), channel_id=1, source_target_pairs={{0,8},{2,10},{4,12},{6,14},{8,0},{10,2},{12,4},{14,6},{16,24},{18,... | collective-permute-start | bytes 442376 | tf_op jit(solution)/shard_map/ppermute | solution.py:661
  305.9 5.4 %collective-permute-start.31 = (bf16[1,1,2,1,48,384]{5,4,3,2,1,0:T(8,128)(2,1)S(1)}, bf16[1,1,2,1,48,384]{5,4,3,2,1,0:T(8,128)(2,1)S(1)}, u32[]{:S(2)}, u32[]{:S(2)}) collective-permute-start(bf16[1,1,2,1,48,384]{5,4,3,2,1,0:T(8,128)(2,1)S(1)} %constant_dynamic-slice_fusion.11), channel_id=1, source_target_pairs={{0,16},{2,18},{4,20},{6,22},{8,24},{10,26},{12,28},{14,30},{16,0},... | collective-permute-start | bytes 221192 | tf_op jit(solution)/shard_map/ppermute | solution.py:661
  311.3 4.0 collective-permute-start.32
  315.3 3.8 collective-permute-start.8
  316.0 1.7 collective-permute-start.3
  317.7 7.1 %collective-permute-start.20 = (bf16[2,1,2,1,48,512]{5,4,3,2,1,0:T(8,128)(2,1)S(1)}, bf16[2,1,2,1,48,512]{5,4,3,2,1,0:T(8,128)(2,1)S(1)}, u32[]{:S(2)}, u32[]{:S(2)}) collective-permute-start(bf16[2,1,2,1,48,512]{5,4,3,2,1,0:T(8,128)(2,1)S(1)} %constant_dynamic-slice_fusion.22), channel_id=1, source_target_pairs={{0,8},{2,10},{4,12},{6,14},{8,0},{10,2},{12,4},{14,6},{16,24},{18,... | collective-permute-start | bytes 589832 | tf_op jit(solution)/shard_map/ppermute | solution.py:661
  319.1 6.2 %collective-permute-start.4 = (bf16[2,2,1,1,16,1024]{5,4,3,2,1,0:T(8,128)(2,1)S(1)}, bf16[2,2,1,1,16,1024]{5,4,3,2,1,0:T(8,128)(2,1)S(1)}, u32[]{:S(2)}, u32[]{:S(2)}) collective-permute-start(bf16[2,2,1,1,16,1024]{5,4,3,2,1,0:T(8,128)(2,1)S(1)} %constant_dynamic-slice_fusion.40), channel_id=1, source_target_pairs={{0,4},{2,6},{4,0},{6,2},{8,12},{10,14},{12,8},{14,10},{16,20},{18,... | collective-permute-start | bytes 393224 | tf_op jit(solution)/shard_map/ppermute | solution.py:661
  319.8 29.0 %copy-start.52 = (bf16[3,768,768]{2,1,0:T(8,128)(2,1)S(1)}, bf16[3,768,768]{2,1,0:T(8,128)(2,1)}, u32[]{:S(2)}) copy-start(bf16[3,768,768]{2,1,0:T(8,128)(2,1)} %get-tuple-element.113) | copy-start | bytes 10616836
  324.8 23.4 %collective-permute-start.9 = (bf16[2,2,1,1,16,2304]{5,4,3,2,1,0:T(8,128)(2,1)S(1)}, bf16[2,2,1,1,16,2304]{5,4,3,2,1,0:T(8,128)(2,1)S(1)}, u32[]{:S(2)}, u32[]{:S(2)}) collective-permute-start(bf16[2,2,1,1,16,2304]{5,4,3,2,1,0:T(8,128)(2,1)S(1)} %constant_dynamic-slice_fusion.34), channel_id=1, source_target_pairs={{0,4},{2,6},{4,0},{6,2},{8,12},{10,14},{12,8},{14,10},{16,20},{18,... | collective-permute-start | bytes 884744 | tf_op jit(solution)/shard_map/ppermute | solution.py:661
  325.4 4.3 collective-permute-start.5
  329.8 6.6 %collective-permute-start.21 = (bf16[1,1,2,1,48,512]{5,4,3,2,1,0:T(8,128)(2,1)S(1)}, bf16[1,1,2,1,48,512]{5,4,3,2,1,0:T(8,128)(2,1)S(1)}, u32[]{:S(2)}, u32[]{:S(2)}) collective-permute-start(bf16[1,1,2,1,48,512]{5,4,3,2,1,0:T(8,128)(2,1)S(1)} %constant_dynamic-slice_fusion.21), channel_id=1, source_target_pairs={{0,16},{2,18},{4,20},{6,22},{8,24},{10,26},{12,28},{14,30},{16,0},... | collective-permute-start | bytes 294920 | tf_op jit(solution)/shard_map/ppermute | solution.py:661
  336.3 4.8 %collective-permute-start.6 = (bf16[1,1,1,1,16,1024]{5,4,3,2,1,0:T(8,128)(2,1)S(1)}, bf16[1,1,1,1,16,1024]{5,4,3,2,1,0:T(8,128)(2,1)S(1)}, u32[]{:S(2)}, u32[]{:S(2)}) collective-permute-start(bf16[1,1,1,1,16,1024]{5,4,3,2,1,0:T(8,128)(2,1)S(1)} %constant_dynamic-slice_fusion.38), channel_id=1, source_target_pairs={{0,16},{2,18},{4,20},{6,22},{8,24},{10,26},{12,28},{14,30},{16,0},... | collective-permute-start | bytes 98312 | tf_op jit(solution)/shard_map/ppermute | solution.py:661
  341.2 4.1 collective-permute-start.22
  345.2 14.5 %collective-permute-start.7 = (bf16[1,1,1,1,16,512]{5,4,3,2,1,0:T(8,128)(2,1)S(1)}, bf16[1,1,1,1,16,512]{5,4,3,2,1,0:T(8,128)(2,1)S(1)}, u32[]{:S(2)}, u32[]{:S(2)}) collective-permute-start(bf16[1,1,1,1,16,512]{5,4,3,2,1,0:T(8,128)(2,1)S(1)} %constant_dynamic-slice_fusion.36), channel_id=1, source_target_pairs={{0,1},{1,0},{2,3},{3,2},{4,5},{5,4},{6,7},{7,6},{8,9},{9,8},{10,11... | collective-permute-start | bytes 49160 | tf_op jit(solution)/shard_map/ppermute | solution.py:638
  348.3 5.2 %collective-permute-start.10 = (bf16[2,1,1,1,16,2304]{5,4,3,2,1,0:T(8,128)(2,1)S(1)}, bf16[2,1,1,1,16,2304]{5,4,3,2,1,0:T(8,128)(2,1)S(1)}, u32[]{:S(2)}, u32[]{:S(2)}) collective-permute-start(bf16[2,1,1,1,16,2304]{5,4,3,2,1,0:T(8,128)(2,1)S(1)} %constant_dynamic-slice_fusion.33), channel_id=1, source_target_pairs={{0,8},{2,10},{4,12},{6,14},{8,0},{10,2},{12,4},{14,6},{16,24},{18,... | collective-permute-start | bytes 442376 | tf_op jit(solution)/shard_map/ppermute | solution.py:661
  353.6 5.9 %collective-permute-start.11 = (bf16[1,1,1,1,16,2304]{5,4,3,2,1,0:T(8,128)(2,1)S(1)}, bf16[1,1,1,1,16,2304]{5,4,3,2,1,0:T(8,128)(2,1)S(1)}, u32[]{:S(2)}, u32[]{:S(2)}) collective-permute-start(bf16[1,1,1,1,16,2304]{5,4,3,2,1,0:T(8,128)(2,1)S(1)} %constant_dynamic-slice_fusion.32), channel_id=1, source_target_pairs={{0,16},{2,18},{4,20},{6,22},{8,24},{10,26},{12,28},{14,30},{16,0},... | collective-permute-start | bytes 221192 | tf_op jit(solution)/shard_map/ppermute | solution.py:661
  355.8 15.0 %collective-permute-start.24 = (bf16[2,2,1,1,144,768]{5,4,3,2,1,0:T(8,128)(2,1)}, bf16[2,2,1,1,144,768]{5,4,3,2,1,0:T(8,128)(2,1)S(1)}, u32[]{:S(2)}, u32[]{:S(2)}) collective-permute-start(bf16[2,2,1,1,144,768]{5,4,3,2,1,0:T(8,128)(2,1)} %constant_dynamic-slice_fusion.18), channel_id=1, source_target_pairs={{0,4},{2,6},{4,0},{6,2},{8,12},{10,14},{12,8},{14,10},{16,20},{18,... | collective-permute-start | bytes 2654216 | tf_op jit(solution)/shard_map/ppermute | solution.py:661
  359.5 4.0 collective-permute-start.12
  371.0 10.6 %collective-permute-start.25 = (bf16[2,1,1,1,144,768]{5,4,3,2,1,0:T(8,128)(2,1)S(1)}, bf16[2,1,1,1,144,768]{5,4,3,2,1,0:T(8,128)(2,1)S(1)}, u32[]{:S(2)}, u32[]{:S(2)}) collective-permute-start(bf16[2,1,1,1,144,768]{5,4,3,2,1,0:T(8,128)(2,1)S(1)} %constant_dynamic-slice_fusion.17), channel_id=1, source_target_pairs={{0,8},{2,10},{4,12},{6,14},{8,0},{10,2},{12,4},{14,6},{16,24},{18,... | collective-permute-start | bytes 1327112 | tf_op jit(solution)/shard_map/ppermute | solution.py:661
  375.5 21.4 %collective-permute-start.39 = (bf16[2,2,2,1,48,1536]{5,4,3,2,1,0:T(8,128)(2,1)S(1)}, bf16[2,2,2,1,48,1536]{5,4,3,2,1,0:T(8,128)(2,1)S(1)}, u32[]{:S(2)}, u32[]{:S(2)}) collective-permute-start(bf16[2,2,2,1,48,1536]{5,4,3,2,1,0:T(8,128)(2,1)S(1)} %constant_dynamic-slice_fusion.3), channel_id=1, source_target_pairs={{0,1},{1,0},{2,3},{3,2},{4,5},{5,4},{6,7},{7,6},{8,9},{9,8},{10,11... | collective-permute-start | bytes 3538952 | tf_op jit(solution)/shard_map/ppermute | solution.py:638
  381.7 8.6 %collective-permute-start.26 = (bf16[1,1,1,1,144,768]{5,4,3,2,1,0:T(8,128)(2,1)S(1)}, bf16[1,1,1,1,144,768]{5,4,3,2,1,0:T(8,128)(2,1)S(1)}, u32[]{:S(2)}, u32[]{:S(2)}) collective-permute-start(bf16[1,1,1,1,144,768]{5,4,3,2,1,0:T(8,128)(2,1)S(1)} %constant_dynamic-slice_fusion.16), channel_id=1, source_target_pairs={{0,16},{2,18},{4,20},{6,22},{8,24},{10,26},{12,28},{14,30},{16,0},... | collective-permute-start | bytes 663560 | tf_op jit(solution)/shard_map/ppermute | solution.py:661
  385.0 16.9 %collective-permute-start.34 = (bf16[2,2,1,1,192,768]{5,4,3,2,1,0:T(8,128)(2,1)S(1)}, bf16[2,2,1,1,192,768]{5,4,3,2,1,0:T(8,128)(2,1)S(1)}, u32[]{:S(2)}, u32[]{:S(2)}) collective-permute-start(bf16[2,2,1,1,192,768]{5,4,3,2,1,0:T(8,128)(2,1)S(1)} %constant_dynamic-slice_fusion.8), channel_id=1, source_target_pairs={{0,4},{2,6},{4,0},{6,2},{8,12},{10,14},{12,8},{14,10},{16,20},{18,... | collective-permute-start | bytes 3538952 | tf_op jit(solution)/shard_map/ppermute | solution.py:661
  390.4 8.0 %collective-permute-start.27 = (bf16[1,1,1,1,144,384]{5,4,3,2,1,0:T(8,128)(2,1)S(1)}, bf16[1,1,1,1,144,384]{5,4,3,2,1,0:T(8,128)(2,1)S(1)}, u32[]{:S(2)}, u32[]{:S(2)}) collective-permute-start(bf16[1,1,1,1,144,384]{5,4,3,2,1,0:T(8,128)(2,1)S(1)} %constant_dynamic-slice_fusion.15), channel_id=1, source_target_pairs={{0,1},{1,0},{2,3},{3,2},{4,5},{5,4},{6,7},{7,6},{8,9},{9,8},{10,11... | collective-permute-start | bytes 331784 | tf_op jit(solution)/shard_map/ppermute | solution.py:638
  397.3 16.2 %collective-permute-start.40 = (bf16[2,1,2,1,48,1536]{5,4,3,2,1,0:T(8,128)(2,1)S(1)}, bf16[2,1,2,1,48,1536]{5,4,3,2,1,0:T(8,128)(2,1)S(1)}, u32[]{:S(2)}, u32[]{:S(2)}) collective-permute-start(bf16[2,1,2,1,48,1536]{5,4,3,2,1,0:T(8,128)(2,1)S(1)} %constant_dynamic-slice_fusion.2), channel_id=1, source_target_pairs={{0,8},{2,10},{4,12},{6,14},{8,0},{10,2},{12,4},{14,6},{16,24},{18,... | collective-permute-start | bytes 1769480 | tf_op jit(solution)/shard_map/ppermute | solution.py:661
  402.0 22.9 %collective-permute-start.35 = (bf16[2,1,1,1,192,768]{5,4,3,2,1,0:T(8,128)(2,1)S(1)}, bf16[2,1,1,1,192,768]{5,4,3,2,1,0:T(8,128)(2,1)S(1)}, u32[]{:S(2)}, u32[]{:S(2)}) collective-permute-start(bf16[2,1,1,1,192,768]{5,4,3,2,1,0:T(8,128)(2,1)S(1)} %constant_dynamic-slice_fusion.7), channel_id=1, source_target_pairs={{0,8},{2,10},{4,12},{6,14},{8,0},{10,2},{12,4},{14,6},{16,24},{18,... | collective-permute-start | bytes 1769480 | tf_op jit(solution)/shard_map/ppermute | solution.py:661
  413.6 11.9 %collective-permute-start.41 = (bf16[1,1,2,1,48,1536]{5,4,3,2,1,0:T(8,128)(2,1)S(1)}, bf16[1,1,2,1,48,1536]{5,4,3,2,1,0:T(8,128)(2,1)S(1)}, u32[]{:S(2)}, u32[]{:S(2)}) collective-permute-start(bf16[1,1,2,1,48,1536]{5,4,3,2,1,0:T(8,128)(2,1)S(1)} %constant_dynamic-slice_fusion.1), channel_id=1, source_target_pairs={{0,16},{2,18},{4,20},{6,22},{8,24},{10,26},{12,28},{14,30},{16,0},... | collective-permute-start | bytes 884744 | tf_op jit(solution)/shard_map/ppermute | solution.py:661
  425.1 10.3 %collective-permute-start.36 = (bf16[1,1,1,1,192,768]{5,4,3,2,1,0:T(8,128)(2,1)S(1)}, bf16[1,1,1,1,192,768]{5,4,3,2,1,0:T(8,128)(2,1)S(1)}, u32[]{:S(2)}, u32[]{:S(2)}) collective-permute-start(bf16[1,1,1,1,192,768]{5,4,3,2,1,0:T(8,128)(2,1)S(1)} %constant_dynamic-slice_fusion.6), channel_id=1, source_target_pairs={{0,16},{2,18},{4,20},{6,22},{8,24},{10,26},{12,28},{14,30},{16,0},... | collective-permute-start | bytes 884744 | tf_op jit(solution)/shard_map/ppermute | solution.py:661
  425.6 11.3 %collective-permute-start.42 = (bf16[1,1,1,1,48,1536]{5,4,3,2,1,0:T(8,128)(2,1)S(1)}, bf16[1,1,1,1,48,1536]{5,4,3,2,1,0:T(8,128)(2,1)S(1)}, u32[]{:S(2)}, u32[]{:S(2)}) collective-permute-start(bf16[1,1,1,1,48,1536]{5,4,3,2,1,0:T(8,128)(2,1)S(1)} %constant_dynamic-slice_fusion), channel_id=1, source_target_pairs={{0,4},{2,6},{4,0},{6,2},{8,12},{10,14},{12,8},{14,10},{16,20},{18,... | collective-permute-start | bytes 442376 | tf_op jit(solution)/shard_map/ppermute | solution.py:661
  435.4 5.2 %collective-permute-start.37 = (bf16[1,1,1,1,192,384]{5,4,3,2,1,0:T(8,128)(2,1)S(1)}, bf16[1,1,1,1,192,384]{5,4,3,2,1,0:T(8,128)(2,1)S(1)}, u32[]{:S(2)}, u32[]{:S(2)}) collective-permute-start(bf16[1,1,1,1,192,384]{5,4,3,2,1,0:T(8,128)(2,1)S(1)} %constant_dynamic-slice_fusion.5), channel_id=1, source_target_pairs={{0,1},{1,0},{2,3},{3,2},{4,5},{5,4},{6,7},{7,6},{8,9},{9,8},{10,11... | collective-permute-start | bytes 442376 | tf_op jit(solution)/shard_map/ppermute | solution.py:638
  (61 other events, 425.7 us)

commit v3 on v2

v3 whole, which is shorter than its diff:
```python
import functools
import jax
import jax.numpy as jnp
from jax import lax
from jax.experimental import pallas as pl
from jax.experimental.pallas import tpu as pltpu
from jax.sharding import Mesh, PartitionSpec as P

HD = 64
F32 = jnp.float32
BF16 = jnp.bfloat16
eps_batch = 1e-05
eps_layer = 1e-06
masked_value = -1e30
GELU_C = 0.7978845608028654
GELU_A = 0.044715


def nn(a, b):
    return lax.dot_general(a, b, (((1,), (0,)), ((), ())), preferred_element_type=F32)


def nt(a, b):
    return lax.dot_general(a, b, (((1,), (1,)), ((), ())), preferred_element_type=F32)


def tn(a, b):
    return lax.dot_general(a, b, (((0,), (0,)), ((), ())), preferred_element_type=F32)


def gelu_of(x):
    t = jnp.tanh(GELU_C * (x + GELU_A * x * x * x))
    return 0.5 * x * (1.0 + t)


def gelu_and_slope(x):
    x2 = x * x
    t = jnp.tanh(x * (GELU_C + (GELU_C * GELU_A) * x2))
    half = 0.5 + 0.5 * t
    slope = half + (0.5 * x) * (1.0 - t * t) * (GELU_C + (3.0 * GELU_C * GELU_A) * x2)
    return x * half, slope


def ln_parts(x):
    mean = jnp.mean(x, axis=-1, keepdims=True)
    c = x - mean
    var = jnp.mean(c * c, axis=-1, keepdims=True)
    r = lax.rsqrt(var + eps_layer)
    return c * r, r


def ln_back(dz, nrm, r, gain):
    u = dz * gain
    return r * (u - jnp.mean(u, axis=-1, keepdims=True) - nrm * jnp.mean(u * nrm, axis=-1, keepdims=True))


def whole(shape):
    return pl.BlockSpec(shape, lambda *_: (0,) * len(shape), pipeline_mode=pl.Buffered(1))


SMEM = pl.BlockSpec(memory_space=pltpu.SMEM)
VMEM = pl.BlockSpec(memory_space=pltpu.VMEM)


def row_of(ref):
    return ref[...].reshape(1, -1)


def put_rows(ref, at, vector):
    for r in range(vector.shape[1] // 128):
        ref[at + r : at + r + 1, :] = vector[:, r * 128 : (r + 1) * 128]


def take_rows(ref, at, size):
    return jnp.concatenate([ref[at + r : at + r + 1, :] for r in range(size // 128)], axis=1)


def part_shape(cols, rows, dp):
    return (2, dp // 2, cols // dp * (rows // 2) // 128, 128)


def part_it(natural, keep_ref, send_ref, core, at=0, lead=None):
    rows, cols = natural.shape[-2:]
    _, hi = keep_ref.shape[:2]
    r, blocks = rows // (2 * hi), cols // 256
    for h in range(hi):
        mine = pl.ds(pl.multiple_of((2 * h + core) * r, 16), r)
        other = pl.ds(pl.multiple_of((2 * h + 1 - core) * r, 16), r)
        for s in range(2):
            for b in range(blocks):
                lanes = slice((s * blocks + b) * 128, (s * blocks + b + 1) * 128)
                keep_ref[s, h, at + b * r : at + (b + 1) * r, :] = natural[mine, lanes]
                send_ref[s, h, at + b * r : at + (b + 1) * r, :] = natural[other, lanes]


def mlp_kernel(ex, seq, pad, parted, place_ref, z2_ref, h1_ref, cot_ref, upw_ref, upb_ref, dnw_ref, dnb_ref, g_ref, *refs):
    if parted:
        out_ref, dk_ref, ds_ref, uk_ref, us_ref, g1_ref, vec_ref, g2_s, g2t_s, acc_o, acc_d, ub_s, bg_s = refs
    else:
        out_ref, dn_ref, up_ref, g1_ref, vec_ref, g2_s, g2t_s, acc_o, acc_d, ub_s, bg_s = refs
    i = pl.program_id(0)
    last = pl.num_programs(0) - 1
    tile = upw_ref.shape[1]

    @pl.when(i == 0)
    def _():
        g2_s[...] = jnp.zeros_like(g2_s)
        for e in range(ex):
            g2_s[e * pad : e * pad + seq, :] = cot_ref[e]
        g2t_s[...] = g2_s[...].T
        acc_o[...] = jnp.zeros_like(acc_o)
        acc_d[...] = jnp.zeros_like(acc_d)
        ub = row_of(upb_ref)
        for j in range(ub_s.shape[0]):
            ub_s[j] = ub[:, j * tile : (j + 1) * tile]

    z2 = z2_ref[...]
    g2 = g2_s[...]
    pre = nn(z2, upw_ref[...]) + ub_s[i]
    act, slope = gelu_and_slope(pre)
    low = act.astype(BF16)
    dg = (nt(g2, dnw_ref[...]) * slope).astype(BF16)
    acc_o[...] += nn(low, dnw_ref[...])
    acc_d[...] += nt(dg, upw_ref[...])
    dn = nn(g2t_s[...], low).astype(BF16)
    up = tn(dg, z2).astype(BF16)
    bg_s[i] = jnp.sum(dg.astype(F32), axis=0, keepdims=True)
    if parted:
        core = place_ref[1]
        even = core == 0
        hi = dk_ref.shape[1]
        r = dn.shape[0] // (2 * hi)
        for j in range(tile // 128):
            d4 = dn[:, j * 128 : (j + 1) * 128].reshape(hi, 2, r, 128)
            dk_ref[0, :, j * r : (j + 1) * r, :] = jnp.where(even, d4[:, 0], d4[:, 1])
            ds_ref[0, :, j * r : (j + 1) * r, :] = jnp.where(even, d4[:, 1], d4[:, 0])
        r, blocks = up.shape[0] // 2, up.shape[1] // 256
        for s in range(2):
            for j in range(blocks):
                lanes = slice((s * blocks + j) * 128, (s * blocks + j + 1) * 128)
                first, second = up[0:r, lanes], up[r : 2 * r, lanes]
                uk_ref[s, 0, j * r : (j + 1) * r, :] = jnp.where(even, first, second)
                us_ref[s, 0, j * r : (j + 1) * r, :] = jnp.where(even, second, first)
    else:
        dn_ref[...] = dn
        up_ref[...] = up

    @pl.when(i == last)
    def _():
        h1 = h1_ref[...]
        out = (h1 + acc_o[...] + row_of(dnb_ref)).astype(BF16)
        for e in range(ex):
            out_ref[e] = out[e * pad : e * pad + seq, :]
        nrm, r = ln_parts(h1)
        dz = acc_d[...]
        gf = g2_s[...].astype(F32)
        g1 = gf + ln_back(dz, nrm, r, row_of(g_ref))
        g1_ref[...] = g1
        n = g1.shape[1] // 128
        for j, v in enumerate((col_sum(gf), col_sum(dz * nrm), col_sum(dz), col_sum(g1))):
            put_rows(vec_ref, j * n, v)
        for j in range(bg_s.shape[0]):
            put_rows(vec_ref, 4 * n + j * (tile // 128), bg_s[j])


def mlp(place, z2, h1, cot, up_w, up_b, down_w, down_b, gain, pad, dp, parted):
    ex, seq, width = cot.shape
    rows = z2.shape[0]
    ff = up_w.shape[1]
    tile = 2 * ff // dp if parted else 384
    steps = ff // tile
    vec_rows = 4 * width // 128 + ff // 128
    if parted:
        dn, up = part_shape(width, ff, dp), part_shape(ff, width, dp)
        per_half = steps // 2
        dn_spec = pl.BlockSpec((1, dn[1], dn[2] // per_half, 128), lambda i: (i // per_half, 0, i % per_half, 0))
        up_spec = pl.BlockSpec((2, 1, up[2], 128), lambda i: (0, i, 0, 0))
        grads = [(dn, dn_spec), (dn, dn_spec), (up, up_spec), (up, up_spec)]
    else:
        grads = [((width, ff), pl.BlockSpec((width, tile), lambda i: (0, i))),
                 ((ff, width), pl.BlockSpec((tile, width), lambda i: (i, 0)))]
    outs = [((ex, seq, width), whole((ex, seq, width)), BF16)] + [(s, b, BF16) for s, b in grads]
    outs += [((rows, width), whole((rows, width)), F32), ((vec_rows, 128), whole((vec_rows, 128)), F32)]
    return pl.pallas_call(
        functools.partial(mlp_kernel, ex, seq, pad, parted),
        grid=(steps,),
        in_specs=[
            SMEM, whole((rows, width)), whole((rows, width)), whole((ex, seq, width)),
            pl.BlockSpec((width, tile), lambda i: (0, i)), whole((ff,)),
            pl.BlockSpec((tile, width), lambda i: (i, 0)),
            whole((width,)), whole((width,)),
        ],
        out_specs=[b for _, b, _ in outs],
        out_shape=[jax.ShapeDtypeStruct(s, d) for s, _, d in outs],
        scratch_shapes=[
            pltpu.VMEM((rows, width), BF16), pltpu.VMEM((width, rows), BF16),
            pltpu.VMEM((rows, width), F32), pltpu.VMEM((rows, width), F32),
            pltpu.VMEM((steps, 1, tile), F32), pltpu.VMEM((steps, 1, tile), F32),
        ],
        compiler_params=pltpu.CompilerParams(dimension_semantics=("arbitrary",), vmem_limit_bytes=44 << 20),
        cost_estimate=pl.CostEstimate(flops=46 * 10**9, bytes_accessed=30 << 20, transcendentals=rows * ff),
        name="mlp_both_ways",
    )(place, z2, h1, cot, up_w, up_b, down_w, down_b, gain)


def stat_rows(channels):
    return max(8, 2 * channels // 128)


def put_stats(ref, first, second):
    lanes = jnp.concatenate([first, second], axis=1)
    n = ref.shape[0]
    for r in range(lanes.shape[1] // 128):
        ref[:, r, :] = jnp.broadcast_to(lanes[:, r * 128 : (r + 1) * 128], (n, 128))


def get_stats(ref, channels):
    total = jnp.sum(ref[...], axis=0)
    rows = 2 * channels // 128
    half = rows // 2
    first = jnp.concatenate([total[r : r + 1, :] for r in range(half)], axis=1)
    second = jnp.concatenate([total[r : r + 1, :] for r in range(half, rows)], axis=1)
    return first, second


def mean_rstd(ref, channels, count):
    s1, s2 = get_stats(ref, channels)
    mean = s1 * (1.0 / count)
    return mean, lax.rsqrt(s2 * (1.0 / count) - mean * mean + eps_batch)


def real_columns(rows, cols):
    return (lax.broadcasted_iota(jnp.int32, (rows, 1), 0) & 15) < cols


def col_sum(x):
    return jnp.sum(x, axis=0, keepdims=True)


def head_mask(rows, second):
    lane = lax.broadcasted_iota(jnp.int32, (rows, 2 * HD), 1)
    return (lane >= HD) if second else (lane < HD)


def attn_fwd_kernel(ex, n_image, pad, pre_ref, len_ref, h0_ref, g_ref, s_ref, wq_ref, wk_ref, wv_ref, qb_ref, vb_ref,
                    ow_ref, ob_ref, g2_ref, s2_ref,
                    z1_ref, q_ref, k_ref, v_ref, p_ref, attn_ref, h1_ref, z2_ref, acc, qb_s, vb_s):
    i = pl.program_id(0)
    last = pl.num_programs(0) - 1
    wide = wq_ref.shape[1]

    @pl.when(i == 0)
    def _():
        nrm, _r = ln_parts(h0_ref[...].astype(F32))
        z1_ref[...] = (nrm * row_of(g_ref) + row_of(s_ref)).astype(BF16)
        acc[...] = jnp.zeros_like(acc)
        qb, vb = row_of(qb_ref), row_of(vb_ref)
        for j in range(qb_s.shape[0]):
            qb_s[j] = qb[:, j * wide : (j + 1) * wide]
            vb_s[j] = vb[:, j * wide : (j + 1) * wide]

    z1 = z1_ref[...]
    q_ref[...] = (nn(z1, wq_ref[...]) + qb_s[i]).astype(BF16)
    k_ref[...] = nn(z1, wk_ref[...]).astype(BF16)
    v_ref[...] = (nn(z1, wv_ref[...]) + vb_s[i]).astype(BF16)
    zero = jnp.zeros((pad, 2 * HD), BF16)
    first = head_mask(pad, False)

    def example(e, carry):
        row0 = pl.multiple_of(e * pad, 16)
        key = lax.broadcasted_iota(jnp.int32, (pad, pad), 1)
        qry = lax.broadcasted_iota(jnp.int32, (pad, pad), 0)
        limit = jnp.maximum(qry + 1, n_image + pre_ref[e])
        limit = jnp.minimum(limit, n_image + len_ref[e])
        vis = key < limit
        for pair in range(wide // (2 * HD)):
            cols = slice(pair * 2 * HD, (pair + 1) * 2 * HD)
            q2 = q_ref[pl.ds(row0, pad), cols] * jnp.asarray(0.125, BF16)
            k2 = k_ref[pl.ds(row0, pad), cols]
            v2 = v_ref[pl.ds(row0, pad), cols]
            out = None
            for h in range(2):
                sel = first if h == 0 else jnp.logical_not(first)
                sc = nt(jnp.where(sel, q2, zero), k2)
                sc = jnp.where(vis, sc, masked_value)
                top = jnp.max(sc, axis=-1, keepdims=True)
                ex_ = jnp.exp(sc - top)
                tot = jnp.sum(ex_, axis=-1, keepdims=True)
                p = (ex_ * (1.0 / tot)).astype(BF16)
                p_ref[e, pair * 2 + h] = p
                o = nn(p, jnp.where(sel, v2, zero))
                out = o if out is None else out + o
            attn_ref[pl.ds(row0, pad), cols] = out.astype(BF16)
        return carry

    lax.fori_loop(0, ex, example, 0)
    acc[...] += nn(attn_ref[...], ow_ref[...])

    @pl.when(i == last)
    def _():
        h1 = h0_ref[...].astype(F32) + acc[...] + row_of(ob_ref)
        h1_ref[...] = h1
        nrm, _r = ln_parts(h1)
        z2_ref[...] = (nrm * row_of(g2_ref) + row_of(s2_ref)).astype(BF16)


def attn_fwd(h0, prefix, text_len, ln1_gain, ln1_shift, qkv_w, qb, vb, out_w, out_b, ln2_gain, ln2_shift, ex, n_image, pad, wide=256):
    rows, width = h0.shape
    groups = width // wide
    heads = width // HD
    hg = wide // HD
    cols = lambda off: pl.BlockSpec((width, wide), lambda i, *_: (0, i + off * groups))
    vec = whole((width,))
    part = pl.BlockSpec((rows, wide), lambda i, *_: (0, i))
    return pl.pallas_call(
        functools.partial(attn_fwd_kernel, ex, n_image, pad),
        grid_spec=pltpu.PrefetchScalarGridSpec(
            num_scalar_prefetch=2,
            grid=(groups,),
            in_specs=[whole((rows, width)), vec, vec, cols(0), cols(1), cols(2), vec, vec,
                      pl.BlockSpec((wide, width), lambda i, *_: (i, 0)), vec, vec, vec],
            out_specs=[whole((rows, width)), part, part, part,
                       pl.BlockSpec((ex, hg, pad, pad), lambda i, *_: (0, i, 0, 0)),
                       part, whole((rows, width)), whole((rows, width))],
            scratch_shapes=[pltpu.VMEM((rows, width), F32)] + [pltpu.VMEM((groups, 1, wide), F32)] * 2,
        ),
        out_shape=[jax.ShapeDtypeStruct((rows, width), BF16)] * 4 + [
            jax.ShapeDtypeStruct((ex, heads, pad, pad), BF16),
            jax.ShapeDtypeStruct((rows, width), BF16),
            jax.ShapeDtypeStruct((rows, width), F32),
            jax.ShapeDtypeStruct((rows, width), BF16)],
        compiler_params=pltpu.CompilerParams(dimension_semantics=("arbitrary",), vmem_limit_bytes=40 << 20),
        cost_estimate=pl.CostEstimate(flops=32 * 10**9, bytes_accessed=30 << 20, transcendentals=heads * rows * pad),
        name="attention_forward",
    )(prefix, text_len, h0, ln1_gain, ln1_shift, qkv_w, qkv_w, qkv_w, qb, vb, out_w, out_b, ln2_gain, ln2_shift)


def attn_bwd_kernel(ex, n_image, txt, cols_real, pad, parted, place_ref, g1_ref, ow_ref, attn_ref, q_ref, k_ref, v_ref, p_ref, z1_ref, h0_ref, wq_ref, wk_ref, wv_ref, g_ref, *refs):
    if parted:
        ak_ref, as_ref, text_ref, dtok_ref, vec_ref, ow_s, qkv_s = refs[:7]
    else:
        ow_s, qkv_s, text_ref, dtok_ref, vec_ref = refs[:5]
    g1b_s, g1t_s, dat_s, dq_s, dk_s, dv_s, acc, bias_s = refs[-8:]
    i = pl.program_id(0)
    last = pl.num_programs(0) - 1
    wide = wq_ref.shape[1]

    @pl.when(i == 0)
    def _():
        g1b_s[...] = g1_ref[...].astype(BF16)
        g1t_s[...] = g1b_s[...].T
        acc[...] = jnp.zeros_like(acc)

    ow_s[i] = nn(g1t_s[...], attn_ref[...]).astype(BF16)
    dat_s[...] = nt(g1b_s[...], ow_ref[...]).astype(BF16)
    zero = jnp.zeros((pad, 2 * HD), BF16)
    first = head_mask(pad, False)

    def example(e, carry):
        row0 = pl.multiple_of(e * pad, 16)
        for pair in range(wide // (2 * HD)):
            cols = slice(pair * 2 * HD, (pair + 1) * 2 * HD)
            q2 = q_ref[pl.ds(row0, pad), cols]
            k2 = k_ref[pl.ds(row0, pad), cols]
            v2 = v_ref[pl.ds(row0, pad), cols]
            da2 = dat_s[pl.ds(row0, pad), cols]
            dq = dk = dv = None
            for h in range(2):
                sel = first if h == 0 else jnp.logical_not(first)
                pb = p_ref[e, pair * 2 + h]
                p = pb.astype(F32)
                dah = jnp.where(sel, da2, zero)
                dp = nt(dah, v2)
                inner = jnp.sum(p * dp, axis=-1, keepdims=True)
                ds = (p * (dp - inner)).astype(BF16)
                dvh = tn(pb, dah)
                dqh = nn(ds, jnp.where(sel, k2, zero))
                dkh = tn(ds, jnp.where(sel, q2, zero))
                dq = dqh if dq is None else dq + dqh
                dk = dkh if dk is None else dk + dkh
                dv = dvh if dv is None else dv + dvh
            dq_s[pl.ds(row0, pad), cols] = (dq * 0.125).astype(BF16)
            dk_s[pl.ds(row0, pad), cols] = (dk * 0.125).astype(BF16)
            dv_s[pl.ds(row0, pad), cols] = dv.astype(BF16)
        return carry

    lax.fori_loop(0, ex, example, 0)
    z1 = z1_ref[...]
    dq, dk, dv = dq_s[...], dk_s[...], dv_s[...]
    width = z1.shape[1]
    for j, d in enumerate((dq, dk, dv)):
        qkv_s[pl.ds(pl.multiple_of(j * width + i * wide, wide), wide), :] = tn(d, z1).astype(BF16)
    acc[...] += nt(dq, wq_ref[...]) + nt(dk, wk_ref[...]) + nt(dv, wv_ref[...])
    bias_s[0, i] = col_sum(dq.astype(F32))
    bias_s[1, i] = col_sum(dv.astype(F32))

    @pl.when(i == last)
    def _():
        nrm, r = ln_parts(h0_ref[...].astype(F32))
        dz = acc[...]
        g0 = g1_ref[...] + ln_back(dz, nrm, r, row_of(g_ref))
        n = width // 128
        vec_ref[5 * n :, :] = jnp.zeros_like(vec_ref[5 * n :, :])
        put_rows(vec_ref, n, col_sum(dz * nrm))
        put_rows(vec_ref, 2 * n, col_sum(dz))
        for j in range(2):
            for t in range(bias_s.shape[1]):
                put_rows(vec_ref, (3 + j) * n + t * (wide // 128), bias_s[j, t])
        gb = g0.astype(BF16)
        px = dtok_ref.shape[0] // ex
        pick_image = image_pick(px, pad, n_image, cols_real)
        tr = lax.broadcasted_iota(jnp.int32, (txt, pad), 0)
        tc = lax.broadcasted_iota(jnp.int32, (txt, pad), 1)
        pick_text = jnp.where(tc == tr + n_image, 1.0, 0.0).astype(BF16)
        tot = jnp.zeros((1, gb.shape[1]), F32)
        for e in range(ex):
            ge = gb[e * pad : (e + 1) * pad, :]
            text_ref[e] = nn(pick_text, ge).astype(BF16)
            dt = nn(pick_image, ge)
            dtok_ref[e * px : (e + 1) * px, :] = dt.astype(BF16)
            tot = tot + jnp.sum(dt, axis=0, keepdims=True)
        put_rows(vec_ref, 0, tot)
        if parted:
            core = place_ref[1]
            part_it(qkv_s, ak_ref, as_ref, core)
            hi = ak_ref.shape[1]
            r = width // (2 * hi)
            at = qkv_s.shape[0] // (2 * hi) * (width // 256)
            for h in range(hi):
                mine = pl.ds(pl.multiple_of((2 * h + core) * r, 16), r)
                other = pl.ds(pl.multiple_of((2 * h + 1 - core) * r, 16), r)
                for blk in range(width // 128):
                    s, j = divmod(blk, width // 256)
                    t, lane = divmod(blk * 128, wide)
                    dst = slice(at + j * r, at + (j + 1) * r)
                    ak_ref[s, h, dst, :] = ow_s[t, mine, lane : lane + 128]
                    as_ref[s, h, dst, :] = ow_s[t, other, lane : lane + 128]


def image_pick(px, pad, n_image, cols_real):
    p = lax.broadcasted_iota(jnp.int32, (px, pad), 0)
    t = lax.broadcasted_iota(jnp.int32, (px, pad), 1)
    col = p & 15
    tok = (p >> 4) * cols_real + col
    return jnp.where((col < cols_real) & (tok == t) & (t < n_image), 1.0, 0.0).astype(BF16)


def attn_bwd(place, g1, out_w, attn, q, k, v, p, z1, h0, qkv_w, ln1_gain, ex, n_image, txt, img_rows, img_cols, pad, dp, parted, wide=256):
    rows, width = h0.shape
    groups = width // wide
    heads = width // HD
    hg = wide // HD
    px = img_rows * 16
    vec_rows = -(-5 * width // 128 // 8) * 8
    cols = lambda off: pl.BlockSpec((width, wide), lambda i: (0, i + off * groups))
    part = pl.BlockSpec((rows, wide), lambda i: (0, i))
    nat_o, nat_q = (groups, width, wide), (3 * width, width)
    sent = part_shape(4 * width, width, dp)
    outs = [(s, BF16) for s in ((sent, sent) if parted else (nat_o, nat_q))]
    outs += [((ex, txt, width), BF16), ((ex * px, width), BF16), ((vec_rows, 128), F32)]
    natural = [pltpu.VMEM(nat_o, BF16), pltpu.VMEM(nat_q, BF16)] if parted else []
    return pl.pallas_call(
        functools.partial(attn_bwd_kernel, ex, n_image, txt, img_cols, pad, parted),
        grid=(groups,),
        in_specs=[SMEM, whole((rows, width)), pl.BlockSpec((wide, width), lambda i: (i, 0)), part, part, part, part,
                  pl.BlockSpec((ex, hg, pad, pad), lambda i: (0, i, 0, 0)),
                  whole((rows, width)), whole((rows, width)), cols(0), cols(1), cols(2), whole((width,))],
        out_specs=[whole(s) for s, _ in outs],
        out_shape=[jax.ShapeDtypeStruct(s, d) for s, d in outs],
        scratch_shapes=natural + [pltpu.VMEM((rows, width), BF16), pltpu.VMEM((width, rows), BF16)]
        + [pltpu.VMEM((rows, wide), BF16)] * 4 + [pltpu.VMEM((rows, width), F32), pltpu.VMEM((2, groups, 1, wide), F32)],
        compiler_params=pltpu.CompilerParams(dimension_semantics=("arbitrary",), vmem_limit_bytes=48 << 20),
        cost_estimate=pl.CostEstimate(flops=42 * 10**9, bytes_accessed=40 << 20, transcendentals=0),
        name="attention_backward",
    )(place, g1, out_w, attn, q, k, v, p, z1, h0, qkv_w, qkv_w, qkv_w, ln1_gain)

def stats_kernel(cols, x_ref, w_ref, parts_ref, xp):
    xp[...] = jnp.zeros_like(xp)
    shape = x_ref.shape
    xp[:, 0:cols, :] = x_ref[...].reshape(shape[0] * shape[1], cols, shape[3])
    a = nn(xp[...].reshape(shape[0] * shape[1] * 16, shape[3]), w_ref[...])
    put_stats(parts_ref, col_sum(a), col_sum(a * a))


def conv_fwd_kernel(count, ex, rows, cols, place_ref, parts_ref, own_ref, got_ref, win_ref, g_ref, s_ref, wmid_ref,
                    xs_ref, act1_ref, wide_ref, act2_ref, parts2_ref):
    s = place_ref[0]
    half = rows // 2
    px = rows * 16
    chan = xs_ref.shape[-1]
    xs_ref[...] = jnp.zeros_like(xs_ref)
    for e in range(ex):
        xs_ref[e, pl.ds(s * half, half), 0:cols, :] = own_ref[s * ex + e]
        xs_ref[e, pl.ds((1 - s) * half, half), 0:cols, :] = got_ref[e]
    a1 = nn(xs_ref[...].reshape(ex * px, chan), win_ref[...])
    act1_ref[...] = a1
    mid = a1.shape[1]
    mean, rstd = mean_rstd(parts_ref, mid, count)
    real = real_columns(ex * px, cols)
    act = gelu_of((a1 - mean) * rstd * row_of(g_ref) + row_of(s_ref))
    act = jnp.where(real, act, 0.0)
    for e in range(ex):
        part = act[e * px : (e + 1) * px]
        wide_ref[e, 0:16, :] = jnp.zeros((16, 3 * mid), BF16)
        wide_ref[e, px + 16 : px + 32, :] = jnp.zeros((16, 3 * mid), BF16)
        wide_ref[e, 16 : px + 16, 0:mid] = pltpu.roll(part, 1, 0).astype(BF16)
        wide_ref[e, 16 : px + 16, mid : 2 * mid] = part.astype(BF16)
        wide_ref[e, 16 : px + 16, 2 * mid : 3 * mid] = pltpu.roll(part, px - 1, 0).astype(BF16)
    one = real_columns(px, cols)
    t1 = jnp.zeros((1, mid), F32)
    t2 = jnp.zeros((1, mid), F32)
    for e in range(ex):
        a2 = nn(wide_ref[e, 0:px, :], wmid_ref[0])
        a2 = a2 + nn(wide_ref[e, 16 : px + 16, :], wmid_ref[1])
        a2 = a2 + nn(wide_ref[e, 32 : px + 32, :], wmid_ref[2])
        a2 = jnp.where(one, a2, 0.0)
        act2_ref[e * px : (e + 1) * px, :] = a2
        t1 = t1 + col_sum(a2)
        t2 = t2 + col_sum(a2 * a2)
    put_stats(parts2_ref, t1, t2)


def expand_kernel(count, cols, parts_ref, act2_ref, g_ref, s_ref, w_ref, relu2_ref, act3_ref, parts3_ref):
    a2 = act2_ref[...]
    mean, rstd = mean_rstd(parts_ref, a2.shape[1], count)
    act = gelu_of((a2 - mean) * rstd * row_of(g_ref) + row_of(s_ref))
    low = jnp.where(real_columns(a2.shape[0], cols), act, 0.0).astype(BF16)
    relu2_ref[...] = low
    a3 = nn(low, w_ref[...])
    act3_ref[...] = a3
    put_stats(parts3_ref, col_sum(a3), col_sum(a3 * a3))


def tokens_kernel(count, ex, cols, n_image, pad, parts_ref, act3_ref, xs_ref, g_ref, s_ref, w_ref, b_ref, text_ref,
                  stem_ref, h0_ref):
    a3 = act3_ref[...]
    mean, rstd = mean_rstd(parts_ref, a3.shape[1], count)
    pre = (a3 - mean) * rstd * row_of(g_ref) + row_of(s_ref) + xs_ref[...].reshape(a3.shape).astype(F32)
    stem = gelu_of(pre).astype(BF16)
    stem_ref[...] = stem
    tok = (nn(stem, w_ref[...]) + row_of(b_ref)).astype(BF16)
    px = a3.shape[0] // ex
    txt = text_ref.shape[1]
    t = lax.broadcasted_iota(jnp.int32, (pad, px), 0)
    p = lax.broadcasted_iota(jnp.int32, (pad, px), 1)
    col = p & 15
    pick = jnp.where((col < cols) & ((p >> 4) * cols + col == t), 1.0, 0.0).astype(BF16)
    tr = lax.broadcasted_iota(jnp.int32, (pad, txt), 0)
    tc = lax.broadcasted_iota(jnp.int32, (pad, txt), 1)
    pick_text = jnp.where(tr == tc + n_image, 1.0, 0.0).astype(BF16)
    for e in range(ex):
        both = nn(pick, tok[e * px : (e + 1) * px, :]) + nn(pick_text, text_ref[e])
        h0_ref[e * pad : (e + 1) * pad, :] = both.astype(BF16)


def dpre_kernel(count, ex, rows, place_ref, parts_ref, act3_ref, xs_ref, g_ref, s_ref, dtok_ref, w_ref, dpre_ref, send_ref, parts4_ref):
    a3 = act3_ref[...]
    mean, rstd = mean_rstd(parts_ref, a3.shape[1], count)
    nrm = (a3 - mean) * rstd
    pre = nrm * row_of(g_ref) + row_of(s_ref) + xs_ref[...].reshape(a3.shape).astype(F32)
    _, slope = gelu_and_slope(pre)
    d = nt(dtok_ref[...], w_ref[...]) * slope
    dpre_ref[...] = d.reshape(dpre_ref.shape)
    put_stats(parts4_ref, col_sum(d), col_sum(d * nrm))
    half = rows // 2
    other = 1 - place_ref[0]
    for e in range(ex):
        send_ref[e] = dpre_ref[e, pl.ds(other * half, half)].astype(BF16)


def back3_kernel(count, cols, parts4_ref, parts3_ref, parts2_ref, act3_ref, dpre_ref, g3_ref, w_ref, act2_ref, g2_ref, s2_ref, veca_ref, vecb_ref,
                 low3_ref, t2_ref, parts5_ref, gain_ref, shift_ref, small_s):
    a3 = act3_ref[...]
    chan = a3.shape[1]
    mean, rstd = mean_rstd(parts3_ref, chan, count)
    s1, s2 = get_stats(parts4_ref, chan)
    gain_ref[...] = s2.reshape(-1)
    shift_ref[...] = s1.reshape(-1)
    nrm = (a3 - mean) * rstd
    d = (row_of(g3_ref) * rstd) * (dpre_ref[...].reshape(a3.shape) - s1 * (1.0 / count) - nrm * (s2 * (1.0 / count)))
    low = jnp.where(real_columns(a3.shape[0], cols), d, 0.0).astype(BF16)
    low3_ref[...] = low
    a2 = act2_ref[...]
    mean2, rstd2 = mean_rstd(parts2_ref, a2.shape[1], count)
    nrm2 = (a2 - mean2) * rstd2
    _, slope = gelu_and_slope(nrm2 * row_of(g2_ref) + row_of(s2_ref))
    t2 = nt(low, w_ref[...]) * slope
    t2_ref[...] = t2
    parts5_ref[...] = jnp.zeros_like(parts5_ref)
    put_stats(parts5_ref, col_sum(t2), col_sum(t2 * nrm2))
    used = veca_ref.shape[0] + vecb_ref.shape[0]
    n = parts5_ref.shape[0]
    each = -(-used // n)
    small_s[0 : veca_ref.shape[0], :] = veca_ref[...]
    small_s[veca_ref.shape[0] : used, :] = vecb_ref[...]
    if used < small_s.shape[0]:
        small_s[used:, :] = jnp.zeros_like(small_s[used:, :])
    for d in range(n):
        parts5_ref[d, 4 : 4 + each, :] = small_s[d * each : (d + 1) * each, :]


def back2_kernel(count, ex, rows, cols, place_ref, parts5_ref, parts2_ref, parts1_ref, act2_ref, t2_ref, g2_ref, wmid_ref, act1_ref, g1_ref, s1_ref,
                 low2_ref, t1_ref, send_ref, parts6_ref, gain_ref, shift_ref, wide):
    a2 = act2_ref[...]
    mid = a2.shape[1]
    px = rows * 16
    mean, rstd = mean_rstd(parts2_ref, mid, count)
    s1, s2 = get_stats(parts5_ref, mid)
    gain_ref[...] = s2.reshape(-1)
    shift_ref[...] = s1.reshape(-1)
    nrm = (a2 - mean) * rstd
    d = (row_of(g2_ref) * rstd) * (t2_ref[...] - s1 * (1.0 / count) - nrm * (s2 * (1.0 / count)))
    d = jnp.where(real_columns(ex * px, cols), d, 0.0)
    low2_ref[...] = d.astype(BF16)
    for e in range(ex):
        part = d[e * px : (e + 1) * px]
        wide[e, 0:16, :] = jnp.zeros((16, 3 * mid), BF16)
        wide[e, px + 16 : px + 32, :] = jnp.zeros((16, 3 * mid), BF16)
        wide[e, 16 : px + 16, 0:mid] = pltpu.roll(part, px - 1, 0).astype(BF16)
        wide[e, 16 : px + 16, mid : 2 * mid] = part.astype(BF16)
        wide[e, 16 : px + 16, 2 * mid : 3 * mid] = pltpu.roll(part, 1, 0).astype(BF16)
    mean1, rstd1 = mean_rstd(parts1_ref, mid, count)
    one = real_columns(px, cols)
    q1 = jnp.zeros((1, mid), F32)
    q2 = jnp.zeros((1, mid), F32)
    for e in range(ex):
        t = None
        for r in range(3):
            for c in range(3):
                term = nt(wide[e, (2 - r) * 16 : (2 - r) * 16 + px, c * mid : (c + 1) * mid], wmid_ref[r, c * mid : (c + 1) * mid, :])
                t = term if t is None else t + term
        nrm1 = (act1_ref[e * px : (e + 1) * px, :] - mean1) * rstd1
        _, slope = gelu_and_slope(nrm1 * row_of(g1_ref) + row_of(s1_ref))
        t = jnp.where(one, t * slope, 0.0)
        t1_ref[e] = t.reshape(rows, 16, mid)
        q1 = q1 + col_sum(t)
        q2 = q2 + col_sum(t * nrm1)
    put_stats(parts6_ref, q1, q2)
    chunk = jnp.sum(parts5_ref[:, 4:8, :], axis=0)
    parts6_ref[:, 4:8, :] = jnp.broadcast_to(chunk[None], (parts6_ref.shape[0], 4, 128))
    half = rows // 2
    other = 1 - place_ref[0]
    for e in range(ex):
        send_ref[e] = t1_ref[e, pl.ds(other * half, half)].astype(BF16)


def conv_grads_kernel(ex, px, parted, place_ref, low2_ref, wide_ref, low3_ref, relu2_ref, *refs):
    mid = low2_ref.shape[1]
    nat_m, nat_o = (refs[2], refs[3]) if parted else (refs[0], refs[1])
    nat_o[...] = tn(low3_ref[...], relu2_ref[...]).astype(BF16)
    for r in range(3):
        tot = None
        for e in range(ex):
            term = tn(low2_ref[e * px : (e + 1) * px, :], wide_ref[e, r * 16 : r * 16 + px, :])
            tot = term if tot is None else tot + term
        for c in range(3):
            for h in range(2):
                at = (h * 9 + r * 3 + c) * (mid // 2)
                src = c * mid + h * (mid // 2)
                nat_m[:, at : at + mid // 2] = tot[:, src : src + mid // 2].astype(BF16)
    if parted:
        part_it(nat_m, refs[0], refs[1], place_ref[1])
        part_it(nat_o, refs[0], refs[1], place_ref[1], at=nat_m.shape[0] // (2 * refs[0].shape[1]) * (nat_m.shape[1] // 256))


def tn_kernel(parted, place_ref, a_ref, b_ref, *refs):
    natural = refs[2] if parted else refs[0]
    natural[...] = tn(a_ref[...], b_ref[...]).astype(BF16)
    if parted:
        part_it(natural, refs[0], refs[1], place_ref[1])


def image_kernel(count, ex, rows, cols, parted, each, places, place_ref, parts6_ref, parts1_ref, x_ref, win_ref, g_ref, t1_ref, gott_ref, dpre_ref, gotd_ref,
                 grad_ref, *refs):
    if parted:
        keep_ref, send_ref, win_grad_ref = refs[0], refs[1], refs[-1]
        refs = refs[2:-1]
    else:
        win_grad_ref, refs = refs[0], refs[1:]
    gain_ref, shift_ref, vec_refs, xp, small_s = refs[0], refs[1], refs[2:-2], refs[-2], refs[-1]
    s = place_ref[0]
    half = rows // 2
    chan = x_ref.shape[-1]
    mid = win_ref.shape[1]
    mean, rstd = mean_rstd(parts1_ref, mid, count)
    s1, s2 = get_stats(parts6_ref, mid)
    gain_ref[...] = s2.reshape(-1)
    shift_ref[...] = s1.reshape(-1)
    real = real_columns(ex * half * 16, cols)
    size = ex * half * 16
    xp[...] = jnp.zeros_like(xp)
    wg = None
    for own in (True, False):
        at = (s if own else 1 - s) * ex
        xp[:, 0:cols, :] = x_ref[pl.ds(at, ex)].reshape(ex * half, cols, chan)
        x = xp[...].reshape(size, chan)
        nrm = (nn(x, win_ref[...]) - mean) * rstd
        if own:
            t = t1_ref[:, pl.ds(s * half, half)].reshape(size, mid)
            dp = dpre_ref[:, pl.ds(s * half, half)].reshape(size, chan)
        else:
            t = gott_ref[...].reshape(size, mid).astype(F32)
            dp = gotd_ref[...].reshape(size, chan).astype(F32)
        d = (row_of(g_ref) * rstd) * (t - s1 * (1.0 / count) - nrm * (s2 * (1.0 / count)))
        low = jnp.where(real, d, 0.0).astype(BF16)
        grad = (nt(low, win_ref[...]) + dp).astype(BF16).reshape(ex, half, 16, chan)
        grad_ref[pl.ds(at, ex)] = grad[:, :, 0:cols, :]
        term = tn(low, x)
        wg = term if wg is None else wg + term
    win_grad_ref[...] = wg.astype(BF16)
    if parted:
        part_it(win_grad_ref, keep_ref, send_ref, place_ref[1])
    for d in range(parts6_ref.shape[0]):
        small_s[d * each : (d + 1) * each, :] = parts6_ref[d, 4 : 4 + each, :]
    for ref, at in zip(vec_refs, places):
        ref[...] = take_rows(small_s, at, ref.shape[0]).reshape(-1)


def call(kernel, outs, *args, place=None, scratch=(), name=None, us=2, limit=24):
    nbytes = sum(a.size * a.dtype.itemsize for a in args)
    return pl.pallas_call(
        kernel,
        out_shape=[jax.ShapeDtypeStruct(s, d) for s, d in outs],
        in_specs=([SMEM] if place is not None else []) + [VMEM] * len(args),
        out_specs=[VMEM] * len(outs),
        scratch_shapes=list(scratch),
        compiler_params=pltpu.CompilerParams(vmem_limit_bytes=limit << 20),
        cost_estimate=pl.CostEstimate(flops=us * 10**9, bytes_accessed=nbytes, transcendentals=0),
        name=name,
    )(*([place] if place is not None else []), *args)


DP = ("far", "near", "core")
AXES = DP + ("space",)


def spread(parts):
    return lax.all_to_all(parts, AXES, split_axis=0, concat_axis=0, tiled=True)


def swap(x, axis="space"):
    return lax.ppermute(x, axis, [(0, 1), (1, 0)])


def tie(*values):
    return lax.optimization_barrier(values)


def combine_kernel(pairs, bits_ref, *refs):
    ins, outs = refs[: 4 * pairs], refs[4 * pairs :]
    for j in range(pairs):
        a, b, c, d = ins[4 * j : 4 * j + 4]
        outs[2 * j][...] = a[:, 0] + b[:, 0]
        outs[2 * j + 1][...] = c[:, 0] + d[:, 0]


def combine(items, tiles):
    bits = jnp.stack([bit for _, _, bit, _, _ in items]).astype(jnp.int32)
    args, in_specs, outs, out_specs = [], [], [], []
    for j, (keep, got, _, before, after) in enumerate(items):
        rows = keep.shape[-2]
        rt = rows // tiles
        view = (before, 2, after, rows, 128)
        block = (before, 1, after, rt, 128)
        mine = pl.BlockSpec(block, lambda t, bits_ref, j=j: (0, bits_ref[j], 0, t, 0))
        other = pl.BlockSpec(block, lambda t, bits_ref, j=j: (0, 1 - bits_ref[j], 0, t, 0))
        keep, got = keep.reshape(view), got.reshape(view)
        args += [keep, got, keep, got]
        in_specs += [mine, mine, other, other]
        outs += [jax.ShapeDtypeStruct((before, after, rows, 128), BF16)] * 2
        out_specs += [pl.BlockSpec((before, after, rt, 128), lambda t, bits_ref: (0, 0, t, 0))] * 2
    size = sum(a.size for a in args)
    res = pl.pallas_call(
        functools.partial(combine_kernel, len(items)),
        grid_spec=pltpu.PrefetchScalarGridSpec(num_scalar_prefetch=1, grid=(tiles,), in_specs=in_specs, out_specs=out_specs),
        out_shape=outs,
        compiler_params=pltpu.CompilerParams(dimension_semantics=("arbitrary",), vmem_limit_bytes=24 << 20),
        cost_estimate=pl.CostEstimate(flops=3 * 10**9, bytes_accessed=3 * size, transcendentals=0),
        name="combine",
    )(bits, *args)
    return [(res[2 * j], res[2 * j + 1]) for j in range(len(items))]


class Halving:
    def __init__(self, keep, send):
        self.left = ["space", "f1", "f0", "near"]
        self.keep, self.got = keep, self.exchange("core", send)

    def exchange(self, name, send):
        if name in ("f0", "f1"):
            flip = 1 if name == "f0" else 2
            return lax.ppermute(send, "far", [(j, j ^ flip) for j in range(4)])
        return lax.ppermute(send, name, [(0, 1), (1, 0)])

    def item(self, name):
        at = self.left.index(name)
        if name in ("f0", "f1"):
            bit = (lax.axis_index("far") // (1 if name == "f0" else 2)) % 2
        else:
            bit = lax.axis_index(name)
        return self.keep, self.got, bit, 2**at, 2 ** (len(self.left) - at - 1)

    def advance(self, name, keep, send):
        self.left.remove(name)
        self.keep, self.got = keep, self.exchange(name, send)

    def done(self):
        rows = self.keep.shape[-2]
        return self.keep.reshape(rows, 128).astype(F32) + self.got.reshape(rows, 128).astype(F32)


def step(moves, tiles, tied):
    res = combine([h.item(name) for h, name in moves], tiles)
    flat = tie(tied, *[x for pair in res for x in pair])
    for j, (h, name) in enumerate(moves):
        h.advance(name, flat[1 + 2 * j], flat[2 + 2 * j])
    return flat[0]


def final(x, r, at=0, blocks=None):
    blocks = x.shape[0] // r if blocks is None else blocks
    x = x[at : at + r * blocks].astype(F32).reshape(blocks, r, 128)
    return x.transpose(0, 2, 1).reshape(blocks * 128, r)


def halve_dp(x, axis, bit):
    size = lax.axis_size(DP)
    mine = (lax.axis_index(DP) // bit) % 2
    keep = lax.dynamic_index_in_dim(x, mine, axis, keepdims=True)
    send = lax.dynamic_index_in_dim(x, 1 - mine, axis, keepdims=True)
    return keep + lax.ppermute(send, DP, [(j, j ^ bit) for j in range(size)])


def scattered(grad_t):
    size = lax.axis_size(DP)
    bits = size.bit_length() - 1
    cols, rows = grad_t.shape
    x = grad_t.reshape((2,) * bits + (cols // size, rows))
    for b in range(bits):
        x = halve_dp(x, bits - 1 - b, 1 << b)
    half = rows // 2
    mine = lax.axis_index("space")
    keep = lax.dynamic_slice_in_dim(x, mine * half, half, axis=x.ndim - 1)
    send = lax.dynamic_slice_in_dim(x, (1 - mine) * half, half, axis=x.ndim - 1)
    return (keep + swap(send)).reshape(cols // size, half).astype(F32).T


def shards(
    image_in, text_in, prefix, text_len, cotangent,
    conv_in_w, bn1_gain, bn1_shift, conv_mid_w, bn2_gain, bn2_shift, conv_out_w, bn3_gain, bn3_shift,
    proj_w, proj_b, ln1_gain, ln1_shift, qkv_w, query_bias, value_bias, out_w, out_b,
    ln2_gain, ln2_shift, up_w, up_b, down_w, down_b,
):
    n_dev, dp = lax.axis_size(AXES), lax.axis_size(DP)
    band_ex, band_rows, cols, chan = image_in.shape
    mid = conv_in_w.shape[1]
    width = proj_w.shape[1]
    ff = up_w.shape[1]
    ex, txt, _ = text_in.shape
    rows = band_rows * lax.axis_size("space")
    n_image = rows * cols
    seq = n_image + txt
    pad = -(-seq // 16) * 16
    px = rows * 16
    count = float(band_ex * band_rows * cols * n_dev)
    me = lax.axis_index("space").astype(jnp.int32)
    place = jnp.stack([me, lax.axis_index("core").astype(jnp.int32)])
    small, large = (n_dev, stat_rows(mid), 128), (n_dev, stat_rows(chan), 128)
    wmid = conv_mid_w.reshape(3, 3 * mid, mid)
    weights = [(mid, chan), (mid, 9 * mid), (chan, mid), (width, chan), (3 * width, width), (width, width), (ff, width), (width, ff)]
    parted = dp == 16 and all(c % (16 * dp) == 0 and r % 256 == 0 for c, r in weights)
    hi = dp // 2

    def grad_outs(c, r):
        return [(part_shape(c, r, dp), BF16)] * 2 if parted else [((c, r), BF16)]

    def natural(c, r):
        return [pltpu.VMEM((c, r), BF16)] if parted else []

    got_x = swap(lax.dynamic_slice_in_dim(image_in, (1 - me) * ex, ex, axis=0))
    parts1, = call(functools.partial(stats_kernel, cols), [(small, F32)], image_in, conv_in_w,
                   scratch=[pltpu.VMEM((band_ex * band_rows, 16, chan), BF16)], name="stats_one")
    parts1 = spread(parts1)
    xs, act1, wide, act2, parts2 = call(
        functools.partial(conv_fwd_kernel, count, ex, rows, cols),
        [((ex, rows, 16, chan), BF16), ((ex * px, mid), F32), ((ex, px + 32, 3 * mid), BF16), ((ex * px, mid), F32), (small, F32)],
        parts1, image_in, got_x, conv_in_w, bn1_gain, bn1_shift, wmid, place=place, name="conv_three", us=4)
    parts2 = spread(parts2)
    relu2, act3, parts3 = call(
        functools.partial(expand_kernel, count, cols),
        [((ex * px, mid), BF16), ((ex * px, chan), F32), (large, F32)],
        parts2, act2, bn2_gain, bn2_shift, conv_out_w, name="expand")
    parts3 = spread(parts3)
    stem, h0 = call(
        functools.partial(tokens_kernel, count, ex, cols, n_image, pad),
        [((ex * px, chan), BF16), ((ex * pad, width), BF16)],
        parts3, act3, xs, bn3_gain, bn3_shift, proj_w, proj_b, text_in, name="tokens", us=5)
    z1, q, k, v, p, attn, h1, z2 = attn_fwd(h0, prefix, text_len, ln1_gain, ln1_shift, qkv_w, query_bias, value_bias,
                                            out_w, out_b, ln2_gain, ln2_shift, ex, n_image, pad)
    mlp_outs = mlp(place, z2, h1, cotangent, up_w, up_b, down_w, down_b, ln2_gain, pad, dp, parted)
    block_out, mlp_grads, (g1, veca) = mlp_outs[0], mlp_outs[1:-2], mlp_outs[-2:]
    if parted:
        down, up = Halving(*mlp_grads[:2]), Halving(*mlp_grads[2:])
    att_outs = attn_bwd(place, g1, out_w, attn, q, k, v, p, z1, h0, qkv_w, ln1_gain, ex, n_image, txt, rows, cols, pad, dp, parted)
    att_grads, (text_grad, dtok, vecb) = att_outs[:-3], att_outs[-3:]
    if parted:
        dtok = step([(down, "space"), (up, "f0")], 3, dtok)
        att = Halving(*att_grads)
    dpre, dsend, parts4 = call(
        functools.partial(dpre_kernel, count, ex, rows),
        [((ex, rows, 16, chan), F32), ((ex, band_rows, 16, chan), BF16), (large, F32)],
        parts3, act3, xs, bn3_gain, bn3_shift, dtok, proj_w, place=place, name="stem_back", us=7)
    got_d = swap(dsend)
    parts4 = spread(parts4)
    proj_g = call(functools.partial(tn_kernel, parted), grad_outs(width, chan), dtok, stem, place=place, scratch=natural(width, chan), name="proj_grad")
    if parted:
        proj = Halving(*proj_g)
        dpre = step([(att, "near")], 3, dpre)
    low3, t2, parts5, bn3_gg, bn3_sg = call(
        functools.partial(back3_kernel, count, cols),
        [((ex * px, chan), BF16), ((ex * px, mid), F32), (small, F32), ((chan,), F32), ((chan,), F32)],
        parts4, parts3, parts2, act3, dpre, bn3_gain, conv_out_w, act2, bn2_gain, bn2_shift, veca, vecb,
        scratch=[pltpu.VMEM((n_dev * -(-(veca.shape[0] + vecb.shape[0]) // n_dev), 128), F32)], name="back_three", us=4)
    parts5 = spread(parts5)
    if parted:
        t2 = step([(down, "near"), (up, "space"), (proj, "f0")], 3, t2)
    low2, t1, tsend, parts6, bn2_gg, bn2_sg = call(
        functools.partial(back2_kernel, count, ex, rows, cols),
        [((ex * px, mid), BF16), ((ex, rows, 16, mid), F32), ((ex, band_rows, 16, mid), BF16), (small, F32), ((mid,), F32), ((mid,), F32)],
        parts5, parts2, parts1, act2, t2, bn2_gain, wmid, act1, bn1_gain, bn1_shift,
        place=place, scratch=[pltpu.VMEM((ex, px + 32, 3 * mid), BF16)], name="back_two", us=4)
    got_t = swap(tsend)
    parts6 = spread(parts6)
    conv_g = call(
        functools.partial(conv_grads_kernel, ex, px, parted),
        [(part_shape(mid, 9 * mid, dp)[:2] + (part_shape(mid, 9 * mid, dp)[2] + part_shape(chan, mid, dp)[2], 128), BF16)] * 2
        if parted else [((mid, 9 * mid), BF16), ((chan, mid), BF16)],
        low2, wide, low3, relu2, place=place, scratch=natural(mid, 9 * mid) + natural(chan, mid), name="conv_grads")
    if parted:
        conv = Halving(*conv_g)
        t1 = step([(down, "f0"), (up, "near"), (att, "f0"), (proj, "near")], 3, t1)
        t1 = step([(conv, "space")], 1, t1)
    each = -(-(veca.shape[0] + vecb.shape[0]) // n_dev)
    n, off = width // 128, veca.shape[0]
    places = [off, off + n, off + 2 * n, off + 3 * n, off + 4 * n, 3 * n, n, 2 * n, 4 * n, 0]
    sizes = [width] * 8 + [ff, width]
    last = call(
        functools.partial(image_kernel, count, ex, rows, cols, parted, each, places),
        [(image_in.shape, BF16)] + grad_outs(mid, chan) + [((mid,), F32)] * 2 + [((s,), F32) for s in sizes],
        parts6, parts1, image_in, conv_in_w, bn1_gain, t1, got_t, dpre, got_d,
        place=place, scratch=[pltpu.VMEM((ex * band_rows, 16, chan), BF16), pltpu.VMEM((n_dev * each, 128), F32)] + natural(mid, chan),
        name="image_back", us=5)
    image_grad, sums = last[0], last[3 if parted else 2 :]
    bn1_gg, bn1_sg, vecs = sums[0], sums[1], sums[2:]
    if parted:
        in_x = (last[1] + swap(last[2], "core")).reshape((2 * hi,) + last[1].shape[2:])
        image_grad = step([(conv, "near")], 1, image_grad)
        image_grad = step([(down, "f1"), (up, "f1"), (att, "space"), (proj, "space")], 3, image_grad)
        in_x = jnp.sum(lax.all_to_all(in_x, ("space", "far", "near"), split_axis=0, concat_axis=0, tiled=True).astype(F32), axis=0)
        image_grad = step([(conv, "f0"), (proj, "f1")], 1, image_grad)
        image_grad = step([(att, "f1"), (conv, "f1")], 1, image_grad)
        conv_x, att_x = conv.done(), att.done()
        r_mid, r_out3, r_q, r_w = mid // dp, chan // dp, 3 * width // dp, width // dp
        g_in = final(in_x, r_mid)
        g_mid = final(conv_x, r_mid, 0, 9 * mid // 256)
        g_out3 = final(conv_x, r_out3, r_mid * (9 * mid // 256), mid // 256)
        g_proj = final(proj.done(), r_w)
        g_qkv = final(att_x, r_q, 0, width // 256)
        g_out = final(att_x, r_w, r_q * (width // 256), width // 256)
        g_up = final(up.done(), ff // dp)
        g_down = final(down.done(), r_w)
    else:
        out_n = att_outs[0].transpose(1, 0, 2).reshape(width, width)
        g_in, g_mid, g_out3, g_proj, g_qkv, g_out, g_up, g_down = [
            scattered(x) for x in (last[1], conv_g[0], conv_g[1], proj_g[0], att_outs[1], out_n, mlp_grads[1], mlp_grads[0])]
    return (
        block_out, image_grad, text_grad,
        g_in, bn1_gg, bn1_sg,
        g_mid.reshape(3, 3, mid // 2, g_mid.shape[1]), bn2_gg, bn2_sg,
        g_out3, bn3_gg, bn3_sg,
        g_proj, vecs[0], vecs[1], vecs[2],
        g_qkv, vecs[3], vecs[4],
        g_out, vecs[5], vecs[6], vecs[7],
        g_up, vecs[8],
        g_down, vecs[9],
    )


def solution(mesh):
    dp, space = mesh.devices.shape
    fine = Mesh(mesh.devices.reshape(dp // 4, 2, 2, space), AXES)
    return jax.shard_map(
        shards,
        mesh=fine,
        in_specs=(
            P(DP, "space", None, None),
            P(AXES, None, None),
            P(AXES),
            P(AXES),
            P(AXES, None, None),
            P(),
            P(),
            P(),
            P(),
            P(),
            P(),
            P(),
            P(),
            P(),
            P(),
            P(),
            P(),
            P(),
            P(),
            P(),
            P(),
            P(),
            P(),
            P(),
            P(),
            P(),
            P(),
            P(),
            P(),
        ),
        out_specs=(
            P(AXES, None, None),
            P(DP, "space", None, None),
            P(AXES, None, None),
            P("space", DP),
            P(),
            P(),
            P(None, None, "space", DP),
            P(),
            P(),
            P("space", DP),
            P(),
            P(),
            P("space", DP),
            P(),
            P(),
            P(),
            P("space", DP),
            P(),
            P(),
            P("space", DP),
            P(),
            P(),
            P(),
            P("space", DP),
            P(),
            P("space", DP),
            P(),
        ),
        check_vma=False,
    )
```

time: 447 us -> 354 us (0.79)
  waiting for transfers between devices: 115 us -> 43.7 us
  starting transfers between devices: 73.5 us -> 50.6 us
  Pallas kernels: 137 us -> 157 us
  other arithmetic: 17.5 us -> 1.5 us
    ppermute x43 -> x29, waiting for transfers between devices: 105 us -> 25.2 us  [the longest x10 21.1 us: exchange(): return lax.ppermute(send, 'far', [(j, j ^ flip) for j in range(4)])]
    unnamed x162 -> x242, local copies, waits for them, and re-layouts: 27 us -> 63.3 us
    pallas_call x12 -> x20, Pallas kernels: 72.5 us -> 94.2 us  [the longest x1 42 us: mlp(): pl.pallas_call(functools.partial(mlp_kernel, ex, seq, pad, parted), grid=...]
    dynamic_slice x40 -> x0, local copies, waits for them, and re-layouts: 17.1 us -> none  [the longest x32 15.4 us: halve_dp(): send = lax.dynamic_index_in_dim(x, 1 - mine, axis, keepdims=True)]
    ppermute x43 -> x29, starting transfers between devices: 48.3 us -> 31.5 us  [the longest x10 14 us: exchange(): return lax.ppermute(send, 'far', [(j, j ^ flip) for j in range(4)])]
    add x32 -> x6, other arithmetic: 12 us -> 0.93 us  [the longest x1 0.8 us: shards(): last[1] + swap(last[2], 'core')]
    slice x16 -> x3, local copies, waits for them, and re-layouts: 9.65 us -> 0.66 us  [final(): x = x[at:at + r * blocks].astype(F32).reshape(blocks, r, 128)]
    all_to_all x6 -> x5, waiting for transfers between devices: 10.6 us -> 18.4 us  [the longest x4 18.4 us: spread(): return lax.all_to_all(parts, AXES, split_axis=0, concat_axis=0, tiled=True)]
  transfers between devices with their start and end apart: 49 -> 34, of which waited for: 27 -> 10; matrix products, arithmetic and copies ran while one was open for 12% -> 2% of each run, Pallas kernels for 5% -> 24%
where the time goes in v3:
time: 354 us; the launch traced here: 349 us
  Pallas kernels  157 us (44%)
  local copies, waits for them, and re-layouts  68.4 us (19%)
  starting transfers between devices  50.6 us (14%)
  waiting for transfers between devices  43.7 us (12%)
  blocking collectives  25.9 us (7%)
    unnamed x242, local copies, waits for them, and re-layouts  63.3 us
    pallas_call x1, Pallas kernels, mlp(): pl.pallas_call(functools.partial(mlp_kernel, ex, seq, pad, parted), grid=...  42 us
    pallas_call x1, Pallas kernels, attn_bwd(): pl.pallas_call(functools.partial(attn_bwd_kernel, ex, n_image, txt, img_c...  37.6 us
    pallas_call x10, Pallas kernels, call(): pl.pallas_call(kernel, out_shape=[jax.ShapeDtypeStruct(s, d) for s, d in...  27.5 us
    all_to_all x2, blocking collectives, spread(): return lax.all_to_all(parts, AXES, split_axis=0, concat_axis=0, tiled=True)  25.9 us
    pallas_call x1, Pallas kernels, attn_fwd(): pl.pallas_call(functools.partial(attn_fwd_kernel, ex, n_image, pad), grid...  25.3 us
    pallas_call x9, Pallas kernels, combine(): pl.pallas_call(functools.partial(combine_kernel, len(items)), grid_spec=p...  24.7 us
    ppermute x10, waiting for transfers between devices, exchange(): return lax.ppermute(send, 'far', [(j, j ^ flip) for j in range(4)])  21.1 us
  transfers between devices with their start and end apart: 34, of which 10 were waited for; matrix products, arithmetic and copies ran while one was open for 2% of the time, Pallas kernels for 24%

profile of v3, /device:TPU:0, one launch (start us, length us, event | category | flops | bytes accessed | tf_op | source)
XLA Modules:
  0.0 348.9 jit_solution(15539985971198738479)
XLA Ops:
  0.7 2.1 constant_dynamic-slice_fusion
  2.8 2.9 collective-permute-start
  6.8 1.2 stats_one.1
  8.0 4.9 %all-to-all-start = ((f32[32,8,128]{2,1,0:T(8,128)}), f32[32,8,128]{2,1,0:T(8,128)S(1)}, u32[]{:S(2)}, u32[]{:S(2)}) async-start(f32[32,8,128]{2,1,0:T(8,128)} %stats_one.1), calls=%async_computation | async-start | bytes 262144 | tf_op jit(solution)/shard_map/all_to_all | solution.py:738
  13.1 10.9 %all-to-all-done.parts_ref.parts1_ref = f32[32,8,128]{2,1,0:T(8,128)S(1)} async-done(((f32[32,8,128]{2,1,0:T(8,128)}), f32[32,8,128]{2,1,0:T(8,128)S(1)}, u32[]{:S(2)}, u32[]{:S(2)}) %all-to-all-start) | async-done | bytes 131104 | tf_op jit(solution)/shard_map/all_to_all | solution.py:738
  25.1 2.8 conv_three.1
  29.8 13.3 %all_to_all.35.parts_ref.parts2_ref = f32[32,8,128]{2,1,0:T(8,128)S(1)} all-to-all(f32[32,8,128]{2,1,0:T(8,128)S(1)} %get-tuple-element.179), channel_id=1, replica_groups=mesh['far'=4,'near'=2,'core'=2,'space'=2] {'far','near','core','space'}, dimensions={0} | all-to-all | bytes 262144 | tf_op jit(solution)/shard_map/all_to_all | solution.py:738
  44.9 12.6 %all_to_all.36.parts_ref.parts3_ref = f32[32,16,128]{2,1,0:T(8,128)S(1)} all-to-all(f32[32,16,128]{2,1,0:T(8,128)S(1)} %get-tuple-element.181), channel_id=1, replica_groups=mesh['far'=4,'near'=2,'core'=2,'space'=2] {'far','near','core','space'}, dimensions={0} | all-to-all | bytes 524288 | tf_op jit(solution)/shard_map/all_to_all | solution.py:738
  57.7 2.9 tokens.1
  61.9 25.3 %attention_forward.1 = (bf16[816,768]{1,0:T(8,128)(2,1)S(1)}, bf16[816,768]{1,0:T(8,128)(2,1)S(1)}, bf16[816,768]{1,0:T(8,128)(2,1)S(1)}, bf16[816,768]{1,0:T(8,...) custom-call(s32[3]{0:T(128)S(1)} %copy-done.60, ...), custom_call_target="tpu_custom_call" | custom-call | flops 32000000000 | bytes 31457280 | tf_op jit(solution)/shard_map/attention_forward/pallas_call | solution.py:315
  87.1 1.4 copy-done.116
  90.7 42.0 %mlp_both_ways.1 = (bf16[3,260,768]{2,1,0:T(8,128)(2,1)}, bf16[2,8,576,128]{3,2,1,0:T(8,128)(2,1)S(1)}, bf16[2,8,576,128]{3,2,1,0:T(8,128)(2,1)}, bf16[2,8,576,1...) custom-call(s32[2]{0:T(128)S(1)} %copy-done.78, ...), custom_call_target="tpu_custom_call" | custom-call | flops 46000001024 | bytes 31457280 | tf_op jit(solution)/shard_map/mlp_both_ways/pallas_call | solution.py:184
  132.6 1.4 copy-done
  135.1 37.6 %attention_backward.1 = (bf16[2,8,576,128]{3,2,1,0:T(8,128)(2,1)}, bf16[2,8,576,128]{3,2,1,0:T(8,128)(2,1)}, bf16[3,64,768]{2,1,0:T(8,128)(2,1)}, bf16[672,768]{1,0:T(8,128)(2,1)S(1)}, f32[32,128]{1,0:T(8,128)S(1)}) custom-call(s32[2]{0:T(128)S(1)} %copy-done.78, f32[816,768]{1,0:T(8,128)} %get-tuple-element.188.g1_ref, bf16[768,768]{1,0:T(8,128)(2,1)S(1)} %copy-done.23, ...), custom_call_target="tpu_custom_call" | custom-call | flops 41999998976 | bytes 41943040 | tf_op jit(solution)/shard_map/attention_backward/pallas_call | solution.py:462
  174.5 1.7 copy-done.1
  176.2 6.4 %combine.9 = (bf16[1,8,576,128]{3,2,1,0:T(8,128)(2,1)S(1)}, bf16[1,8,576,128]{3,2,1,0:T(8,128)(2,1)}, bf16[4,2,576,128]{3,2,1,0:T(8,128)(2,1)S(1)}, bf16[4,2,576,128]{3,2,1,0:T(8,128)(2,1)}) custom-call(s32[2]{0:T(128)S(1)} %pad_add_fusion.1.bits_ref, bf16[1,2,8,576,128]{4,3,2,1,0:T(8,128)(2,1)S(1)} %bitcast.107, ...), custom_call_target="tpu_custom_call" | custom-call | flops 3000000000 | bytes 28311552 | tf_op jit(solution)/shard_map/combine/pallas_call | solution.py:773
  185.1 4.5 %stem_back.1 = (f32[3,14,16,1024]{3,2,1,0:T(8,128)S(1)}, bf16[3,7,16,1024]{3,2,1,0:T(8,128)(2,1)S(1)}, f32[32,16,128]{2,1,0:T(8,128)}) custom-call(s32[2]{0:T(128)S(1)} %copy-done.79, f32[32,16,128]{2,1,0:T(8,128)S(1)} %copy-done.9, f32[672,1024]{1,0:T(8,128)S(1)} %copy-done.86, bf16[3,14,16,1024]{3,2,1,0:T(8,128)(2,1)S(1)} %copy-done.106, ...), custom_call_target="tpu_custom_call" | custom-call | flops 7000000000 | bytes 7004160 | tf_op jit(solution)/shard_map/stem_back/pallas_call | solution.py:721
  190.4 1.6 copy-done.92
  192.1 2.6 all-to-all-start.3
  194.7 1.3 copy-done.91
  196.0 1.2 copy-done.97
  197.2 3.1 proj_grad.1
  201.6 1.7 copy-done.62
  203.3 3.7 %combine.10 = (bf16[8,1,576,128]{3,2,1,0:T(8,128)(2,1)S(1)}, bf16[8,1,576,128]{3,2,1,0:T(8,128)(2,1)}) custom-call(s32[1]{0:T(128)} %bitcast.8.bits_ref, bf16[8,2,1,576,128]{4,3,2,1,0:T(8,128)(2,1)S(1)} %bitcast.143, bf16[8,2,1,576,128]{4,3,2,1,0:T(8,128)(2,1)} %bitcast.10.refs_1_.refs_3_, bf16[8,2,1,576,128]{4,3,2,1,0:T(8,128)(2,1)S(1)} %bitcast.144, ...), custom_call_target="tpu_custom_call" | custom-call | flops 3000000000 | bytes 14155776 | tf_op jit(solution)/shard_map/combine/pallas_call | solution.py:773
  208.0 1.7 collective-permute-start.9
  209.7 7.5 %all-to-all-done.3.parts4_ref = f32[32,16,128]{2,1,0:T(8,128)S(1)} async-done(((f32[32,16,128]{2,1,0:T(8,128)}), f32[32,16,128]{2,1,0:T(8,128)S(1)}, u32[]{:S(2)}, u32[]{:S(2)}) %all-to-all-start.3) | async-done | bytes 262176 | tf_op jit(solution)/shard_map/all_to_all | solution.py:738
  221.8 1.8 copy-done.87
  223.6 1.8 copy-done.93
  225.3 1.1 copy-done.101
  227.9 1.9 back_three.1
  232.5 3.5 %all-to-all-start.4 = ((f32[32,8,128]{2,1,0:T(8,128)}), f32[32,8,128]{2,1,0:T(8,128)}, u32[]{:S(2)}, u32[]{:S(2)}) async-start(f32[32,8,128]{2,1,0:T(8,128)} %copy-done.19), calls=%async_computation.4 | async-start | bytes 262144 | tf_op jit(solution)/shard_map/all_to_all | solution.py:738
  236.0 1.1 copy-done.5
  237.1 4.6 %combine.11 = (bf16[4,1,576,128]{3,2,1,0:T(8,128)(2,1)S(1)}, bf16[4,1,576,128]{3,2,1,0:T(8,128)(2,1)}, bf16[1,4,576,128]{3,2,1,0:T(8,128)(2,1)S(1)}, bf16[1,4,57...) custom-call(s32[3]{0:T(128)S(1)} %pad_add_fusion.2.bits_ref, ...), custom_call_target="tpu_custom_call" | custom-call | flops 3000000000 | bytes 18874368 | tf_op jit(solution)/shard_map/combine/pallas_call | solution.py:773
  244.1 1.7 collective-permute-start.7
  245.8 1.5 collective-permute-start.8
  249.1 1.3 copy-done.25
  251.1 1.1 copy-done.102
  254.4 3.4 back_two.1
  257.8 2.4 conv_grads.1
  261.1 1.5 collective-permute-start.10
  263.3 3.9 %all-to-all-start.5 = ((f32[32,8,128]{2,1,0:T(8,128)}), f32[32,8,128]{2,1,0:T(8,128)S(1)}, u32[]{:S(2)}, u32[]{:S(2)}) async-start(f32[32,8,128]{2,1,0:T(8,128)} %get-tuple-element.231), calls=%async_computation.5 | async-start | bytes 262144 | tf_op jit(solution)/shard_map/all_to_all | solution.py:738
  267.2 6.8 %collective-permute-done.10 = bf16[4,2,192,128]{3,2,1,0:T(8,128)(2,1)} collective-permute-done((bf16[4,2,192,128]{3,2,1,0:T(8,128)(2,1)}, bf16[4,2,192,128]{3,2,1,0:T(8,128)(2,1)}, u32[]{:S(2)}, u32[]{:S(2)}) %collective-permute-start.10) | collective-permute-done | bytes 393248 | tf_op jit(solution)/shard_map/ppermute | solution.py:792
  276.6 1.3 copy-done.64
  277.9 4.5 %combine.12 = (bf16[2,1,576,128]{3,2,1,0:T(8,128)(2,1)S(1)}, bf16[2,1,576,128]{3,2,1,0:T(8,128)(2,1)}, bf16[2,1,576,128]{3,2,1,0:T(8,128)(2,1)S(1)}, bf16[2,1,57...) custom-call(s32[4]{0:T(128)S(1)} %pad_add_fusion.3.bits_ref, ...), custom_call_target="tpu_custom_call" | custom-call | flops 3000000000 | bytes 16515072 | tf_op jit(solution)/shard_map/combine/pallas_call | solution.py:773
  283.9 1.2 collective-permute-start.15
  287.0 2.0 collective-permute-start.18
  289.6 1.5 collective-permute-start.14
  293.1 1.8 copy-done.94
  296.0 4.2 %image_back.1 = (bf16[6,7,14,1024]{3,2,1,0:T(8,128)(2,1)}, bf16[2,8,64,128]{3,2,1,0:T(8,128)(2,1)S(1)}, bf16[2,8,64,128]{3,2,1,0:T(8,128)(2,1)S(1)}, f32[256]{0:...) custom-call(s32[2]{0:T(128)S(1)} %copy-done.82, ...), custom_call_target="tpu_custom_call" | custom-call | flops 5000000000 | bytes 6292480 | tf_op jit(solution)/shard_map/image_back/pallas_call | solution.py:721
  300.3 3.6 %collective-permute-done.15 = bf16[2,1,576,128]{3,2,0,1:T(8,128)(2,1)} collective-permute-done((bf16[2,1,576,128]{3,2,0,1:T(8,128)(2,1)}, bf16[2,1,576,128]{3,2,0,1:T(8,128)(2,1)}, u32[]{:S(2)}, u32[]{:S(2)}) %collective-permute-start.15) | collective-permute-done | bytes 294944 | tf_op jit(solution)/shard_map/ppermute | solution.py:792
  304.8 3.1 combine.15
  308.2 2.7 collective-permute-start.28
  311.8 4.1 %all-to-all-start.6 = ((bf16[16,64,128]{2,1,0:T(8,128)(2,1)}), bf16[16,64,128]{2,1,0:T(8,128)(2,1)S(1)}, u32[]{:S(2)}, u32[]{:S(2)}) async-start(bf16[16,64,128]{2,1,0:T(8,128)(2,1)} %bitcast.49), calls=%async_computation.6 | async-start | bytes 524288 | tf_op jit(solution)/shard_map/all_to_all | solution.py:959
  315.9 2.8 collective-permute-start.27
  318.7 1.5 collective-permute-start.20
  320.2 1.5 collective-permute-start.19
  322.3 2.7 collective-permute-done.20
  325.0 1.3 collective-permute-done.19
  327.0 1.2 collective-permute-start.25
  328.2 1.6 collective-permute-done.27
  332.8 3.6 %collective-permute-done.22 = bf16[2,1,208,128]{3,2,0,1:T(8,128)(2,1)S(1)} collective-permute-done((bf16[2,1,208,128]{3,2,0,1:T(8,128)(2,1)S(1)}, bf16[2,1,208,128]{3,2,0,1:T(8,128)(2,1)S(1)}, u32[]{:S(2)}, u32[]{:S(2)}) %collective-permute-start.22) | collective-permute-done | bytes 106528 | tf_op jit(solution)/shard_map/ppermute | solution.py:792
  337.1 1.4 collective-permute-start.26
  338.5 1.6 collective-permute-start.24
  340.7 5.1 %collective-permute-done.24 = bf16[1,1,208,128]{3,2,1,0:T(8,128)(2,1)S(1)} collective-permute-done((bf16[1,1,208,128]{3,2,1,0:T(8,128)(2,1)S(1)}, bf16[1,1,208,128]{3,2,1,0:T(8,128)(2,1)S(1)}, u32[]{:S(2)}, u32[]{:S(2)}) %collective-permute-start.24) | collective-permute-done | bytes 53280 | tf_op jit(solution)/shard_map/ppermute | solution.py:792
  (295 shorter events, 55.1 us)
Async XLA Ops:
  2.8 21.2 %copy-start.24 = (bf16[3,3,256,256]{3,2,1,0:T(8,128)(2,1)S(1)}, bf16[3,3,256,256]{3,2,1,0:T(8,128)(2,1)}, u32[]{:S(2)}) copy-start(bf16[3,3,256,256]{3,2,1,0:T(8,128)(2,1)} %param.37) | copy-start | bytes 3538948
  2.8 21.2 %collective-permute-start = (bf16[3,7,14,1024]{3,2,1,0:T(8,128)(2,1)}, bf16[3,7,14,1024]{3,2,1,0:T(8,128)(2,1)S(1)}, u32[]{:S(2)}, u32[]{:S(2)}) collective-permute-start(bf16[3,7,14,1024]{3,2,1,0:T(8,128)(2,1)} %constant_dynamic-slice_fusion), channel_id=1, source_target_pairs={{0,1},{1,0},{2,3},{3,2},{4,5},{5,4},{6,7},{7,6},{8,9},{9,8},{10,11... | collective-permute-start | bytes 1806344 | tf_op jit(solution)/shard_map/ppermute | solution.py:742
  6.8 17.2 %copy-start.55 = (f32[256]{0:T(256)S(1)}, f32[256]{0:T(256)}, u32[]{:S(2)}) copy-start(f32[256]{0:T(256)} %s1_ref.1) | copy-start | bytes 3076
  6.8 17.2 %copy-start.58 = (f32[256]{0:T(256)S(1)}, f32[256]{0:T(256)}, u32[]{:S(2)}) copy-start(f32[256]{0:T(256)} %g_ref.15) | copy-start | bytes 3076
  8.0 15.9 %all-to-all-start = ((f32[32,8,128]{2,1,0:T(8,128)}), f32[32,8,128]{2,1,0:T(8,128)S(1)}, u32[]{:S(2)}, u32[]{:S(2)}) async-start(f32[32,8,128]{2,1,0:T(8,128)} %stats_one.1), calls=%async_computation | async-start | bytes 262144 | tf_op jit(solution)/shard_map/all_to_all | solution.py:738
  13.1 14.9 %copy-start.77 = (s32[2]{0:T(128)}, s32[2]{0:T(128)S(1)}, u32[]{:S(2)}) copy-start(s32[2]{0:T(128)S(1)} %pad_add_fusion.place_ref) | copy-start | bytes 28
  25.1 18.1 %copy-start.32 = (bf16[256,1024]{1,0:T(8,128)(2,1)S(1)}, bf16[256,1024]{1,0:T(8,128)(2,1)}, u32[]{:S(2)}) copy-start(bf16[256,1024]{1,0:T(8,128)(2,1)} %w_ref.9) | copy-start | bytes 1572868
  25.1 18.1 %copy-start.54 = (f32[256]{0:T(256)S(1)}, f32[256]{0:T(256)}, u32[]{:S(2)}) copy-start(f32[256]{0:T(256)} %s2_ref.3) | copy-start | bytes 3076
  25.1 18.1 %copy-start.57 = (f32[256]{0:T(256)S(1)}, f32[256]{0:T(256)}, u32[]{:S(2)}) copy-start(f32[256]{0:T(256)} %g2_ref.5) | copy-start | bytes 3076
  29.8 14.3 %copy-start.100 = (f32[672,256]{1,0:T(8,128)}, f32[672,256]{1,0:T(8,128)S(1)}, u32[]{:S(2)}) copy-start(f32[672,256]{1,0:T(8,128)S(1)} %get-tuple-element.180.act2_ref) | copy-start | bytes 2064388
  29.8 27.7 %copy-start.105 = (bf16[3,14,16,1024]{3,2,1,0:T(8,128)(2,1)}, bf16[3,14,16,1024]{3,2,1,0:T(8,128)(2,1)S(1)}, u32[]{:S(2)}) copy-start(bf16[3,14,16,1024]{3,2,1,0:T(8,128)(2,1)S(1)} %get-tuple-element.183.xs_ref) | copy-start | bytes 4128772
  43.1 14.4 %copy-start.20 = (bf16[1024,768]{1,0:T(8,128)(2,1)S(1)}, bf16[1024,768]{1,0:T(8,128)(2,1)}, u32[]{:S(2)}) copy-start(bf16[1024,768]{1,0:T(8,128)(2,1)} %w_ref.8) | copy-start | bytes 4718596
  43.1 14.4 %copy-start.39 = (bf16[3,64,768]{2,1,0:T(8,128)(2,1)S(1)}, bf16[3,64,768]{2,1,0:T(8,128)(2,1)}, u32[]{:S(2)}) copy-start(bf16[3,64,768]{2,1,0:T(8,128)(2,1)} %text_ref.1) | copy-start | bytes 884740
  43.2 14.4 %copy-start.43 = (f32[768]{0:T(1024)S(1)}, f32[768]{0:T(1024)}, u32[]{:S(2)}) copy-start(f32[768]{0:T(1024)} %b_ref.1) | copy-start | bytes 9220
  43.2 14.4 %copy-start.52 = (f32[1024]{0:T(1024)S(1)}, f32[1024]{0:T(1024)}, u32[]{:S(2)}) copy-start(f32[1024]{0:T(1024)} %s_ref.9) | copy-start | bytes 12292
  43.2 14.4 %copy-start.53 = (f32[1024]{0:T(1024)S(1)}, f32[1024]{0:T(1024)}, u32[]{:S(2)}) copy-start(f32[1024]{0:T(1024)} %g3_ref.1) | copy-start | bytes 12292
  44.9 15.7 %copy-start.85 = (f32[672,1024]{1,0:T(8,128)}, f32[672,1024]{1,0:T(8,128)S(1)}, u32[]{:S(2)}) copy-start(f32[672,1024]{1,0:T(8,128)S(1)} %get-tuple-element.182.act3_ref) | copy-start | bytes 8257540
  61.7 25.4 %copy-start.107 = (bf16[816,768]{1,0:T(8,128)(2,1)}, bf16[816,768]{1,0:T(8,128)(2,1)S(1)}, u32[]{:S(2)}) copy-start(bf16[816,768]{1,0:T(8,128)(2,1)S(1)} %get-tuple-element.184.h0_ref) | copy-start | bytes 3760132
  61.8 28.8 %copy-start.22 = (bf16[3,260,768]{2,1,0:T(8,128)(2,1)S(1)}, bf16[3,260,768]{2,1,0:T(8,128)(2,1)}, u32[]{:S(2)}) copy-start(bf16[3,260,768]{2,1,0:T(8,128)(2,1)} %cot_ref.1) | copy-start | bytes 3594244
  61.8 28.8 %copy-start.42 = (f32[3072]{0:T(1024)S(1)}, f32[3072]{0:T(1024)}, u32[]{:S(2)}) copy-start(f32[3072]{0:T(1024)} %upb_ref.1) | copy-start | bytes 36868
  61.8 28.8 %copy-start.50 = (f32[768]{0:T(1024)S(1)}, f32[768]{0:T(1024)}, u32[]{:S(2)}) copy-start(f32[768]{0:T(1024)} %dnb_ref.1) | copy-start | bytes 9220
  61.9 28.8 %copy-start.78 = (s32[2]{0:T(128)S(1)}, s32[2]{0:T(128)}, u32[]{:S(2)}) copy-start(s32[2]{0:T(128)} %copy-done.77) | copy-start | bytes 28
  134.6 39.9 %collective-permute-start.1 = (bf16[2,8,576,128]{3,2,1,0:T(8,128)(2,1)}, bf16[2,8,576,128]{3,2,1,0:T(8,128)(2,1)}, u32[]{:S(2)}, u32[]{:S(2)}) collective-permute-start(bf16[2,8,576,128]{3,2,1,0:T(8,128)(2,1)} %get-tuple-element.197), channel_id=1, source_target_pairs={{0,2},{2,0},{1,3},{3,1},{4,6},{6,4},{5,7},{7,5},{8,10},{10,8},{9,1... | collective-permute-start | bytes 7077896 | tf_op jit(solution)/shard_map/ppermute | solution.py:793
  134.7 39.8 %collective-permute-start.2 = (bf16[2,8,576,128]{3,2,1,0:T(8,128)(2,1)}, bf16[2,8,576,128]{3,2,1,0:T(8,128)(2,1)}, u32[]{:S(2)}, u32[]{:S(2)}) collective-permute-start(bf16[2,8,576,128]{3,2,1,0:T(8,128)(2,1)} %get-tuple-element.199), channel_id=1, source_target_pairs={{0,2},{2,0},{1,3},{3,1},{4,6},{6,4},{5,7},{7,5},{8,10},{10,8},{9,1... | collective-permute-start | bytes 7077896 | tf_op jit(solution)/shard_map/ppermute | solution.py:793
  174.3 27.3 %collective-permute-start.3 = (bf16[2,8,576,128]{3,2,1,0:T(8,128)(2,1)}, bf16[2,8,576,128]{3,2,1,0:T(8,128)(2,1)}, u32[]{:S(2)}, u32[]{:S(2)}) collective-permute-start(bf16[2,8,576,128]{3,2,1,0:T(8,128)(2,1)} %get-tuple-element.208), channel_id=1, source_target_pairs={{0,2},{2,0},{1,3},{3,1},{4,6},{6,4},{5,7},{7,5},{8,10},{10,8},{9,1... | collective-permute-start | bytes 7077896 | tf_op jit(solution)/shard_map/ppermute | solution.py:793
  176.1 8.9 %copy-start.9 = (f32[32,16,128]{2,1,0:T(8,128)S(1)}, f32[32,16,128]{2,1,0:T(8,128)}, u32[]{:S(2)}) copy-start(f32[32,16,128]{2,1,0:T(8,128)} %copy-done.8) | copy-start | bytes 786436
  176.2 8.9 %copy-start.21 = (bf16[1024,768]{1,0:T(8,128)(2,1)S(1)}, bf16[1024,768]{1,0:T(8,128)(2,1)}, u32[]{:S(2)}) copy-start(bf16[1024,768]{1,0:T(8,128)(2,1)} %w_ref.8) | copy-start | bytes 4718596
  176.2 8.9 %copy-start.79 = (s32[2]{0:T(128)S(1)}, s32[2]{0:T(128)}, u32[]{:S(2)}) copy-start(s32[2]{0:T(128)} %copy-done.77) | copy-start | bytes 28
  176.2 8.9 %copy-start.86 = (f32[672,1024]{1,0:T(8,128)S(1)}, f32[672,1024]{1,0:T(8,128)}, u32[]{:S(2)}) copy-start(f32[672,1024]{1,0:T(8,128)} %copy-done.85) | copy-start | bytes 8257540
  176.2 8.9 %copy-start.96 = (bf16[672,768]{1,0:T(8,128)(2,1)S(1)}, bf16[672,768]{1,0:T(8,128)(2,1)}, u32[]{:S(2)}) copy-start(bf16[672,768]{1,0:T(8,128)(2,1)} %copy-done.95) | copy-start | bytes 3096580
  176.2 8.9 %copy-start.106 = (bf16[3,14,16,1024]{3,2,1,0:T(8,128)(2,1)S(1)}, bf16[3,14,16,1024]{3,2,1,0:T(8,128)(2,1)}, u32[]{:S(2)}) copy-start(bf16[3,14,16,1024]{3,2,1,0:T(8,128)(2,1)} %copy-done.105) | copy-start | bytes 4128772
  183.6 11.1 %copy-start.80 = (s32[2]{0:T(128)S(1)}, s32[2]{0:T(128)}, u32[]{:S(2)}) copy-start(s32[2]{0:T(128)} %copy-done.77) | copy-start | bytes 28
  183.6 52.4 %collective-permute-start.4 = (bf16[1,8,576,128]{3,2,1,0:T(8,128)(2,1)}, bf16[1,8,576,128]{3,2,1,0:T(8,128)(2,1)S(1)}, u32[]{:S(2)}, u32[]{:S(2)}) collective-permute-start(bf16[1,8,576,128]{3,2,1,0:T(8,128)(2,1)} %get-tuple-element.217), channel_id=1, source_target_pairs={{0,1},{1,0},{2,3},{3,2},{4,5},{5,4},{6,7},{7,6},{8,9},{9,8},{10,11... | collective-permute-start | bytes 3538952 | tf_op jit(solution)/shard_map/ppermute | solution.py:793
  184.3 51.7 %collective-permute-start.5 = (bf16[4,2,576,128]{3,2,1,0:T(8,128)(2,1)}, bf16[4,2,576,128]{3,2,1,0:T(8,128)(2,1)}, u32[]{:S(2)}, u32[]{:S(2)}) collective-permute-start(bf16[4,2,576,128]{3,2,1,0:T(8,128)(2,1)} %get-tuple-element.219), channel_id=1, source_target_pairs={{0,8},{8,0},{16,24},{24,16},{1,9},{9,1},{17,25},{25,17},{2,10},{10... | collective-permute-start | bytes 3538952 | tf_op jit(solution)/shard_map/ppermute | solution.py:792
  192.1 25.2 %all-to-all-start.3 = ((f32[32,16,128]{2,1,0:T(8,128)}), f32[32,16,128]{2,1,0:T(8,128)S(1)}, u32[]{:S(2)}, u32[]{:S(2)}) async-start(f32[32,16,128]{2,1,0:T(8,128)} %get-tuple-element.205), calls=%async_computation.3 | async-start | bytes 524288 | tf_op jit(solution)/shard_map/all_to_all | solution.py:738
  201.3 34.7 %collective-permute-start.6 = (bf16[2,8,192,128]{3,2,1,0:T(8,128)(2,1)}, bf16[2,8,192,128]{3,2,1,0:T(8,128)(2,1)}, u32[]{:S(2)}, u32[]{:S(2)}) collective-permute-start(bf16[2,8,192,128]{3,2,1,0:T(8,128)(2,1)} %get-tuple-element.222), channel_id=1, source_target_pairs={{0,2},{2,0},{1,3},{3,1},{4,6},{6,4},{5,7},{7,5},{8,10},{10,8},{9,1... | collective-permute-start | bytes 2359304 | tf_op jit(solution)/shard_map/ppermute | solution.py:793
  208.0 54.6 %collective-permute-start.9 = (bf16[8,1,576,128]{3,2,1,0:T(8,128)(2,1)}, bf16[8,1,576,128]{3,2,1,0:T(8,128)(2,1)}, u32[]{:S(2)}, u32[]{:S(2)}) collective-permute-start(bf16[8,1,576,128]{3,2,1,0:T(8,128)(2,1)} %get-tuple-element.238), channel_id=1, source_target_pairs={{0,4},{4,0},{1,5},{5,1},{2,6},{6,2},{3,7},{7,3},{8,12},{12,8},{9,1... | collective-permute-start | bytes 3538952 | tf_op jit(solution)/shard_map/ppermute | solution.py:793
  232.5 14.9 %all-to-all-start.4 = ((f32[32,8,128]{2,1,0:T(8,128)}), f32[32,8,128]{2,1,0:T(8,128)}, u32[]{:S(2)}, u32[]{:S(2)}) async-start(f32[32,8,128]{2,1,0:T(8,128)} %copy-done.19), calls=%async_computation.4 | async-start | bytes 262144 | tf_op jit(solution)/shard_map/all_to_all | solution.py:738
  237.1 10.2 %copy-start.56 = (f32[256]{0:T(256)S(1)}, f32[256]{0:T(256)}, u32[]{:S(2)}) copy-start(f32[256]{0:T(256)} %s1_ref.1) | copy-start | bytes 3076
  237.1 10.2 %copy-start.59 = (f32[256]{0:T(256)S(1)}, f32[256]{0:T(256)}, u32[]{:S(2)}) copy-start(f32[256]{0:T(256)} %g_ref.15) | copy-start | bytes 3076
  244.1 30.4 %collective-permute-start.7 = (bf16[4,1,576,128]{3,2,1,0:T(8,128)(2,1)}, bf16[4,1,576,128]{3,2,1,0:T(8,128)(2,1)}, u32[]{:S(2)}, u32[]{:S(2)}) collective-permute-start(bf16[4,1,576,128]{3,2,1,0:T(8,128)(2,1)} %get-tuple-element.234), channel_id=1, source_target_pairs={{0,4},{4,0},{1,5},{5,1},{2,6},{6,2},{3,7},{7,3},{8,12},{12,8},{9,1... | collective-permute-start | bytes 1769480 | tf_op jit(solution)/shard_map/ppermute | solution.py:793
  245.8 28.7 %collective-permute-start.8 = (bf16[1,4,576,128]{3,2,1,0:T(8,128)(2,1)}, bf16[1,4,576,128]{3,2,1,0:T(8,128)(2,1)}, u32[]{:S(2)}, u32[]{:S(2)}) collective-permute-start(bf16[1,4,576,128]{3,2,1,0:T(8,128)(2,1)} %get-tuple-element.236), channel_id=1, source_target_pairs={{0,1},{1,0},{2,3},{3,2},{4,5},{5,4},{6,7},{7,6},{8,9},{9,8},{10,11... | collective-permute-start | bytes 1769480 | tf_op jit(solution)/shard_map/ppermute | solution.py:793
  257.8 16.8 %copy-start.29 = (bf16[4,1,576,128]{3,2,1,0:T(8,128)(2,1)S(1)}, bf16[4,1,576,128]{3,2,1,0:T(8,128)(2,1)}, u32[]{:S(2)}) copy-start(bf16[4,1,576,128]{3,2,1,0:T(8,128)(2,1)} %copy-done.28) | copy-start | bytes 1769476
  261.1 24.0 %collective-permute-start.11 = (bf16[2,8,208,128]{3,2,1,0:T(8,128)(2,1)S(1)}, bf16[2,8,208,128]{3,2,1,0:T(8,128)(2,1)S(1)}, u32[]{:S(2)}, u32[]{:S(2)}) collective-permute-start(bf16[2,8,208,128]{3,2,1,0:T(8,128)(2,1)S(1)} %get-tuple-element.255), channel_id=1, source_target_pairs={{0,2},{2,0},{1,3},{3,1},{4,6},{6,4},{5,7},{7,5},{8,10},{10,8},{9,1... | collective-permute-start | bytes 2555912 | tf_op jit(solution)/shard_map/ppermute | solution.py:793
  261.1 12.9 %collective-permute-start.10 = (bf16[4,2,192,128]{3,2,1,0:T(8,128)(2,1)}, bf16[4,2,192,128]{3,2,1,0:T(8,128)(2,1)}, u32[]{:S(2)}, u32[]{:S(2)}) collective-permute-start(bf16[4,2,192,128]{3,2,1,0:T(8,128)(2,1)} %get-tuple-element.240), channel_id=1, source_target_pairs={{0,8},{8,0},{16,24},{24,16},{1,9},{9,1},{17,25},{25,17},{2,10},{10... | collective-permute-start | bytes 1179656 | tf_op jit(solution)/shard_map/ppermute | solution.py:792
  262.6 24.4 %collective-permute-start.13 = (bf16[3,7,16,1024]{3,2,1,0:T(8,128)(2,1)S(1)}, bf16[3,7,16,1024]{3,2,1,0:T(8,128)(2,1)}, u32[]{:S(2)}, u32[]{:S(2)}) collective-permute-start(bf16[3,7,16,1024]{3,2,1,0:T(8,128)(2,1)S(1)} %copy-done.27), channel_id=1, source_target_pairs={{0,1},{1,0},{2,3},{3,2},{4,5},{5,4},{6,7},{7,6},{8,9},{9,8},{10,11... | collective-permute-start | bytes 2064392 | tf_op jit(solution)/shard_map/ppermute | solution.py:742
  263.3 27.8 %all-to-all-start.5 = ((f32[32,8,128]{2,1,0:T(8,128)}), f32[32,8,128]{2,1,0:T(8,128)S(1)}, u32[]{:S(2)}, u32[]{:S(2)}) async-start(f32[32,8,128]{2,1,0:T(8,128)} %get-tuple-element.231), calls=%async_computation.5 | async-start | bytes 262144 | tf_op jit(solution)/shard_map/all_to_all | solution.py:738
  274.0 14.9 %collective-permute-start.12 = (bf16[3,7,16,256]{3,2,1,0:T(8,128)(2,1)}, bf16[3,7,16,256]{3,2,1,0:T(8,128)(2,1)S(1)}, u32[]{:S(2)}, u32[]{:S(2)}) collective-permute-start(bf16[3,7,16,256]{3,2,1,0:T(8,128)(2,1)} %get-tuple-element.259), channel_id=1, source_target_pairs={{0,1},{1,0},{2,3},{3,2},{4,5},{5,4},{6,7},{7,6},{8,9},{9,8},{10,11... | collective-permute-start | bytes 516104 | tf_op jit(solution)/shard_map/ppermute | solution.py:742
  283.1 20.8 %collective-permute-start.17 = (bf16[4,1,576,128]{3,2,1,0:T(8,128)(2,1)}, bf16[4,1,576,128]{3,2,1,0:T(8,128)(2,1)}, u32[]{:S(2)}, u32[]{:S(2)}) collective-permute-start(bf16[4,1,576,128]{3,2,1,0:T(8,128)(2,1)} %get-tuple-element.272), channel_id=1, source_target_pairs={{0,8},{8,0},{16,24},{24,16},{1,9},{9,1},{17,25},{25,17},{2,10},{10... | collective-permute-start | bytes 1769480 | tf_op jit(solution)/shard_map/ppermute | solution.py:792
  283.9 19.9 %collective-permute-start.15 = (bf16[2,1,576,128]{3,2,0,1:T(8,128)(2,1)}, bf16[2,1,576,128]{3,2,0,1:T(8,128)(2,1)}, u32[]{:S(2)}, u32[]{:S(2)}) collective-permute-start(bf16[2,1,576,128]{3,2,0,1:T(8,128)(2,1)} %bitcast.31), channel_id=1, source_target_pairs={{0,8},{8,0},{16,24},{24,16},{1,9},{9,1},{17,25},{25,17},{2,10},{10... | collective-permute-start | bytes 884744 | tf_op jit(solution)/shard_map/ppermute | solution.py:792
  285.1 18.7 %collective-permute-start.16 = (bf16[2,1,576,128]{3,2,0,1:T(8,128)(2,1)S(1)}, bf16[2,1,576,128]{3,2,0,1:T(8,128)(2,1)}, u32[]{:S(2)}, u32[]{:S(2)}) collective-permute-start(bf16[2,1,576,128]{3,2,0,1:T(8,128)(2,1)S(1)} %bitcast.131), channel_id=1, source_target_pairs={{0,4},{4,0},{1,5},{5,1},{2,6},{6,2},{3,7},{7,3},{8,12},{12,8},{9,1... | collective-permute-start | bytes 884744 | tf_op jit(solution)/shard_map/ppermute | solution.py:793
  287.0 13.2 %collective-permute-start.18 = (bf16[4,1,192,128]{3,2,1,0:T(8,128)(2,1)}, bf16[4,1,192,128]{3,2,1,0:T(8,128)(2,1)S(1)}, u32[]{:S(2)}, u32[]{:S(2)}) collective-permute-start(bf16[4,1,192,128]{3,2,1,0:T(8,128)(2,1)} %get-tuple-element.274), channel_id=1, source_target_pairs={{0,4},{4,0},{1,5},{5,1},{2,6},{6,2},{3,7},{7,3},{8,12},{12,8},{9,1... | collective-permute-start | bytes 589832 | tf_op jit(solution)/shard_map/ppermute | solution.py:793
  289.6 18.3 %collective-permute-start.14 = (bf16[1,8,208,128]{3,2,1,0:T(8,128)(2,1)}, bf16[1,8,208,128]{3,2,1,0:T(8,128)(2,1)S(1)}, u32[]{:S(2)}, u32[]{:S(2)}) collective-permute-start(bf16[1,8,208,128]{3,2,1,0:T(8,128)(2,1)} %get-tuple-element.263), channel_id=1, source_target_pairs={{0,1},{1,0},{2,3},{3,2},{4,5},{5,4},{6,7},{7,6},{8,9},{9,8},{10,11... | collective-permute-start | bytes 1277960 | tf_op jit(solution)/shard_map/ppermute | solution.py:793
  300.2 10.8 %collective-permute-start.23 = (bf16[2,8,64,128]{3,2,1,0:T(8,128)(2,1)S(1)}, bf16[2,8,64,128]{3,2,1,0:T(8,128)(2,1)S(1)}, u32[]{:S(2)}, u32[]{:S(2)}) collective-permute-start(bf16[2,8,64,128]{3,2,1,0:T(8,128)(2,1)S(1)} %get-tuple-element.304), channel_id=1, source_target_pairs={{0,2},{2,0},{1,3},{3,1},{4,6},{6,4},{5,7},{7,5},{8,10},{10,8},{9,1... | collective-permute-start | bytes 786440 | tf_op jit(solution)/shard_map/ppermute | solution.py:742
  308.2 14.1 %collective-permute-start.28 = (bf16[1,1,576,128]{3,2,1,0:T(8,128)(2,1)S(1)}, bf16[1,1,576,128]{3,2,1,0:T(8,128)(2,1)S(1)}, u32[]{:S(2)}, u32[]{:S(2)}) collective-permute-start(bf16[1,1,576,128]{3,2,1,0:T(8,128)(2,1)S(1)} %get-tuple-element.329), channel_id=1, source_target_pairs={{0,16},{8,24},{16,0},{24,8},{1,17},{9,25},{17,1},{25,9},{2,18},{10... | collective-permute-start | bytes 442376 | tf_op jit(solution)/shard_map/ppermute | solution.py:792
  311.8 28.2 %all-to-all-start.6 = ((bf16[16,64,128]{2,1,0:T(8,128)(2,1)}), bf16[16,64,128]{2,1,0:T(8,128)(2,1)S(1)}, u32[]{:S(2)}, u32[]{:S(2)}) async-start(bf16[16,64,128]{2,1,0:T(8,128)(2,1)} %bitcast.49), calls=%async_computation.6 | async-start | bytes 524288 | tf_op jit(solution)/shard_map/all_to_all | solution.py:959
  315.9 13.9 %collective-permute-start.27 = (bf16[1,1,576,128]{3,2,1,0:T(8,128)(2,1)S(1)}, bf16[1,1,576,128]{3,2,1,0:T(8,128)(2,1)S(1)}, u32[]{:S(2)}, u32[]{:S(2)}) collective-permute-start(bf16[1,1,576,128]{3,2,1,0:T(8,128)(2,1)S(1)} %get-tuple-element.326), channel_id=1, source_target_pairs={{0,16},{8,24},{16,0},{24,8},{1,17},{9,25},{17,1},{25,9},{2,18},{10... | collective-permute-start | bytes 442376 | tf_op jit(solution)/shard_map/ppermute | solution.py:792
  318.7 6.3 %collective-permute-start.20 = (bf16[1,2,192,128]{3,2,1,0:T(8,128)(2,1)S(1)}, bf16[1,2,192,128]{3,2,1,0:T(8,128)(2,1)S(1)}, u32[]{:S(2)}, u32[]{:S(2)}) collective-permute-start(bf16[1,2,192,128]{3,2,1,0:T(8,128)(2,1)S(1)} %get-tuple-element.287), channel_id=1, source_target_pairs={{0,1},{1,0},{2,3},{3,2},{4,5},{5,4},{6,7},{7,6},{8,9},{9,8},{10,11... | collective-permute-start | bytes 294920 | tf_op jit(solution)/shard_map/ppermute | solution.py:793
  320.2 6.1 %collective-permute-start.19 = (bf16[4,1,208,128]{3,2,1,0:T(8,128)(2,1)S(1)}, bf16[4,1,208,128]{3,2,1,0:T(8,128)(2,1)S(1)}, u32[]{:S(2)}, u32[]{:S(2)}) collective-permute-start(bf16[4,1,208,128]{3,2,1,0:T(8,128)(2,1)S(1)} %get-tuple-element.285), channel_id=1, source_target_pairs={{0,4},{4,0},{1,5},{5,1},{2,6},{6,2},{3,7},{7,3},{8,12},{12,8},{9,1... | collective-permute-start | bytes 638984 | tf_op jit(solution)/shard_map/ppermute | solution.py:793
  321.7 11.1 %collective-permute-start.21 = (bf16[1,2,576,128]{3,2,1,0:T(8,128)(2,1)S(1)}, bf16[1,2,576,128]{3,2,1,0:T(8,128)(2,1)S(1)}, u32[]{:S(2)}, u32[]{:S(2)}) collective-permute-start(bf16[1,2,576,128]{3,2,1,0:T(8,128)(2,1)S(1)} %get-tuple-element.294), channel_id=1, source_target_pairs={{0,1},{1,0},{2,3},{3,2},{4,5},{5,4},{6,7},{7,6},{8,9},{9,8},{10,11... | collective-permute-start | bytes 884744 | tf_op jit(solution)/shard_map/ppermute | solution.py:793
  327.0 5.2 %collective-permute-start.25 = (bf16[1,1,192,128]{3,2,1,0:T(8,128)(2,1)S(1)}, bf16[1,1,192,128]{3,2,1,0:T(8,128)(2,1)S(1)}, u32[]{:S(2)}, u32[]{:S(2)}) collective-permute-start(bf16[1,1,192,128]{3,2,1,0:T(8,128)(2,1)S(1)} %get-tuple-element.314), channel_id=1, source_target_pairs={{0,16},{8,24},{16,0},{24,8},{1,17},{9,25},{17,1},{25,9},{2,18},{10... | collective-permute-start | bytes 147464 | tf_op jit(solution)/shard_map/ppermute | solution.py:792
  331.7 4.7 %collective-permute-start.22 = (bf16[2,1,208,128]{3,2,0,1:T(8,128)(2,1)S(1)}, bf16[2,1,208,128]{3,2,0,1:T(8,128)(2,1)S(1)}, u32[]{:S(2)}, u32[]{:S(2)}) collective-permute-start(bf16[2,1,208,128]{3,2,0,1:T(8,128)(2,1)S(1)} %bitcast.138), channel_id=1, source_target_pairs={{0,8},{8,0},{16,24},{24,16},{1,9},{9,1},{17,25},{25,17},{2,10},{10... | collective-permute-start | bytes 319496 | tf_op jit(solution)/shard_map/ppermute | solution.py:792
  337.1 10.0 %collective-permute-start.26 = (bf16[1,1,576,128]{3,2,1,0:T(8,128)(2,1)S(1)}, bf16[1,1,576,128]{3,2,1,0:T(8,128)(2,1)S(1)}, u32[]{:S(2)}, u32[]{:S(2)}) collective-permute-start(bf16[1,1,576,128]{3,2,1,0:T(8,128)(2,1)S(1)} %get-tuple-element.319), channel_id=1, source_target_pairs={{0,16},{8,24},{16,0},{24,8},{1,17},{9,25},{17,1},{25,9},{2,18},{10... | collective-permute-start | bytes 442376 | tf_op jit(solution)/shard_map/ppermute | solution.py:792
  338.5 7.3 %collective-permute-start.24 = (bf16[1,1,208,128]{3,2,1,0:T(8,128)(2,1)S(1)}, bf16[1,1,208,128]{3,2,1,0:T(8,128)(2,1)S(1)}, u32[]{:S(2)}, u32[]{:S(2)}) collective-permute-start(bf16[1,1,208,128]{3,2,1,0:T(8,128)(2,1)S(1)} %get-tuple-element.308), channel_id=1, source_target_pairs={{0,16},{8,24},{16,0},{24,8},{1,17},{9,25},{17,1},{25,9},{2,18},{10... | collective-permute-start | bytes 159752 | tf_op jit(solution)/shard_map/ppermute | solution.py:792
  (89 other events, 201.6 us)
